TPU v7x, 32 devices: a whole 2x2x4 slice. The times are simulated.
32 devices in a mesh: frame: 4 (over z), fsdp: 8 (over y, x, core).
Axes of the slice: x: 2, y: 2, z: 4, core: 2. Of those that a mesh axis runs over, the one named last changes fastest.
Arguments:
- video: bfloat16 [8, 8, 196, 768], P('fsdp', 'frame'), may hold values from -6 to 6
- temporal_entry: bfloat16 [768, 2304], P('fsdp'), may hold values from -0.3125 to 0.3125
- temporal_exit: bfloat16 [768, 768], P('fsdp'), may hold values from -0.625 to 0.625
- spatial_entry: bfloat16 [768, 2304], P('fsdp'), may hold values from -0.3125 to 0.3125
- spatial_exit: bfloat16 [768, 768], P('fsdp'), may hold values from -1.25 to 1.25
- expand_weight: bfloat16 [768, 3072], P('fsdp'), may hold values from -0.21875 to 0.21875
- contract_weight: bfloat16 [3072, 768], P('fsdp'), may hold values from -0.109375 to 0.109375
- layer_gains: bfloat16 [3, 768], P(None, 'fsdp'), may hold values from 0.25 to 1.75
- layer_shifts: bfloat16 [3, 768], P(None, 'fsdp'), may hold values from -4 to 4
- branch_biases: bfloat16 [3, 768], P(None, 'fsdp'), may hold values from -4 to 4
- expand_bias: bfloat16 [3072], P('fsdp'), may hold values from -4 to 4
- cotangent: bfloat16 [8, 8, 196, 768], P('fsdp', 'frame'), may hold values from -6 to 6
Outputs:
- layer_output: bfloat16 [8, 8, 196, 768], P('fsdp', 'frame')
- input_grad: float32 [8, 8, 196, 768], P('fsdp', 'frame')
- temporal_entry_grad: float32 [768, 2304], P('fsdp')
- temporal_exit_grad: float32 [768, 768], P('fsdp')
- spatial_entry_grad: float32 [768, 2304], P('fsdp')
- spatial_exit_grad: float32 [768, 768], P('fsdp')
- expand_weight_grad: float32 [768, 3072], P('fsdp')
- contract_weight_grad: float32 [3072, 768], P('fsdp')
- layer_gains_grad: float32 [3, 768], P(None, 'fsdp')
- layer_shifts_grad: float32 [3, 768], P(None, 'fsdp')
- branch_biases_grad: float32 [3, 768], P(None, 'fsdp')
- expand_bias_grad: float32 [3072], P('fsdp')
All inputs are finite; a program needn't handle non-finite values.
Results may differ from a plain program's by a relative error of at most 0.024.
The roundings to bfloat16 on the way count: a program that leaves them out, or rounds other values in their place, can miss the bound.
Values may be sent and summed in bfloat16 or wider, within the bound.
No kernel may reach another device: no remote copies, remote signals or barrier semaphores. Data moves between devices by JAX's collectives and lax.ppermute only.
A program may use at most 192 MiB of HBM per device.

v0:
```python
import jax
import jax.numpy as jnp
from jax import lax
from jax.sharding import PartitionSpec as P

HEADS = 12


norm_eps = 1e-05


def layer_norm(values, norm_gain, norm_shift):
    average = jnp.mean(values, axis=-1, keepdims=True)
    centred = values - average
    variance = jnp.mean(centred * centred, axis=-1, keepdims=True)
    return centred * lax.rsqrt(variance + norm_eps) * norm_gain + norm_shift


def rounded(values):
    return lax.optimization_barrier(values.astype(jnp.bfloat16)).astype(jnp.float32)


def dense(first_op, second_op):
    return jnp.dot(first_op, second_op, preferred_element_type=jnp.float32)


def dense_left(first_op, second_op):
    return lax.dot_general(
        first_op, second_op, (((0,), (0,)), ((), ())), preferred_element_type=jnp.float32
    )


def dense_right(first_op, second_op):
    return lax.dot_general(
        first_op, second_op, (((1,), (1,)), ((), ())), preferred_element_type=jnp.float32
    )


def split_heads(packed):
    outer = packed.shape
    parted = packed.reshape(outer[:-1] + (3, HEADS, outer[-1] // (3 * HEADS)))
    return (parted[..., 0, :, :], parted[..., 1, :, :], parted[..., 2, :, :])


def attend_forward(packed, layout):
    key_layout = layout.replace("l", "m")
    queries, key_rows, values = split_heads(packed)
    factor = queries.shape[-1] ** (-0.5)
    scores = (
        jnp.einsum(
            layout + "hd," + key_layout + "hd->cqhlm",
            queries,
            key_rows,
            preferred_element_type=jnp.float32,
        )
        * factor
    )
    highest = jnp.max(scores, axis=-1, keepdims=True)
    raised = jnp.exp(scores - highest)
    row_totals = jnp.sum(raised, axis=-1, keepdims=True)
    attention = (raised / row_totals).astype(jnp.bfloat16)
    blended = jnp.einsum(
        "cqhlm," + key_layout + "hd->" + layout + "hd",
        attention,
        values,
        preferred_element_type=jnp.float32,
    )
    outer = packed.shape
    return (
        blended.reshape(outer[:-1] + (outer[-1] // 3,)).astype(jnp.bfloat16),
        highest + jnp.log(row_totals),
    )


def attend_backward(packed, logsum, grad_blended, layout):
    key_layout = layout.replace("l", "m")
    queries, key_rows, values = split_heads(packed)
    factor = queries.shape[-1] ** (-0.5)
    outer = grad_blended.shape
    grad_heads = grad_blended.reshape(outer[:-1] + (HEADS, outer[-1] // HEADS))
    scores = (
        jnp.einsum(
            layout + "hd," + key_layout + "hd->cqhlm",
            queries,
            key_rows,
            preferred_element_type=jnp.float32,
        )
        * factor
    )
    attention = jnp.exp(scores - logsum)
    grad_values = jnp.einsum(
        "cqhlm," + layout + "hd->" + key_layout + "hd",
        attention.astype(jnp.bfloat16),
        grad_heads,
        preferred_element_type=jnp.float32,
    )
    grad_attention = jnp.einsum(
        layout + "hd," + key_layout + "hd->cqhlm",
        grad_heads,
        values,
        preferred_element_type=jnp.float32,
    )
    grad_scores = (
        attention * (grad_attention - jnp.sum(grad_attention * attention, axis=-1, keepdims=True))
    ).astype(jnp.bfloat16)
    grad_queries = (
        jnp.einsum(
            "cqhlm," + key_layout + "hd->" + layout + "hd",
            grad_scores,
            key_rows,
            preferred_element_type=jnp.float32,
        )
        * factor
    )
    grad_keys = (
        jnp.einsum(
            "cqhlm," + layout + "hd->" + key_layout + "hd",
            grad_scores,
            queries,
            preferred_element_type=jnp.float32,
        )
        * factor
    )
    stacked = jnp.stack([grad_queries, grad_keys, grad_values], axis=-3)
    return stacked.reshape(packed.shape).astype(jnp.bfloat16)


def body(
    video,
    temporal_entry,
    temporal_exit,
    spatial_entry,
    spatial_exit,
    expand_weight,
    contract_weight,
    layer_gains,
    layer_shifts,
    branch_biases,
    expand_bias,
    cotangent,
):
    clips_here, frames_here, places, model_width = video.shape
    rows_shape = (clips_here, frames_here, places)
    entry_time, exit_time, entry_space, exit_space, gains_low, shifts_low, biases_low = (
        lax.all_gather(temporal_entry, "fsdp", axis=0, tiled=True),
        lax.all_gather(temporal_exit, "fsdp", axis=0, tiled=True),
        lax.all_gather(spatial_entry, "fsdp", axis=0, tiled=True),
        lax.all_gather(spatial_exit, "fsdp", axis=0, tiled=True),
        lax.all_gather(layer_gains, "fsdp", axis=1, tiled=True),
        lax.all_gather(layer_shifts, "fsdp", axis=1, tiled=True),
        lax.all_gather(branch_biases, "fsdp", axis=1, tiled=True),
    )
    expand_full, contract_full, expand_bias_full = (
        lax.all_gather(expand_weight, "fsdp", axis=0, tiled=True),
        lax.all_gather(contract_weight, "fsdp", axis=0, tiled=True),
        lax.all_gather(expand_bias, "fsdp", axis=0, tiled=True),
    )
    gains = gains_low.astype(jnp.float32)
    shifts = shifts_low.astype(jnp.float32)
    biases = biases_low.astype(jnp.float32)
    tokens = video.astype(jnp.float32).reshape(-1, model_width)
    normed_one = layer_norm(tokens, gains[0], shifts[0]).astype(jnp.bfloat16)
    packed_frame = dense(normed_one, entry_time).astype(jnp.bfloat16)
    packed_place = lax.all_to_all(
        packed_frame.reshape(rows_shape + (3 * model_width,)),
        "frame",
        split_axis=2,
        concat_axis=1,
        tiled=True,
    )
    blended_place, logsum_time = attend_forward(packed_place, "clq")
    blended_time = lax.all_to_all(
        blended_place, "frame", split_axis=1, concat_axis=2, tiled=True
    ).reshape(-1, model_width)
    after_time = tokens + (dense(blended_time, exit_time) + biases[0])
    normed_two = layer_norm(after_time, gains[1], shifts[1]).astype(jnp.bfloat16)
    packed_space = (
        dense(normed_two, entry_space).astype(jnp.bfloat16).reshape(rows_shape + (3 * model_width,))
    )
    blended_space, logsum_space = attend_forward(packed_space, "cql")
    blended_rows = blended_space.reshape(-1, model_width)
    after_space = after_time + (dense(blended_rows, exit_space) + biases[1])
    normed_three = layer_norm(after_space, gains[2], shifts[2]).astype(jnp.bfloat16)
    hidden = dense(normed_three, expand_full) + expand_bias_full.astype(jnp.float32)
    active = jax.nn.gelu(hidden, approximate=False).astype(jnp.bfloat16)
    layer_output = (
        (after_space + (dense(active, contract_full) + biases[2]))
        .astype(jnp.bfloat16)
        .reshape(video.shape)
    )
    grad_top = cotangent.astype(jnp.float32).reshape(-1, model_width)
    grad_branch = grad_top.astype(jnp.bfloat16)
    grad_bias_last = jnp.sum(grad_branch.astype(jnp.float32), axis=0)
    grad_contract = dense_left(active, grad_branch)
    grad_active = dense_right(grad_branch, contract_full)
    gelu_pull = jax.vjp(lambda inner: jax.nn.gelu(inner, approximate=False), hidden)[1]
    grad_hidden = gelu_pull(grad_active)[0].astype(jnp.bfloat16)
    grad_expand = dense_left(normed_three, grad_hidden)
    grad_expand_bias = jnp.sum(grad_hidden.astype(jnp.float32), axis=0)
    grad_normed = rounded(dense_right(grad_hidden, expand_full))
    norm_pull = jax.vjp(layer_norm, after_space, gains[2], shifts[2])[1]
    grad_inner, grad_gain_last, grad_shift_last = norm_pull(grad_normed)
    grad_after_space = grad_top + grad_inner
    mlp_parts = (
        lax.psum_scatter(grad_expand, "fsdp", scatter_dimension=0, tiled=True),
        lax.psum_scatter(grad_contract, "fsdp", scatter_dimension=0, tiled=True),
        lax.psum_scatter(grad_expand_bias, "fsdp", scatter_dimension=0, tiled=True),
    )
    grad_branch = grad_after_space.astype(jnp.bfloat16)
    grad_bias_space = jnp.sum(grad_branch.astype(jnp.float32), axis=0)
    grad_exit_space = dense_left(blended_rows, grad_branch)
    grad_blended = (
        dense_right(grad_branch, exit_space)
        .astype(jnp.bfloat16)
        .reshape(rows_shape + (model_width,))
    )
    grad_packed = attend_backward(packed_space, logsum_space, grad_blended, "cql").reshape(
        -1, 3 * model_width
    )
    grad_entry_space = dense_left(normed_two, grad_packed)
    grad_normed = rounded(dense_right(grad_packed, entry_space))
    norm_pull = jax.vjp(layer_norm, after_time, gains[1], shifts[1])[1]
    grad_inner, grad_gain_space, grad_shift_space = norm_pull(grad_normed)
    grad_after_time = grad_after_space + grad_inner
    grad_branch = grad_after_time.astype(jnp.bfloat16)
    grad_bias_time = jnp.sum(grad_branch.astype(jnp.float32), axis=0)
    grad_exit_time = dense_left(blended_time, grad_branch)
    grad_blended = (
        dense_right(grad_branch, exit_time)
        .astype(jnp.bfloat16)
        .reshape(rows_shape + (model_width,))
    )
    grad_blended_place = lax.all_to_all(
        grad_blended, "frame", split_axis=2, concat_axis=1, tiled=True
    )
    grad_packed_place = attend_backward(packed_place, logsum_time, grad_blended_place, "clq")
    grad_packed_frame = lax.all_to_all(
        grad_packed_place, "frame", split_axis=1, concat_axis=2, tiled=True
    ).reshape(-1, 3 * model_width)
    grad_entry_time = dense_left(normed_one, grad_packed_frame)
    grad_normed_one = rounded(dense_right(grad_packed_frame, entry_time))
    norm_pull = jax.vjp(layer_norm, tokens, gains[0], shifts[0])[1]
    grad_inner, grad_gain_time, grad_shift_time = norm_pull(grad_normed_one)
    input_grad = (grad_after_time + grad_inner).reshape(video.shape)
    grad_gains = jnp.stack([grad_gain_time, grad_gain_space, grad_gain_last])
    grad_shifts = jnp.stack([grad_shift_time, grad_shift_space, grad_shift_last])
    grad_biases = jnp.stack([grad_bias_time, grad_bias_space, grad_bias_last])
    attention_parts = (
        lax.psum_scatter(grad_entry_time, "fsdp", scatter_dimension=0, tiled=True),
        lax.psum_scatter(grad_exit_time, "fsdp", scatter_dimension=0, tiled=True),
        lax.psum_scatter(grad_entry_space, "fsdp", scatter_dimension=0, tiled=True),
        lax.psum_scatter(grad_exit_space, "fsdp", scatter_dimension=0, tiled=True),
        lax.psum_scatter(grad_gains, "fsdp", scatter_dimension=1, tiled=True),
        lax.psum_scatter(grad_shifts, "fsdp", scatter_dimension=1, tiled=True),
        lax.psum_scatter(grad_biases, "fsdp", scatter_dimension=1, tiled=True),
    )
    shares = (
        lax.psum_scatter(
            attention_parts[0].astype(jnp.bfloat16), "frame", scatter_dimension=0, tiled=True
        ).astype(jnp.float32),
        lax.psum_scatter(
            attention_parts[1].astype(jnp.bfloat16), "frame", scatter_dimension=0, tiled=True
        ).astype(jnp.float32),
        lax.psum_scatter(
            attention_parts[2].astype(jnp.bfloat16), "frame", scatter_dimension=0, tiled=True
        ).astype(jnp.float32),
        lax.psum_scatter(
            attention_parts[3].astype(jnp.bfloat16), "frame", scatter_dimension=0, tiled=True
        ).astype(jnp.float32),
        lax.psum_scatter(
            mlp_parts[0].astype(jnp.bfloat16), "frame", scatter_dimension=0, tiled=True
        ).astype(jnp.float32),
        lax.psum_scatter(
            mlp_parts[1].astype(jnp.bfloat16), "frame", scatter_dimension=0, tiled=True
        ).astype(jnp.float32),
        lax.psum_scatter(
            jnp.moveaxis(attention_parts[4], 0, 1).astype(jnp.bfloat16),
            "frame",
            scatter_dimension=0,
            tiled=True,
        ).astype(jnp.float32),
        lax.psum_scatter(
            jnp.moveaxis(attention_parts[5], 0, 1).astype(jnp.bfloat16),
            "frame",
            scatter_dimension=0,
            tiled=True,
        ).astype(jnp.float32),
        lax.psum_scatter(
            jnp.moveaxis(attention_parts[6], 0, 1).astype(jnp.bfloat16),
            "frame",
            scatter_dimension=0,
            tiled=True,
        ).astype(jnp.float32),
        lax.psum_scatter(
            mlp_parts[2].astype(jnp.bfloat16), "frame", scatter_dimension=0, tiled=True
        ).astype(jnp.float32),
    )
    pieces = (
        lax.all_gather(shares[0].astype(jnp.bfloat16), "frame", axis=0, tiled=True).astype(
            jnp.float32
        ),
        lax.all_gather(shares[1].astype(jnp.bfloat16), "frame", axis=0, tiled=True).astype(
            jnp.float32
        ),
        lax.all_gather(shares[2].astype(jnp.bfloat16), "frame", axis=0, tiled=True).astype(
            jnp.float32
        ),
        lax.all_gather(shares[3].astype(jnp.bfloat16), "frame", axis=0, tiled=True).astype(
            jnp.float32
        ),
        lax.all_gather(shares[4].astype(jnp.bfloat16), "frame", axis=0, tiled=True).astype(
            jnp.float32
        ),
        lax.all_gather(shares[5].astype(jnp.bfloat16), "frame", axis=0, tiled=True).astype(
            jnp.float32
        ),
        lax.all_gather(shares[6].astype(jnp.bfloat16), "frame", axis=0, tiled=True).astype(
            jnp.float32
        ),
        lax.all_gather(shares[7].astype(jnp.bfloat16), "frame", axis=0, tiled=True).astype(
            jnp.float32
        ),
        lax.all_gather(shares[8].astype(jnp.bfloat16), "frame", axis=0, tiled=True).astype(
            jnp.float32
        ),
        lax.all_gather(shares[9].astype(jnp.bfloat16), "frame", axis=0, tiled=True).astype(
            jnp.float32
        ),
    )
    totals = (
        pieces[0],
        pieces[1],
        pieces[2],
        pieces[3],
        pieces[4],
        pieces[5],
        jnp.moveaxis(pieces[6], 0, 1),
        jnp.moveaxis(pieces[7], 0, 1),
        jnp.moveaxis(pieces[8], 0, 1),
        pieces[9],
    )
    return (
        layer_output,
        input_grad,
        totals[0],
        totals[1],
        totals[2],
        totals[3],
        totals[4],
        totals[5],
        totals[6],
        totals[7],
        totals[8],
        totals[9],
    )


def solution(mesh):
    placed = (
        P("fsdp", "frame", None, None),
        P("fsdp", None),
        P("fsdp", None),
        P("fsdp", None),
        P("fsdp", None),
        P("fsdp", None),
        P("fsdp", None),
        P(None, "fsdp"),
        P(None, "fsdp"),
        P(None, "fsdp"),
        P("fsdp"),
        P("fsdp", "frame", None, None),
    )
    return jax.shard_map(
        body,
        mesh=mesh,
        in_specs=placed,
        out_specs=(
            P("fsdp", "frame", None, None),
            P("fsdp", "frame", None, None),
            P("fsdp", None),
            P("fsdp", None),
            P("fsdp", None),
            P("fsdp", None),
            P("fsdp", None),
            P("fsdp", None),
            P(None, "fsdp"),
            P(None, "fsdp"),
            P(None, "fsdp"),
            P("fsdp"),
        ),
        check_vma=False,
    )
```

profile of v0, /device:TPU:0, one launch (start us, length us, event | category | flops | bytes accessed | tf_op | source)
XLA Modules:
  0.0 897.7 jit_solution(17567543899120378904)
XLA Ops:
  13.8 10.3 %all-gather = bf16[8,96,3]{1,2,0:T(4,128)(2,1)S(1)} all-gather(bf16[1,96,3]{1,2,0:T(4,128)(2,1)S(1)} %bitcast.220), channel_id=1, replica_groups=mesh['frame'=4,'fsdp'=8] {'fsdp'}, dimensions={0}, use_global_device_ids=true | all-gather | bytes 5184 | tf_op jit(solution)/shard_map/all_gather | solution.py:149
  24.5 8.9 all-gather.1
  33.5 13.1 %all-gather.14.cloned.1.call-done = bf16[768,2304]{1,0:T(8,128)(2,1)} async-done(((bf16[96,2304]{1,0:T(8,128)(2,1)}), bf16[768,2304]{1,0:T(8,128)(2,1)}) %all-gather.14.cloned.1.call-update) | async-done | bytes 3538960 | tf_op jit(solution)/shard_map/all_gather | solution.py:145
  54.8 47.3 %all_to_all.60 = bf16[1,2,196,2304]{3,1,0,2:T(2,128)(2,1)S(1)} all-to-all(bf16[1,2,196,2304]{3,1,0,2:T(2,128)(2,1)S(1)} %copy.129), channel_id=1, replica_groups=mesh['frame'=4,'fsdp'=8] {'frame'}, dimensions={2} | all-to-all | bytes 3612672 | tf_op jit(solution)/shard_map/all_to_all | solution.py:164
  124.9 8.9 all-gather.2
  133.9 7.9 all-gather.3
  192.2 16.3 %multiply_convert_fusion.1 = (bf16[392,3072]{1,0:T(8,128)(2,1)}, f32[392,3072]{1,0:T(8,128)}, f32[392,3072]{1,0:T(8,128)}) fusion(f32[3072]{0:T(1024)S(1)} %bitcast.212, bf16[768,3072]{1,0:T(8,128)(2,1)} %all-gather.22.cloned.1.call-done, f32[392,768]{1,0:T(8,128)} %copy-done.5, f32[768]{0:T(1024)S(1)} %get-tuple-element.77, f32[768]{0:T(1024)S(1)} %get-tuple-element.74, ...), kind=kOutput, calls=%fused_computation.9 | convolution fusion | flops 1930672128 | bytes 17986624 | tf_op jit(solution)/shard_map/dot_general | solution.py:24
  208.5 7.3 all-gather.24.cloned.1.call-done
  215.8 9.0 convert_reduce_fusion
  271.6 7.3 fusion.83
  292.5 15.5 %all-to-all-done.2 = bf16[1,2,196,768]{3,1,0,2:T(2,128)(2,1)} async-done(((bf16[1,2,196,768]{3,1,0,2:T(2,128)(2,1)}), bf16[1,2,196,768]{3,1,0,2:T(2,128)(2,1)}, u32[]{:S(2)}, u32[]{:S(2)}) %all-to-all-start.2) | async-done | bytes 602144 | tf_op jit(solution)/shard_map/all_to_all | solution.py:233
  335.9 44.6 %all-to-all-done.3 = bf16[1,8,49,2304]{3,2,0,1:T(8,128)(2,1)S(1)} async-done(((bf16[1,8,49,2304]{3,2,0,1:T(8,128)(2,1)}), bf16[1,8,49,2304]{3,2,0,1:T(8,128)(2,1)S(1)}, u32[]{:S(2)}, u32[]{:S(2)}) %all-to-all-start.3) | async-done | bytes 1806368 | tf_op jit(solution)/shard_map/all_to_all | solution.py:237
  390.5 7.3 fusion.84
  408.4 8.9 fusion.64
  423.0 42.7 %reduce-scatter.25.cloned.1.call-done = f32[96,2304]{1,0:T(8,128)} async-done(((f32[768,2304]{1,0:T(8,128)}), f32[96,2304]{1,0:T(8,128)}) %reduce-scatter.25.cloned.1.call-update) | async-done | bytes 884752 | tf_op jit(solution)/shard_map/reduce_scatter | solution.py:249
  471.5 74.1 %reduce-scatter.41.cloned.1.call-done = f32[96,3072]{1,0:T(8,128)} async-done(((f32[768,3072]{1,0:T(8,128)}), f32[96,3072]{1,0:T(8,128)}) %reduce-scatter.41.cloned.1.call-update) | async-done | bytes 1179664 | tf_op jit(solution)/shard_map/reduce_scatter | solution.py:205
  558.3 23.2 %all-reduce.4 = bf16[3072]{0:T(1024)(128)(2,1)S(1)} all-reduce(f32[3072]{0:T(1024)S(1)} %get-tuple-element.115), channel_id=20, replica_groups=mesh['frame'=4,'fsdp'=8] {'fsdp'}, use_global_device_ids=true, to_apply=%region_46.0.clone | all-reduce | flops 3072 | bytes 18432
  581.6 12.0 %all-reduce.5 = bf16[384]{0:T(512)(128)(2,1)S(1)} all-reduce(bf16[384]{0:T(512)(128)(2,1)S(1)} %dynamic-slice.15), channel_id=21, replica_groups=mesh['frame'=4,'fsdp'=8] {'frame'}, use_global_device_ids=true, to_apply=%region_47.0.clone | all-reduce | flops 384 | bytes 1536
  599.2 20.2 %reduce-scatter.51.cloned.1.call-done = f32[96,3]{1,0:T(8,128)} async-done(((f32[768,3]{1,0:T(8,128)}), f32[96,3]{1,0:T(8,128)}) %reduce-scatter.51.cloned.1.call-update) | async-done | bytes 1168
  620.3 35.9 %reduce-scatter.49.cloned.1.call-done = f32[96,3]{1,0:T(8,128)} async-done(((f32[768,3]{1,0:T(8,128)}), f32[96,3]{1,0:T(8,128)}) %reduce-scatter.49.cloned.1.call-update) | async-done | bytes 1168
  657.1 11.7 %all-reduce.6 = (bf16[96,3]{0,1:T(4,128)(2,1)S(1)}, bf16[96,3]{0,1:T(4,128)(2,1)S(1)}, bf16[96,3]{0,1:T(4,128)(2,1)S(1)}, bf16[384]{0:T(512)(128)(2,1)S(1)}) all-reduce(bf16[96,3]{0,1:T(4,128)(2,1)S(1)} %bitcast.216, bf16[96,3]{0,1:T(4,128)(2,1)S(1)} %bitcast.215, ...), channel_id=15, replica_groups=mesh['frame'=4,'fsdp'=8] {'frame'}, use_global_device_ids=true, to_apply=%region_34.0.clone | all-reduce | flops 1248 | bytes 4992
  668.8 7.6 all-gather.5
  677.1 9.6 %all-gather.6 = bf16[4,24,3]{1,2,0:T(4,128)(2,1)S(1)} all-gather(bf16[1,24,3]{1,2,0:T(4,128)(2,1)S(1)} %dynamic-slice_bitcast_fusion), channel_id=1, replica_groups=mesh['frame'=4,'fsdp'=8] {'frame'}, dimensions={0}, use_global_device_ids=true | all-gather | bytes 720 | tf_op jit(solution)/shard_map/all_gather | solution.py:323
  686.7 49.3 %reduce-scatter.45.cloned.1.call-done = f32[384,768]{1,0:T(8,128)} async-done(((f32[3072,768]{1,0:T(8,128)}), f32[384,768]{1,0:T(8,128)}) %reduce-scatter.45.cloned.1.call-update) | async-done | bytes 1179664 | tf_op jit(solution)/shard_map/reduce_scatter | solution.py:206
  738.9 10.9 %all-gather.4 = bf16[4,24,3]{1,2,0:T(4,128)(2,1)S(1)} all-gather(bf16[1,24,3]{1,2,0:T(4,128)(2,1)S(1)} %dynamic-slice_bitcast_fusion.2), channel_id=1, replica_groups=mesh['frame'=4,'fsdp'=8] {'frame'}, dimensions={0}, use_global_device_ids=true | all-gather | bytes 720 | tf_op jit(solution)/shard_map/all_gather | solution.py:317
  751.1 6.9 reduce-scatter.39.cloned.1.call-done
  758.0 13.9 %all_gather.73 = bf16[96,768]{1,0:T(8,128)(2,1)S(1)} all-gather(bf16[24,768]{1,0:T(8,128)(2,1)} %reduce-scatter.39.cloned.1.call-done), channel_id=1, replica_groups=mesh['frame'=4,'fsdp'=8] {'frame'}, dimensions={0}, use_global_device_ids=true | all-gather | bytes 184320 | tf_op jit(solution)/shard_map/all_gather | solution.py:308
  778.3 14.1 %all_gather.71 = bf16[96,768]{1,0:T(8,128)(2,1)S(1)} all-gather(bf16[24,768]{1,0:T(8,128)(2,1)} %reduce-scatter.31.cloned.1.call-done), channel_id=1, replica_groups=mesh['frame'=4,'fsdp'=8] {'frame'}, dimensions={0}, use_global_device_ids=true | all-gather | bytes 184320 | tf_op jit(solution)/shard_map/all_gather | solution.py:302
  800.0 18.3 %all_gather.72 = bf16[96,2304]{1,0:T(8,128)(2,1)S(1)} all-gather(bf16[24,2304]{1,0:T(8,128)(2,1)} %reduce-scatter.35.cloned.1.call-done), channel_id=1, replica_groups=mesh['frame'=4,'fsdp'=8] {'frame'}, dimensions={0}, use_global_device_ids=true | all-gather | bytes 552960 | tf_op jit(solution)/shard_map/all_gather | solution.py:305
  823.1 18.2 %all_gather.70 = bf16[96,2304]{1,0:T(8,128)(2,1)S(1)} all-gather(bf16[24,2304]{1,0:T(8,128)(2,1)} %reduce-scatter.27.cloned.1.call-done), channel_id=1, replica_groups=mesh['frame'=4,'fsdp'=8] {'frame'}, dimensions={0}, use_global_device_ids=true | all-gather | bytes 552960 | tf_op jit(solution)/shard_map/all_gather | solution.py:299
  847.4 20.6 %all_gather.74 = bf16[96,3072]{1,0:T(8,128)(2,1)S(1)} all-gather(bf16[24,3072]{1,0:T(8,128)(2,1)} %reduce-scatter.43.cloned.1.call-done), channel_id=1, replica_groups=mesh['frame'=4,'fsdp'=8] {'frame'}, dimensions={0}, use_global_device_ids=true | all-gather | bytes 737280 | tf_op jit(solution)/shard_map/all_gather | solution.py:311
  873.3 16.0 %all_gather.75 = bf16[384,768]{1,0:T(8,128)(2,1)S(1)} all-gather(bf16[96,768]{1,0:T(8,128)(2,1)} %reduce-scatter.47.cloned.1.call-done), channel_id=1, replica_groups=mesh['frame'=4,'fsdp'=8] {'frame'}, dimensions={0}, use_global_device_ids=true | all-gather | bytes 737280 | tf_op jit(solution)/shard_map/all_gather | solution.py:314
  (331 shorter events, 261.7 us)
Async XLA Ops:
  7.2 39.4 %all-gather.14.cloned.1.call-start = ((), (), s32[]{:S(2)}) async-start(), calls=%async_computation.19 | async-start | bytes 3981312 | tf_op jit(solution)/shard_map/all_gather | solution.py:145
  7.9 141.6 %all-gather.16.cloned.1.call-start = ((), (), s32[]{:S(2)}) async-start(), calls=%async_computation.20 | async-start | bytes 1327104 | tf_op jit(solution)/shard_map/all_gather | solution.py:146
  8.7 144.7 %all-gather.18.cloned.1.call-start = ((), (), s32[]{:S(2)}) async-start(), calls=%async_computation.21 | async-start | bytes 3981312 | tf_op jit(solution)/shard_map/all_gather | solution.py:147
  9.4 179.0 %all-gather.20.cloned.1.call-start = ((), (), s32[]{:S(2)}) async-start(), calls=%async_computation.22 | async-start | bytes 1327104 | tf_op jit(solution)/shard_map/all_gather | solution.py:148
  10.0 182.2 %all-gather.22.cloned.1.call-start = ((), (), s32[]{:S(2)}) async-start(), calls=%async_computation.23 | async-start | bytes 5308416 | tf_op jit(solution)/shard_map/all_gather | solution.py:154
  13.3 38.3 %copy-start.39 = (f32[392]{0:T(512)}, f32[392]{0:T(512)S(1)}, u32[]{:S(2)}) copy-start(f32[392]{0:T(512)S(1)} %rsqrt.36) | copy-start | bytes 4708
  24.4 27.2 %copy-start.37 = (f32[392]{0:T(512)}, f32[392]{0:T(512)S(1)}, u32[]{:S(2)}) copy-start(f32[392]{0:T(512)S(1)} %div.81) | copy-start | bytes 4708
  24.5 27.1 %copy-start.3 = (f32[392,768]{1,0:T(8,128)}, f32[392,768]{1,0:T(8,128)S(1)}, u32[]{:S(2)}) copy-start(f32[392,768]{1,0:T(8,128)S(1)} %reshape.422) | copy-start | bytes 3612676
  117.8 16.1 %copy-start.49 = (bf16[384]{0:T(512)(128)(2,1)S(1)}, bf16[384]{0:T(512)(128)(2,1)}, u32[]{:S(2)}) copy-start(bf16[384]{0:T(512)(128)(2,1)} %param.22) | copy-start | bytes 2308
  120.8 26.5 %all-to-all-start.1 = ((bf16[1,8,49,768]{3,2,0,1:T(8,128)(2,1)}), bf16[1,8,49,768]{3,2,0,1:T(8,128)(2,1)S(1)}, u32[]{:S(2)}, u32[]{:S(2)}) async-start(bf16[1,8,49,768]{3,2,0,1:T(8,128)(2,1)} %reshape.471), calls=%async_computation.1 | async-start | bytes 1376256 | tf_op jit(solution)/shard_map/all_to_all | solution.py:172
  124.3 91.5 %all-gather.24.cloned.1.call-start = ((), (), s32[]{:S(2)}) async-start(), calls=%async_computation.24 | async-start | bytes 5308416 | tf_op jit(solution)/shard_map/all_gather | solution.py:155
  124.9 292.5 %reduce-scatter.37.cloned.1.call-start = ((), (), s32[]{:S(2)}) async-start(), calls=%async_computation.31 | async-start | bytes 2654208 | tf_op jit(solution)/shard_map/reduce_scatter | solution.py:252
  238.5 180.7 %reduce-scatter.29.cloned.1.call-start = ((), (), s32[]{:S(2)}) async-start(), calls=%async_computation.27 | async-start | bytes 2654208 | tf_op jit(solution)/shard_map/reduce_scatter | solution.py:250
  271.6 149.3 %reduce-scatter.33.cloned.1.call-start = ((), (), s32[]{:S(2)}) async-start(), calls=%async_computation.29 | async-start | bytes 7962624 | tf_op jit(solution)/shard_map/reduce_scatter | solution.py:251
  286.5 21.5 %all-to-all-start.2 = ((bf16[1,2,196,768]{3,1,0,2:T(2,128)(2,1)}), bf16[1,2,196,768]{3,1,0,2:T(2,128)(2,1)}, u32[]{:S(2)}, u32[]{:S(2)}) async-start(bf16[1,2,196,768]{3,1,0,2:T(2,128)(2,1)} %copy.153), calls=%async_computation.2 | async-start | bytes 1204224 | tf_op jit(solution)/shard_map/all_to_all | solution.py:233
  329.7 50.7 %all-to-all-start.3 = ((bf16[1,8,49,2304]{3,2,0,1:T(8,128)(2,1)}), bf16[1,8,49,2304]{3,2,0,1:T(8,128)(2,1)S(1)}, u32[]{:S(2)}, u32[]{:S(2)}) async-start(bf16[1,8,49,2304]{3,2,0,1:T(8,128)(2,1)} %reshape.472), calls=%async_computation.3 | async-start | bytes 4128768 | tf_op jit(solution)/shard_map/all_to_all | solution.py:237
  333.5 132.2 %reduce-scatter.25.cloned.1.call-start = ((), (), s32[]{:S(2)}) async-start(), calls=%async_computation.25 | async-start | bytes 7962624 | tf_op jit(solution)/shard_map/reduce_scatter | solution.py:249
  389.3 156.4 %reduce-scatter.41.cloned.1.call-start = ((), (), s32[]{:S(2)}) async-start(), calls=%async_computation.33 | async-start | bytes 10616832 | tf_op jit(solution)/shard_map/reduce_scatter | solution.py:205
  397.8 195.9 %reduce-scatter.53.cloned.1.call-start = ((), (), s32[]{:S(2)}) async-start(), calls=%async_computation.39 | async-start | bytes 442368
  400.6 218.8 %reduce-scatter.51.cloned.1.call-start = ((), (), s32[]{:S(2)}) async-start(), calls=%async_computation.38 | async-start | bytes 442368
  407.3 248.9 %reduce-scatter.49.cloned.1.call-start = ((), (), s32[]{:S(2)}) async-start(), calls=%async_computation.37 | async-start | bytes 442368
  408.3 327.7 %reduce-scatter.45.cloned.1.call-start = ((), (), s32[]{:S(2)}) async-start(), calls=%async_computation.35 | async-start | bytes 10616832 | tf_op jit(solution)/shard_map/reduce_scatter | solution.py:206
  417.3 340.7 %reduce-scatter.39.cloned.1.call-start = ((), (), s32[]{:S(2)}) async-start(), calls=%async_computation.32 | async-start | bytes 184320 | tf_op jit(solution)/shard_map/reduce_scatter | solution.py:267
  419.1 359.2 %reduce-scatter.31.cloned.1.call-start = ((), (), s32[]{:S(2)}) async-start(), calls=%async_computation.28 | async-start | bytes 184320 | tf_op jit(solution)/shard_map/reduce_scatter | solution.py:261
  420.8 46.9 %copy-start.51 = (u32[32]{0:T(128)S(1)}, u32[32]{0:T(128)}, u32[]{:S(2)}) copy-start(u32[32]{0:T(128)} %constant.110) | copy-start | bytes 388
  420.8 47.5 %copy-start.45 = (u32[32]{0:T(128)S(1)}, u32[32]{0:T(128)}, u32[]{:S(2)}) copy-start(u32[32]{0:T(128)} %constant.92) | copy-start | bytes 388
  420.8 379.2 %reduce-scatter.35.cloned.1.call-start = ((), (), s32[]{:S(2)}) async-start(), calls=%async_computation.30 | async-start | bytes 552960 | tf_op jit(solution)/shard_map/reduce_scatter | solution.py:264
  422.9 125.0 %copy-start.44 = (f32[768]{0:T(1024)S(1)}, f32[768]{0:T(1024)}, u32[]{:S(2)}) copy-start(f32[768]{0:T(1024)} %get-tuple-element.71) | copy-start | bytes 9220
  422.9 400.2 %reduce-scatter.27.cloned.1.call-start = ((), (), s32[]{:S(2)}) async-start(), calls=%async_computation.26 | async-start | bytes 552960 | tf_op jit(solution)/shard_map/reduce_scatter | solution.py:258
  467.7 379.8 %reduce-scatter.43.cloned.1.call-start = ((), (), s32[]{:S(2)}) async-start(), calls=%async_computation.34 | async-start | bytes 737280 | tf_op jit(solution)/shard_map/reduce_scatter | solution.py:270
  547.8 325.5 %reduce-scatter.47.cloned.1.call-start = ((), (), s32[]{:S(2)}) async-start(), calls=%async_computation.36 | async-start | bytes 737280 | tf_op jit(solution)/shard_map/reduce_scatter | solution.py:273
  553.8 40.8 %copy-start.9 = (f32[392,768]{1,0:T(8,128)S(1)}, f32[392,768]{1,0:T(8,128)}, u32[]{:S(2)}) copy-start(f32[392,768]{1,0:T(8,128)} %copy-done.8) | copy-start | bytes 3612676
  (47 other events, 157.6 us)
Sparse Core Ops, SparseCore 0:
  9.9 36.6 all-gather.13
  48.5 24.0 all-gather.15
  74.5 33.9 all-gather.17
  110.2 24.0 all-gather.19
  136.1 38.9 all-gather.21
  176.8 38.9 all-gather.23
  238.6 42.4 reduce-scatter.36
  284.8 42.4 reduce-scatter.28
  330.9 65.4 reduce-scatter.32
  400.2 65.4 reduce-scatter.24
  469.2 76.4 reduce-scatter.40
  548.6 33.8 reduce-scatter.52
  585.5 33.8 reduce-scatter.50
  622.3 33.8 reduce-scatter.48
  659.5 76.4 reduce-scatter.44
  738.7 19.2 reduce-scatter.38
  760.8 17.4 reduce-scatter.30
  781.0 18.9 reduce-scatter.34
  803.0 20.0 reduce-scatter.26
  825.8 21.5 reduce-scatter.42
  849.7 23.5 reduce-scatter.46
where the time goes:
time: 905 us; the launch traced here: 898 us
  waiting for transfers between devices  339 us (37%)
  blocking collectives  259 us (29%)
  local copies, waits for them, and re-layouts  116 us (13%)
  matrix products  114 us (13%)
  other arithmetic  37.4 us (4%)
  between operations  18.5 us (2%)
  starting transfers between devices  13.4 us (1%)
    reduce_scatter x1, waiting for transfers between devices, body(): lax.psum_scatter(grad_expand, 'fsdp', scatter_dimension=0, tiled=True)  74.1 us
    unnamed x24, waiting for transfers between devices  60 us
    reduce_scatter x1, waiting for transfers between devices, body(): lax.psum_scatter(grad_contract, 'fsdp', scatter_dimension=0, tiled=True)  49.3 us
    all_to_all x1, blocking collectives, body(): lax.all_to_all(packed_frame.reshape(rows_shape + (3 * model_width,)), 'fr...  47.3 us
    unnamed x3, blocking collectives  46.8 us
    all_to_all x1, waiting for transfers between devices, body(): lax.all_to_all(grad_packed_place, 'frame', split_axis=1, concat_axis=2, t...  44.6 us
    reduce_scatter x1, waiting for transfers between devices, body(): lax.psum_scatter(grad_entry_time, 'fsdp', scatter_dimension=0, tiled=True)  42.7 us
    dot_general x6, matrix products, dense(): return jnp.dot(first_op, second_op, preferred_element_type=jnp.float32)  37.5 us
  transfers between devices with their start and end apart: 24, of which 15 were waited for; matrix products, arithmetic and copies ran while one was open for 26% of the time, Pallas kernels for 0%

commit v1 on v0

--- a/solution.py
+++ b/solution.py
@@ -1,6 +1,10 @@
+import functools
+
 import jax
 import jax.numpy as jnp
 from jax import lax
+from jax.experimental import pallas as pl
+from jax.experimental.pallas import tpu as pltpu
 from jax.sharding import PartitionSpec as P
 
 HEADS = 12
@@ -125,7 +129,7 @@
     return stacked.reshape(packed.shape).astype(jnp.bfloat16)
 
 
-def body(
+def general_body(
     video,
     temporal_entry,
     temporal_exit,
@@ -355,6 +359,828 @@
     )
 
 
+BF = jnp.bfloat16
+F32 = jnp.float32
+D = 768
+FRAME_ROWS = 208
+PLACES = 196
+HERE = 49
+PIECE = 104
+ROWS = 416
+SPOTS = 400
+GROUP = 80
+SHARD = 96
+HALF = 48
+WIDE = 3072
+NEG = -1e30
+HBM = pl.BlockSpec(memory_space=pl.ANY)
+VMEM = pl.BlockSpec(memory_space=pltpu.VMEM)
+
+
+def nn(a, b):
+    return jnp.dot(a, b, preferred_element_type=F32)
+
+
+def nt(a, b):
+    return lax.dot_general(a, b, (((1,), (1,)), ((), ())), preferred_element_type=F32)
+
+
+def tn(a, b):
+    return lax.dot_general(a, b, (((0,), (0,)), ((), ())), preferred_element_type=F32)
+
+
+def normalised(values):
+    average = jnp.mean(values, axis=-1, keepdims=True)
+    centred = values - average
+    variance = jnp.mean(centred * centred, axis=-1, keepdims=True)
+    scale = lax.rsqrt(variance + norm_eps)
+    return centred * scale, scale
+
+
+def norm_back(grad, unit, scale, gain):
+    moved = grad * gain
+    inner = scale * (
+        moved
+        - jnp.mean(moved, axis=-1, keepdims=True)
+        - unit * jnp.mean(moved * unit, axis=-1, keepdims=True)
+    )
+    return (
+        inner,
+        jnp.sum(grad * unit, axis=0, keepdims=True),
+        jnp.sum(grad, axis=0, keepdims=True),
+    )
+
+
+def picks(target, columns):
+    lanes = lax.broadcasted_iota(jnp.int32, (target.shape[0], columns), 1)
+    return jnp.where(lanes == target, 1.0, 0.0).astype(BF)
+
+
+def row_index(rows):
+    return lax.broadcasted_iota(jnp.int32, (rows, 1), 0)
+
+
+def at_least(value, limit):
+    return jnp.where(value >= limit, 1, 0)
+
+
+def place_from_piece():
+    r = row_index(SPOTS)
+    col = ((r >> 1) & 3) * PIECE + (r & 1) * HERE + (r >> 3)
+    return picks(jnp.where(r < 8 * HERE, col, -1), ROWS)
+
+
+def piece_parts():
+    c = row_index(ROWS)
+    k = at_least(c, PIECE) + at_least(c, 2 * PIECE) + at_least(c, 3 * PIECE)
+    rem = c - PIECE * k
+    f = at_least(rem, HERE)
+    return k, f, rem - HERE * f, rem < 2 * HERE
+
+
+def piece_from_place():
+    k, f, p, valid = piece_parts()
+    return picks(jnp.where(valid, p * 8 + k * 2 + f, -1), SPOTS)
+
+
+def frame_from_piece(me):
+    r = row_index(ROWS)
+    f = at_least(r, FRAME_ROWS)
+    pl_ = r - FRAME_ROWS * f
+    q = at_least(pl_, HERE) + at_least(pl_, 2 * HERE) + at_least(pl_, 3 * HERE)
+    k = (q - me) & 3
+    col = k * PIECE + f * HERE + pl_ - HERE * q
+    return picks(jnp.where(pl_ < PLACES, col, -1), ROWS)
+
+
+def piece_from_frame(me):
+    k, f, p, valid = piece_parts()
+    q = (me + k) & 3
+    return picks(jnp.where(valid, f * FRAME_ROWS + HERE * q + p, -1), ROWS)
+
+
+def small_row(params, index, width=D):
+    block = index // 8
+    return params[index % 8 : index % 8 + 1, block * D : block * D + width]
+
+
+def lane_low(rows):
+    return lax.broadcasted_iota(jnp.int32, (rows, 128), 1) < 64
+
+
+def head_masks(factor):
+    lane = lax.broadcasted_iota(jnp.int32, (1, 128), 1)
+    low = jnp.where(lane < 64, factor, 0.0).astype(BF)
+    high = jnp.where(lane < 64, 0.0, factor).astype(BF)
+    return low, high
+
+
+def soft_rows(scores):
+    top = jnp.max(scores, axis=-1, keepdims=True)
+    raised = jnp.exp(scores - top)
+    return raised * (1.0 / jnp.sum(raised, axis=-1, keepdims=True))
+
+
+def soft_cols(scores):
+    top = jnp.max(scores, axis=0, keepdims=True)
+    raised = jnp.exp(scores - top)
+    return raised * (1.0 / jnp.sum(raised, axis=0, keepdims=True))
+
+
+def attend_block(q, k, v, keep):
+    outs = []
+    for mask in head_masks(0.125):
+        scores = jnp.where(keep, nt(q * mask, k), NEG)
+        outs.append(nn(soft_rows(scores).astype(BF), v))
+    return jnp.where(lane_low(q.shape[0]), outs[0], outs[1]).astype(BF)
+
+
+def attend_block_back(q, k, v, do, keep):
+    dq, dk, dv = [], [], []
+    for scaled, mask in zip(head_masks(0.125), head_masks(1.0), strict=True):
+        scores = jnp.where(keep, nt(k, q * scaled), NEG)
+        weight = soft_cols(scores)
+        dv.append(nn(weight.astype(BF), do))
+        dweight = nt(v, do * mask)
+        delta = jnp.sum(dweight * weight, axis=0, keepdims=True)
+        dscore = (weight * (dweight - delta)).astype(BF)
+        dq.append(tn(dscore, k))
+        dk.append(nn(dscore, q))
+    low = lane_low(q.shape[0])
+    return (
+        (jnp.where(low, dq[0], dq[1]) * 0.125).astype(BF),
+        (jnp.where(low, dk[0], dk[1]) * 0.125).astype(BF),
+        jnp.where(low, dv[0], dv[1]).astype(BF),
+    )
+
+
+def wide_product(a_ref, w_ref, out_ref, columns, step, w_offset=0):
+    def body(i, carry):
+        at = pl.multiple_of(i * step, 128)
+        out_ref[:, pl.ds(at, step)] = nn(
+            a_ref[...], w_ref[:, pl.ds(at + w_offset, step)]
+        ).astype(BF)
+        return carry
+
+    lax.fori_loop(0, columns // step, body, 0)
+
+
+def piece_copies(refs, own, weights, extra, sems):
+    copies = []
+
+    def add(src, dst):
+        copies.append(pltpu.make_async_copy(src, dst, sems.at[len(copies)]))
+
+    for core in (0, 1):
+        a, b, xa, yb, a2, b2 = refs[core]
+        for ref, index, relative, half in (
+            (a, None, 0, 0),
+            (b, None, 0, 1),
+            (xa, None, 2, 0),
+            (yb, None, 4, 1),
+            (a2, 0, 4, 0),
+            (a2, 1, 6, 0),
+            (b2, 0, 2, 1),
+            (b2, 1, 6, 1),
+        ):
+            whole = ref if index is None else ref.at[index]
+            shard = own ^ (relative ^ core)
+            rows = pl.ds(pl.multiple_of(shard * SHARD + half * HALF, 16), HALF)
+            add(whole.at[pl.ds(0, HALF)], weights.at[rows])
+            if half == 0 and extra is not None:
+                add(whole.at[pl.ds(HALF, 8)], extra.at[relative ^ core])
+    return copies
+
+
+def temporal_forward(*refs):
+    (x0, x1, x2, x3), refs = refs[:4], refs[4:]
+    pieces, refs = (refs[:6], refs[6:12]), refs[12:]
+    (o0, o1, o2, o3, normed_ref, packed_ref, weight_out, params_out, bias_out), refs = refs[:9], refs[9:]
+    weights, extra, stack, blended, sems, out_sem = refs
+    own = lax.axis_index("fsdp")
+    copies = piece_copies(pieces, own, weights, extra, sems)
+    for c in copies:
+        c.start()
+    for k, ref in enumerate((x0, x1, x2, x3)):
+        stack[pl.ds(k * PIECE, PIECE), :] = ref[...]
+    unit, _ = normalised(stack[...].astype(F32))
+    for c in copies:
+        c.wait()
+    out_copy = pltpu.make_async_copy(weights, weight_out, out_sem)
+    out_copy.start()
+    params = extra[0].astype(F32)
+    for k in range(1, 8):
+        params = params + extra[k].astype(F32)
+    params_out[...] = params
+    for r in range(4):
+        row = small_row(params, 9 + r)
+        bias_out[2 * r : 2 * r + 1, :] = row[:, :384]
+        bias_out[2 * r + 1 : 2 * r + 2, :] = row[:, 384:]
+    normed = (unit * small_row(params, 0) + small_row(params, 3)).astype(BF)
+    normed_ref[...] = nn(place_from_piece(), normed).astype(BF)
+    wide_product(normed_ref, weights, packed_ref, 3 * D, 384)
+    r = lax.broadcasted_iota(jnp.int32, (GROUP, GROUP), 0)
+    c = lax.broadcasted_iota(jnp.int32, (GROUP, GROUP), 1)
+    keep = (r >> 3) == (c >> 3)
+
+    def heads(i, carry):
+        at = pl.multiple_of(i * 128, 128)
+        for t in range(SPOTS // GROUP):
+            rows = pl.ds(t * GROUP, GROUP)
+            blended[rows, pl.ds(at, 128)] = attend_block(
+                packed_ref[rows, pl.ds(at, 128)],
+                packed_ref[rows, pl.ds(at + D, 128)],
+                packed_ref[rows, pl.ds(at + 2 * D, 128)],
+                keep,
+            )
+        return carry
+
+    lax.fori_loop(0, HEADS // 2, heads, 0)
+    back = nn(piece_from_place(), blended[...]).astype(BF)
+    for k, ref in enumerate((o0, o1, o2, o3)):
+        ref[...] = back[k * PIECE : (k + 1) * PIECE]
+    out_copy.wait()
+
+
+def spatial_forward(*refs):
+    (video, params_ref, o0, o1, o2, o3), refs = refs[:6], refs[6:]
+    pieces, refs = (refs[:6], refs[6:12]), refs[12:]
+    outs, refs = refs[:10], refs[10:]
+    after_ref, normed_ref, packed_ref, blended, after_two, normed_three, blended_time, w_exit, w_entry, w_last = outs
+    weights, stack, sems, out_sems = refs
+    own = lax.axis_index("fsdp")
+    me = lax.axis_index("frame")
+    copies = piece_copies(pieces, own, weights, None, sems)
+    for c in copies:
+        c.start()
+    params = params_ref[...]
+    for k, ref in enumerate((o0, o1, o2, o3)):
+        stack[pl.ds(k * PIECE, PIECE), :] = ref[...]
+    blended_time[...] = nn(frame_from_piece(me), stack[...]).astype(BF)
+    for c in copies:
+        c.wait()
+    outs_copies = [
+        pltpu.make_async_copy(weights.at[:, pl.ds(0, D)], w_exit, out_sems.at[0]),
+        pltpu.make_async_copy(weights.at[:, pl.ds(D, 3 * D)], w_entry, out_sems.at[1]),
+        pltpu.make_async_copy(weights.at[:, pl.ds(4 * D, D)], w_last, out_sems.at[2]),
+    ]
+    for c in outs_copies:
+        c.start()
+    after = (
+        video[...].astype(F32)
+        + nn(blended_time[...], weights[:, 0:D])
+        + small_row(params, 6)
+    )
+    after_ref[...] = after
+    unit, _ = normalised(after)
+    normed_ref[...] = (unit * small_row(params, 1) + small_row(params, 4)).astype(BF)
+    wide_product(normed_ref, weights, packed_ref, 3 * D, 384, D)
+    keep = lax.broadcasted_iota(jnp.int32, (FRAME_ROWS, FRAME_ROWS), 1) < PLACES
+
+    def heads(i, carry):
+        at = pl.multiple_of(i * 128, 128)
+        for f in range(2):
+            rows = pl.ds(f * FRAME_ROWS, FRAME_ROWS)
+            blended[rows, pl.ds(at, 128)] = attend_block(
+                packed_ref[rows, pl.ds(at, 128)],
+                packed_ref[rows, pl.ds(at + D, 128)],
+                packed_ref[rows, pl.ds(at + 2 * D, 128)],
+                keep,
+            )
+        return carry
+
+    lax.fori_loop(0, HEADS // 2, heads, 0)
+    last = after_ref[...] + nn(blended[...], weights[:, 4 * D : 5 * D]) + small_row(params, 7)
+    after_two[...] = last
+    unit, _ = normalised(last)
+    normed_three[...] = (unit * small_row(params, 2) + small_row(params, 5)).astype(BF)
+    for c in outs_copies:
+        c.wait()
+
+
+def feed_forward(where, normed, after, cot, params_ref, bias, expand, contract, *refs):
+    (output, grad_after, branch, keep_we, send_we, keep_wc, send_wc, small), refs = refs[:8], refs[8:]
+    total, grad_normed, shuffle = refs
+    step = pl.program_id(0)
+    own = where[0]
+    tile = own ^ step
+
+    @pl.when(step == 0)
+    def _():
+        total[...] = jnp.zeros_like(total)
+        grad_normed[...] = jnp.zeros_like(grad_normed)
+        small[...] = jnp.zeros_like(small)
+
+    w_in = expand[...].reshape(D, 384)
+    w_out = jnp.concatenate([contract[0, 0, :, c * D : (c + 1) * D] for c in range(4)], axis=0)
+    hidden = nn(normed[...], w_in) + bias[pl.ds(tile, 1), :]
+    area = 0.5 + 0.5 * lax.erf(hidden * 0.7071067811865476)
+    slope = area + hidden * (0.3989422804014327 * jnp.exp(-0.5 * hidden * hidden))
+    active = (hidden * area).astype(BF)
+    top = cot[...]
+    total[...] += nn(active, w_out)
+    grad_hidden = (nt(top, w_out) * slope).astype(BF)
+    grad_normed[...] += nt(grad_hidden, w_in)
+    small[pl.ds(9 + tile // 2, 1), pl.ds(pl.multiple_of((tile % 2) * 384, 128), 384)] = jnp.sum(
+        grad_hidden.astype(F32), axis=0, keepdims=True
+    )
+    grad_out = tn(active, top).astype(BF)
+    for parity, ref in ((0, keep_wc), (1, send_wc)):
+
+        @pl.when(step % 2 == parity)
+        def _(ref=ref):
+            for c in range(4):
+                ref[0, :, c * D : (c + 1) * D] = grad_out[c * SHARD : (c + 1) * SHARD]
+
+    shuffle[...] = tn(normed[...], grad_hidden)
+    for j in range(4):
+        for parity, ref in ((0, keep_we), (1, send_we)):
+            rows = pl.ds(pl.multiple_of((own ^ (2 * j + parity)) * SHARD, 8), SHARD)
+            ref[j] = shuffle[rows, :].astype(BF)
+
+    @pl.when(step == pl.num_programs(0) - 1)
+    def _():
+        params = params_ref[...]
+        values = after[...]
+        output[...] = (values + (total[...] + small_row(params, 8))).astype(BF)
+        unit, scale = normalised(values)
+        dn = grad_normed[...].astype(BF).astype(F32)
+        inner, dgain, dshift = norm_back(dn, unit, scale, small_row(params, 2))
+        top32 = cot[...].astype(F32)
+        dafter = top32 + inner
+        grad_after[...] = dafter
+        branch[...] = dafter.astype(BF)
+        small[2:3, :] = dgain
+        small[5:6, :] = dshift
+        small[8:9, :] = jnp.sum(top32, axis=0, keepdims=True)
+
+
+def spatial_back(branch, packed, w_last, grad_packed, grad_blended):
+    grad_blended[...] = nt(branch[...], w_last[...]).astype(BF)
+    keep = lax.broadcasted_iota(jnp.int32, (FRAME_ROWS, FRAME_ROWS), 0) < PLACES
+
+    def heads(i, carry):
+        at = pl.multiple_of(i * 128, 128)
+        for f in range(2):
+            rows = pl.ds(f * FRAME_ROWS, FRAME_ROWS)
+            dq, dk, dv = attend_block_back(
+                packed[rows, pl.ds(at, 128)],
+                packed[rows, pl.ds(at + D, 128)],
+                packed[rows, pl.ds(at + 2 * D, 128)],
+                grad_blended[rows, pl.ds(at, 128)],
+                keep,
+            )
+            grad_packed[rows, pl.ds(at, 128)] = dq
+            grad_packed[rows, pl.ds(at + D, 128)] = dk
+            grad_packed[rows, pl.ds(at + 2 * D, 128)] = dv
+        return carry
+
+    lax.fori_loop(0, HEADS // 2, heads, 0)
+
+
+def spatial_back_norm(*refs):
+    grad_packed, branch, grad_after, after, params_ref, small_in, w_entry, w_exit = refs[:8]
+    grad_first, branch_first, d0, d1, d2, d3, small = refs[8:]
+    me = lax.axis_index("frame")
+    params = params_ref[...]
+    dn = nt(grad_packed[...], w_entry[...]).astype(BF).astype(F32)
+    unit, scale = normalised(after[...])
+    inner, dgain, dshift = norm_back(dn, unit, scale, small_row(params, 1))
+    first = grad_after[...] + inner
+    grad_first[...] = first
+    low = first.astype(BF)
+    branch_first[...] = low
+    back = nt(low, w_exit[...]).astype(BF)
+    pieces = nn(piece_from_frame(me), back).astype(BF)
+    for k, ref in enumerate((d0, d1, d2, d3)):
+        ref[...] = pieces[k * PIECE : (k + 1) * PIECE]
+    small[...] = small_in[...]
+    small[1:2, :] = dgain
+    small[4:5, :] = dshift
+    small[6:7, :] = jnp.sum(low.astype(F32), axis=0, keepdims=True)
+    small[7:8, :] = jnp.sum(branch[...].astype(F32), axis=0, keepdims=True)
+
+
+def temporal_back(*refs):
+    xs, gs, refs = refs[:4], refs[4:8], refs[8:]
+    packed, params_ref, small_in, weights = refs[:4]
+    grad_packed, n0, n1, n2, n3, small = refs[4:10]
+    stack, grads = refs[10:]
+    params = params_ref[...]
+    for k, ref in enumerate(gs):
+        stack[pl.ds(k * PIECE, PIECE), :] = ref[...]
+    grads[...] = nn(place_from_piece(), stack[...]).astype(BF)
+    r = lax.broadcasted_iota(jnp.int32, (GROUP, GROUP), 0)
+    c = lax.broadcasted_iota(jnp.int32, (GROUP, GROUP), 1)
+    keep = (r >> 3) == (c >> 3)
+
+    def heads(i, carry):
+        at = pl.multiple_of(i * 128, 128)
+        for t in range(SPOTS // GROUP):
+            rows = pl.ds(t * GROUP, GROUP)
+            dq, dk, dv = attend_block_back(
+                packed[rows, pl.ds(at, 128)],
+                packed[rows, pl.ds(at + D, 128)],
+                packed[rows, pl.ds(at + 2 * D, 128)],
+                grads[rows, pl.ds(at, 128)],
+                keep,
+            )
+            grad_packed[rows, pl.ds(at, 128)] = dq
+            grad_packed[rows, pl.ds(at + D, 128)] = dk
+            grad_packed[rows, pl.ds(at + 2 * D, 128)] = dv
+        return carry
+
+    lax.fori_loop(0, HEADS // 2, heads, 0)
+    dn = nt(grad_packed[...], weights[...]).astype(BF)
+    pieces = nn(piece_from_place(), dn)
+    low = pieces.astype(BF)
+    for k, ref in enumerate((n0, n1, n2, n3)):
+        ref[...] = low[k * PIECE : (k + 1) * PIECE]
+    for k, ref in enumerate(xs):
+        stack[pl.ds(k * PIECE, PIECE), :] = ref[...]
+    unit, _ = normalised(stack[...].astype(F32))
+    small[...] = small_in[...]
+    small[0:1, :] = jnp.sum(pieces * unit, axis=0, keepdims=True)
+    small[3:4, :] = jnp.sum(pieces, axis=0, keepdims=True)
+
+
+def input_back(video, grad_first, params_ref, n0, n1, n2, n3, out, stack):
+    me = lax.axis_index("frame")
+    for k, ref in enumerate((n0, n1, n2, n3)):
+        stack[pl.ds(k * PIECE, PIECE), :] = ref[...]
+    dn = nn(frame_from_piece(me), stack[...])
+    unit, scale = normalised(video[...].astype(F32))
+    moved = dn * small_row(params_ref[...], 0)
+    inner = scale * (
+        moved
+        - jnp.mean(moved, axis=-1, keepdims=True)
+        - unit * jnp.mean(moved * unit, axis=-1, keepdims=True)
+    )
+    out[...] = grad_first[...] + inner
+
+
+def weight_grads(where, a_one, b_one, a_two, b_two, keep, send, shuffle):
+    step = pl.program_id(0)
+    own = where[0]
+
+    @pl.when(step < 2)
+    def _():
+        shuffle[...] = tn(a_one[...], b_one[...])
+
+    @pl.when(step >= 2)
+    def _():
+        shuffle[...] = tn(a_two[...], b_two[...])
+
+    for j in range(4):
+        for parity, ref in ((0, keep), (1, send)):
+            rows = pl.ds(pl.multiple_of((own ^ (2 * j + parity)) * SHARD, 8), SHARD)
+            ref[j] = shuffle[rows, :].astype(BF)
+
+
+def shape(*dims, dtype=BF):
+    return jax.ShapeDtypeStruct(dims, dtype)
+
+
+def cost(flops, nbytes, exps=0):
+    return pl.CostEstimate(flops=int(flops), bytes_accessed=int(nbytes), transcendentals=int(exps))
+
+
+def limit(mebibytes):
+    return pltpu.CompilerParams(vmem_limit_bytes=mebibytes << 20)
+
+
+CORE = [(i, i ^ 1) for i in range(8)]
+ACROSS = [(i, i ^ 2) for i in range(8)]
+UP = [(i, i ^ 4) for i in range(8)]
+NEAR = [(i, i ^ 1) for i in range(4)]
+FAR = [(i, i ^ 2) for i in range(4)]
+
+
+def swap(value, pairs, axis="fsdp"):
+    return lax.ppermute(value, axis, pairs)
+
+
+def shift(value, by):
+    return lax.ppermute(value, "frame", [(i, (i + by) % 4) for i in range(4)])
+
+
+def gather_pieces(first, second):
+    first_x = swap(first, ACROSS)
+    second_y = swap(second, UP)
+    first_two = swap(jnp.stack([first, first_x]), UP)
+    second_two = swap(jnp.stack([second, second_y]), ACROSS)
+    mine = (first, second, first_x, second_y, first_two, second_two)
+    return mine + tuple(swap(v, CORE) for v in mine)
+
+
+def reduce_shards(keep, send, frame):
+    got = [swap(v, CORE) for v in send]
+    sums = [k.astype(F32) + g.astype(F32) for k, g in zip(keep, got, strict=True)]
+    stack = lambda parts: jnp.stack(parts)
+    for_x = stack([t[j, :HALF] for t in sums for j in (1, 3)]).astype(BF)
+    for_y = stack([t[j, HALF:] for t in sums for j in (2, 3)]).astype(BF)
+    from_x = swap(for_x, ACROSS).astype(F32)
+    from_y = swap(for_y, UP).astype(F32)
+    count = len(keep)
+    next_y = stack([sums[i][2, :HALF] + from_x[2 * i + 1] for i in range(count)]).astype(BF)
+    next_x = stack([sums[i][1, HALF:] + from_y[2 * i + 1] for i in range(count)]).astype(BF)
+    got_y = swap(next_y, UP).astype(F32)
+    got_x = swap(next_x, ACROSS).astype(F32)
+    first = stack([sums[i][0, :HALF] + from_x[2 * i] + got_y[i] for i in range(count)])
+    second = stack([sums[i][0, HALF:] + from_y[2 * i] + got_x[i] for i in range(count)])
+    odd = (frame & 1) == 1
+    out = jnp.where(odd, first, second).astype(BF)
+    held = jnp.where(odd, second, first)
+    pair = (held + swap(out, NEAR, "frame").astype(F32)).astype(BF)
+    full = (pair.astype(F32) + swap(pair, FAR, "frame").astype(F32)).astype(BF)
+    other = swap(full, NEAR, "frame")
+    low = jnp.where(odd, other, full)
+    high = jnp.where(odd, full, other)
+    return [
+        jnp.concatenate([low[i], high[i]], axis=0).astype(F32) for i in range(count)
+    ]
+
+
+def reduce_small(small):
+    for pairs in (CORE, ACROSS, UP):
+        small = small + swap(small, pairs)
+    for pairs in (NEAR, FAR):
+        small = small + swap(small, pairs, "frame")
+    return small
+
+
+def spread(shard, own, width):
+    lanes = jnp.arange(8 * width) // width
+    return jnp.where((lanes == own)[None, :], jnp.tile(shard, (1, 8)), jnp.zeros((), shard.dtype))
+
+
+def body(
+    video,
+    temporal_entry,
+    temporal_exit,
+    spatial_entry,
+    spatial_exit,
+    expand_weight,
+    contract_weight,
+    layer_gains,
+    layer_shifts,
+    branch_biases,
+    expand_bias,
+    cotangent,
+):
+    own = lax.axis_index("fsdp")
+    frame = lax.axis_index("frame")
+    where = jnp.stack([own, frame]).astype(jnp.int32)
+
+    contract_rows = contract_weight.reshape(4, SHARD, D).transpose(1, 0, 2).reshape(SHARD, WIDE)
+    forward_weights = lax.all_gather(
+        jnp.concatenate([expand_weight, contract_rows], axis=0), "fsdp", axis=0, tiled=True
+    ).reshape(8, 2, SHARD, WIDE)
+
+    small_rows = jnp.concatenate(
+        [
+            spread(layer_gains, own, SHARD),
+            spread(layer_shifts, own, SHARD),
+            spread(branch_biases, own, SHARD),
+            spread(expand_bias.reshape(1, 384), own, 384).reshape(4, D),
+            jnp.zeros((11, D), BF),
+        ],
+        axis=0,
+    )
+    small_rows = jnp.concatenate([small_rows[0:8], small_rows[8:16], small_rows[16:24]], axis=1)
+    entry_pieces = gather_pieces(
+        jnp.concatenate([temporal_entry[:HALF], small_rows], axis=0), temporal_entry[HALF:]
+    )
+    plane = jnp.concatenate([temporal_exit, spatial_entry, spatial_exit], axis=1)
+
+    by_place = jnp.pad(
+        video.reshape(2, 4, HERE, D).transpose(1, 0, 2, 3).reshape(4, 2 * HERE, D),
+        ((0, 0), (0, PIECE - 2 * HERE), (0, 0)),
+    )
+    pick = lambda k: lax.dynamic_index_in_dim(by_place, (frame + k) & 3, keepdims=False)
+    video_pieces = [pick(0)] + [shift(pick(k), k) for k in (1, 2, 3)]
+    pad_rows = lambda v: jnp.pad(
+        v.reshape(2, PLACES, D), ((0, 0), (0, FRAME_ROWS - PLACES), (0, 0))
+    ).reshape(ROWS, D)
+    tokens = pad_rows(video)
+    cot = pad_rows(cotangent)
+
+    forward = pl.pallas_call(
+        temporal_forward,
+        name="temporal_forward",
+        out_shape=[shape(PIECE, D)] * 4
+        + [
+            shape(SPOTS, D),
+            shape(SPOTS, 3 * D),
+            shape(D, 3 * D),
+            shape(8, 3 * D, dtype=F32),
+            shape(8, 384, dtype=F32),
+        ],
+        in_specs=[VMEM] * 4 + [HBM] * 12,
+        out_specs=[VMEM] * 6 + [HBM] + [VMEM] * 2,
+        scratch_shapes=[
+            pltpu.VMEM((D, 3 * D), BF),
+            pltpu.VMEM((8, 8, 3 * D), BF),
+            pltpu.VMEM((ROWS, D), BF),
+            pltpu.VMEM((SPOTS, D), BF),
+            pltpu.SemaphoreType.DMA((24,)),
+            pltpu.SemaphoreType.DMA,
+        ],
+        compiler_params=limit(32),
+        cost_estimate=cost(3e9, 12e6, 2e6),
+    )(*video_pieces, *entry_pieces)
+    places, (normed_place, packed_place, entry_full, params, bias_full) = forward[:4], forward[4:]
+    blended_pieces = [places[0]] + [shift(places[k], -k) for k in (1, 2, 3)]
+
+    plane_pieces = gather_pieces(plane[:HALF], plane[HALF:])
+    (
+        after_time,
+        normed_two,
+        packed_space,
+        blended_space,
+        after_space,
+        normed_three,
+        blended_time,
+        exit_full,
+        space_full,
+        last_full,
+    ) = pl.pallas_call(
+        spatial_forward,
+        name="spatial_forward",
+        out_shape=[
+            shape(ROWS, D, dtype=F32),
+            shape(ROWS, D),
+            shape(ROWS, 3 * D),
+            shape(ROWS, D),
+            shape(ROWS, D, dtype=F32),
+            shape(ROWS, D),
+            shape(ROWS, D),
+            shape(D, D),
+            shape(D, 3 * D),
+            shape(D, D),
+        ],
+        in_specs=[VMEM] * 6 + [HBM] * 12,
+        out_specs=[VMEM] * 7 + [HBM] * 3,
+        scratch_shapes=[
+            pltpu.VMEM((D, 5 * D), BF),
+            pltpu.VMEM((ROWS, D), BF),
+            pltpu.SemaphoreType.DMA((16,)),
+            pltpu.SemaphoreType.DMA((3,)),
+        ],
+        compiler_params=limit(36),
+        cost_estimate=cost(6e9, 20e6, 2e6),
+    )(tokens, params, *blended_pieces, *plane_pieces)
+
+    whole = lambda *dims: pl.BlockSpec(dims, lambda i, w: (0,) * len(dims))
+    (
+        output,
+        grad_after,
+        branch_last,
+        keep_we,
+        send_we,
+        keep_wc,
+        send_wc,
+        small,
+    ) = pl.pallas_call(
+        feed_forward,
+        name="feed_forward",
+        out_shape=[
+            shape(ROWS, D),
+            shape(ROWS, D, dtype=F32),
+            shape(ROWS, D),
+            shape(4, SHARD, WIDE),
+            shape(4, SHARD, WIDE),
+            shape(4, SHARD, WIDE),
+            shape(4, SHARD, WIDE),
+            shape(16, D, dtype=F32),
+        ],
+        grid_spec=pltpu.PrefetchScalarGridSpec(
+            num_scalar_prefetch=1,
+            grid=(8,),
+            in_specs=[
+                whole(ROWS, D),
+                whole(ROWS, D),
+                whole(ROWS, D),
+                whole(8, 3 * D),
+                whole(8, 384),
+                pl.BlockSpec((8, None, SHARD, 384), lambda i, w: (0, 0, 0, w[0] ^ i)),
+                pl.BlockSpec((1, 1, SHARD, WIDE), lambda i, w: (w[0] ^ i, 1, 0, 0)),
+            ],
+            out_specs=[
+                whole(ROWS, D),
+                whole(ROWS, D),
+                whole(ROWS, D),
+                pl.BlockSpec((4, SHARD, 384), lambda i, w: (0, 0, w[0] ^ i)),
+                pl.BlockSpec((4, SHARD, 384), lambda i, w: (0, 0, w[0] ^ i)),
+                pl.BlockSpec((1, SHARD, WIDE), lambda i, w: (i // 2, 0, 0)),
+                pl.BlockSpec((1, SHARD, WIDE), lambda i, w: (i // 2, 0, 0)),
+                whole(16, D),
+            ],
+            scratch_shapes=[
+                pltpu.VMEM((ROWS, D), F32),
+                pltpu.VMEM((ROWS, D), F32),
+                pltpu.VMEM((D, 384), F32),
+            ],
+        ),
+        compiler_params=limit(40),
+        cost_estimate=cost(12e9, 30e6, 4e6),
+    )(where, normed_three, after_space, cot, params, bias_full, forward_weights, forward_weights)
+    sums_forward = reduce_shards([keep_we, keep_wc], [send_we, send_wc], frame)
+
+    grad_packed = pl.pallas_call(
+        spatial_back,
+        name="spatial_back",
+        out_shape=shape(ROWS, 3 * D),
+        in_specs=[VMEM] * 3,
+        out_specs=VMEM,
+        scratch_shapes=[pltpu.VMEM((ROWS, D), BF)],
+        compiler_params=limit(24),
+        cost_estimate=cost(3e9, 6e6, 2e6),
+    )(branch_last, packed_space, last_full)
+    back = pl.pallas_call(
+        spatial_back_norm,
+        name="spatial_back_norm",
+        out_shape=[shape(ROWS, D, dtype=F32), shape(ROWS, D)]
+        + [shape(PIECE, D)] * 4
+        + [shape(16, D, dtype=F32)],
+        in_specs=[VMEM] * 8,
+        out_specs=[VMEM] * 7,
+        compiler_params=limit(32),
+        cost_estimate=cost(3e9, 12e6, 0),
+    )(grad_packed, branch_last, grad_after, after_time, params, small, space_full, exit_full)
+    grad_first, branch_first, back_pieces, small = back[0], back[1], back[2:6], back[6]
+    grad_pieces = [back_pieces[0]] + [shift(back_pieces[k], k) for k in (1, 2, 3)]
+
+    def grads(a_one, b_one, a_two, b_two):
+        return pl.pallas_call(
+            weight_grads,
+            name="weight_grads",
+            out_shape=[shape(4, SHARD, WIDE)] * 2,
+            grid_spec=pltpu.PrefetchScalarGridSpec(
+                num_scalar_prefetch=1,
+                grid=(8,),
+                in_specs=[
+                    whole(*a_one.shape),
+                    pl.BlockSpec((b_one.shape[0], 384), lambda i, w: (0, jnp.minimum(i, 1))),
+                    whole(*a_two.shape),
+                    pl.BlockSpec((b_two.shape[0], 384), lambda i, w: (0, jnp.maximum(i - 2, 0))),
+                ],
+                out_specs=[pl.BlockSpec((4, SHARD, 384), lambda i, w: (0, 0, i))] * 2,
+                scratch_shapes=[pltpu.VMEM((D, 384), F32)],
+            ),
+            compiler_params=limit(24),
+            cost_estimate=cost(2e9, 10e6, 0),
+        )(where, a_one, b_one, a_two, b_two)
+
+    keep_space, send_space = grads(blended_space, branch_last, normed_two, grad_packed)
+    sums_space = reduce_shards([keep_space], [send_space], frame)[0]
+
+    back = pl.pallas_call(
+        temporal_back,
+        name="temporal_back",
+        out_shape=[shape(SPOTS, 3 * D)] + [shape(PIECE, D)] * 4 + [shape(16, D, dtype=F32)],
+        in_specs=[VMEM] * 12,
+        out_specs=[VMEM] * 6,
+        scratch_shapes=[pltpu.VMEM((ROWS, D), BF), pltpu.VMEM((SPOTS, D), BF)],
+        compiler_params=limit(32),
+        cost_estimate=cost(4e9, 10e6, 2e6),
+    )(*video_pieces, *grad_pieces, packed_place, params, small, entry_full)
+    grad_place, normed_pieces, small = back[0], back[1:5], back[5]
+    normed_back = [normed_pieces[0]] + [shift(normed_pieces[k], -k) for k in (1, 2, 3)]
+
+    keep_time, send_time = grads(blended_time, branch_first, normed_place, grad_place)
+    sums_time = reduce_shards([keep_time], [send_time], frame)[0]
+    small = reduce_small(small)
+
+    input_grad = pl.pallas_call(
+        input_back,
+        name="input_back",
+        out_shape=shape(ROWS, D, dtype=F32),
+        in_specs=[VMEM] * 7,
+        out_specs=VMEM,
+        scratch_shapes=[pltpu.VMEM((ROWS, D), BF)],
+        compiler_params=limit(24),
+        cost_estimate=cost(1e9, 5e6, 0),
+    )(tokens, grad_first, params, *normed_back)
+
+    drop = lambda v: v.reshape(2, FRAME_ROWS, D)[:, :PLACES].reshape(video.shape)
+    mine = lax.dynamic_slice_in_dim(small[:9], own * SHARD, SHARD, axis=1)
+    return (
+        drop(output),
+        drop(input_grad),
+        sums_time[:, D:],
+        sums_time[:, :D],
+        sums_space[:, D:],
+        sums_space[:, :D],
+        sums_forward[0],
+        sums_forward[1].reshape(SHARD, 4, D).transpose(1, 0, 2).reshape(384, D),
+        mine[0:3],
+        mine[3:6],
+        mine[6:9],
+        lax.dynamic_slice_in_dim(small[9:13].reshape(WIDE), own * 384, 384),
+    )
+
+
 def solution(mesh):
     placed = (
         P("fsdp", "frame", None, None),
@@ -370,8 +1196,9 @@
         P("fsdp"),
         P("fsdp", "frame", None, None),
     )
+    special = mesh.shape["fsdp"] == 8 and mesh.shape["frame"] == 4
     return jax.shard_map(
-        body,
+        body if special else general_body,
         mesh=mesh,
         in_specs=placed,
         out_specs=(

time: 905 us -> 477 us (0.53)
  blocking collectives: 259 us -> 0 us
  waiting for transfers between devices: 339 us -> 210 us
  matrix products: 114 us -> 0 us
  Pallas kernels: 0 us -> 114 us
  local copies, waits for them, and re-layouts: 116 us -> 43.6 us
  starting transfers between devices: 13.4 us -> 66.2 us
  other arithmetic: 37.4 us -> 20.4 us
    ppermute x0 -> x62, waiting for transfers between devices: none -> 210 us  [the longest x50 188 us: swap(): return lax.ppermute(value, axis, pairs)]
    reduce_scatter x12 -> x0, waiting for transfers between devices: 199 us -> none  [the longest x1 74.1 us: body(): lax.psum_scatter(grad_expand, 'fsdp', scatter_dimension=0, tiled=True)]
    all_gather x13 -> x0, blocking collectives: 165 us -> none  [the longest x1 20.6 us: body(): lax.all_gather(shares[4].astype(jnp.bfloat16), 'frame', axis=0, tiled=True)]
    pallas_call x0 -> x9, Pallas kernels: none -> 114 us  [the longest x1 27.6 us: body(): pl.pallas_call(feed_forward, name='feed_forward', out_shape=[shape(ROWS,...]
    dot_general x30 -> x0, matrix products: 114 us -> none  [the longest x6 37.5 us: dense(): return jnp.dot(first_op, second_op, preferred_element_type=jnp.float32)]
    ppermute x0 -> x62, starting transfers between devices: none -> 66.2 us  [the longest x50 45.7 us: swap(): return lax.ppermute(value, axis, pairs)]
    all_to_all x3 -> x0, waiting for transfers between devices: 60.1 us -> none  [the longest x1 44.6 us: body(): lax.all_to_all(grad_packed_place, 'frame', split_axis=1, concat_axis=2, t...]
    unnamed x24 -> x1, waiting for transfers between devices: 60 us -> 0.02 us
  transfers between devices with their start and end apart: 24 -> 63, of which waited for: 15 -> 27; matrix products, arithmetic and copies ran while one was open for 26% -> 7% of each run, Pallas kernels for 0% -> 18%
where the time goes in v1:
time: 477 us; the launch traced here: 470 us
  waiting for transfers between devices  210 us (44%)
  Pallas kernels  114 us (24%)
  starting transfers between devices  66.2 us (14%)
  local copies, waits for them, and re-layouts  43.6 us (9%)
  other arithmetic  20.4 us (4%)
  between operations  15.6 us (3%)
    ppermute x50, waiting for transfers between devices, swap(): return lax.ppermute(value, axis, pairs)  188 us
    ppermute x50, starting transfers between devices, swap(): return lax.ppermute(value, axis, pairs)  45.7 us
    unnamed x150, local copies, waits for them, and re-layouts  29.5 us
    pallas_call x1, Pallas kernels, body(): pl.pallas_call(feed_forward, name='feed_forward', out_shape=[shape(ROWS,...  27.6 us
    ppermute x12, waiting for transfers between devices, shift(): return lax.ppermute(value, 'frame', [(i, (i + by) % 4) for i in range(4)])  22.2 us
    pallas_call x1, Pallas kernels, body(): pl.pallas_call(temporal_back, name='temporal_back', out_shape=[shape(SPOT...  21.2 us
    ppermute x12, starting transfers between devices, shift(): return lax.ppermute(value, 'frame', [(i, (i + by) % 4) for i in range(4)])  20.5 us
    pallas_call x1, Pallas kernels, body(): pl.pallas_call(temporal_forward, name='temporal_forward', out_shape=[shap...  16.7 us
  transfers between devices with their start and end apart: 63, of which 27 were waited for; matrix products, arithmetic and copies ran while one was open for 7% of the time, Pallas kernels for 18%

profile of v1, /device:TPU:0, one launch (start us, length us, event | category | flops | bytes accessed | tf_op | source)
XLA Modules:
  0.0 470.2 jit_solution(16293539919286728484)
XLA Ops:
  11.0 3.0 collective-permute-start.3
  16.3 3.5 pad_dynamic-slice_fusion
  25.9 8.1 %collective-permute-done.16.refs_8_ = bf16[48,3840]{1,0:T(8,128)(2,1)S(1)} collective-permute-done((bf16[48,3840]{1,0:T(8,128)(2,1)S(1)}, bf16[48,3840]{1,0:T(8,128)(2,1)S(1)}, u32[]{:S(2)}, u32[]{:S(2)}) %collective-permute-start.16) | collective-permute-done | bytes 368672 | tf_op jit(solution)/shard_map/ppermute | solution.py:860
  35.5 9.5 %collective-permute-done.17.refs_9_ = bf16[48,3840]{1,0:T(8,128)(2,1)S(1)} collective-permute-done((bf16[48,3840]{1,0:T(8,128)(2,1)S(1)}, bf16[48,3840]{1,0:T(8,128)(2,1)S(1)}, u32[]{:S(2)}, u32[]{:S(2)}) %collective-permute-start.17) | collective-permute-done | bytes 368672 | tf_op jit(solution)/shard_map/ppermute | solution.py:860
  47.5 9.1 %collective-permute-done.4.refs_7_ = bf16[48,2304]{1,0:T(8,128)(2,1)S(1)} collective-permute-done((bf16[48,2304]{1,0:T(8,128)(2,1)S(1)}, bf16[48,2304]{1,0:T(8,128)(2,1)S(1)}, u32[]{:S(2)}, u32[]{:S(2)}) %collective-permute-start.4) | collective-permute-done | bytes 221216 | tf_op jit(solution)/shard_map/ppermute | solution.py:860
  58.7 20.0 %collective-permute-done.5.refs_8_ = bf16[2,56,2304]{2,1,0:T(8,128)(2,1)S(1)} collective-permute-done((bf16[2,56,2304]{2,1,0:T(8,128)(2,1)S(1)}, bf16[2,56,2304]{2,1,0:T(8,128)(2,1)S(1)}, u32[]{:S(2)}, u32[]{:S(2)}) %collective-permute-start.5) | collective-permute-done | bytes 516128 | tf_op jit(solution)/shard_map/ppermute | solution.py:860
  79.2 21.2 %collective-permute-done.6.refs_9_ = bf16[2,48,2304]{2,1,0:T(8,128)(2,1)S(1)} collective-permute-done((bf16[2,48,2304]{2,1,0:T(8,128)(2,1)S(1)}, bf16[2,48,2304]{2,1,0:T(8,128)(2,1)S(1)}, u32[]{:S(2)}, u32[]{:S(2)}) %collective-permute-start.6) | collective-permute-done | bytes 442400 | tf_op jit(solution)/shard_map/ppermute | solution.py:860
  104.3 16.7 %temporal_forward.1 = (bf16[104,768]{1,0:T(8,128)(2,1)S(1)}, bf16[104,768]{1,0:T(8,128)(2,1)S(1)}, bf16[104,768]{1,0:T(8,128)(2,1)S(1)}, bf16[104,768]{1,0:T(8,1...) custom-call(bf16[104,768]{1,0:T(8,128)(2,1)S(1)} %bitcast.73, ...), custom_call_target="tpu_custom_call" | custom-call | flops 3000000000 | bytes 12000000 | tf_op jit(solution)/shard_map/temporal_forward/pallas_call | solution.py:968
  123.2 3.4 collective-permute-start.13
  131.1 9.8 %collective-permute-done.14.refs_4_ = bf16[104,768]{1,0:T(8,128)(2,1)S(1)} collective-permute-done((bf16[104,768]{1,0:T(8,128)(2,1)S(1)}, bf16[104,768]{1,0:T(8,128)(2,1)S(1)}, u32[]{:S(2)}, u32[]{:S(2)}) %collective-permute-start.14) | collective-permute-done | bytes 159776 | tf_op jit(solution)/shard_map/ppermute | solution.py:864
  140.9 15.3 %spatial_forward.1 = (f32[416,768]{1,0:T(8,128)S(1)}, bf16[416,768]{1,0:T(8,128)(2,1)S(1)}, bf16[416,2304]{1,0:T(8,128)(2,1)S(1)}, bf16[416,768]{1,0:T(8,128)(2,...) custom-call(bf16[416,768]{1,0:T(8,128)(2,1)S(1)} %bitcast.64, ...), custom_call_target="tpu_custom_call" | custom-call | flops 6000000000 | bytes 20000000 | tf_op jit(solution)/shard_map/spatial_forward/pallas_call | solution.py:1007
  169.3 27.6 %feed_forward.1 = (bf16[416,768]{1,0:T(8,128)(2,1)S(1)}, f32[416,768]{1,0:T(8,128)S(1)}, bf16[416,768]{1,0:T(8,128)(2,1)S(1)}, bf16[4,96,3072]{2,1,0:T(8,128)(2,...) custom-call(s32[2]{0:T(128)S(1)} %pad_add_fusion.where, ...), custom_call_target="tpu_custom_call" | custom-call | flops 12000000000 | bytes 30000000 | tf_op jit(solution)/shard_map/feed_forward/pallas_call | solution.py:1044
  197.5 12.7 %spatial_back.1.refs_0_.b_two = bf16[416,2304]{1,0:T(8,128)(2,1)S(1)} custom-call(bf16[416,768]{1,0:T(8,128)(2,1)S(1)} %get-tuple-element.65.branch.refs_1_.b_one, bf16[416,2304]{1,0:T(8,128)(2,1)S(1)} %copy-done.36, bf16[768,768]{1,0:T(8,128)(2,1)S(1)} %copy-done.48), custom_call_target="tpu_custom_call" | custom-call | flops 3000000000 | bytes 6000000 | tf_op jit(solution)/shard_map/spatial_back/pallas_call | solution.py:1090
  210.4 4.0 spatial_back_norm.1
  217.2 2.8 collective-permute-start.28
  220.1 3.3 collective-permute-done.26.refs_5_
  223.4 6.0 %collective-permute-done.27.refs_6_ = bf16[104,768]{1,0:T(8,128)(2,1)S(1)} collective-permute-done((bf16[104,768]{1,0:T(8,128)(2,1)S(1)}, bf16[104,768]{1,0:T(8,128)(2,1)S(1)}, u32[]{:S(2)}, u32[]{:S(2)}) %collective-permute-start.27) | collective-permute-done | bytes 159776 | tf_op jit(solution)/shard_map/ppermute | solution.py:864
  229.4 21.2 %temporal_back.1 = (bf16[400,2304]{1,0:T(8,128)(2,1)S(1)}, bf16[104,768]{1,0:T(8,128)(2,1)S(1)}, bf16[104,768]{1,0:T(8,128)(2,1)S(1)}, bf16[104,768]{1,0:T(8,128...) custom-call(bf16[104,768]{1,0:T(8,128)(2,1)S(1)} %bitcast.74, ...), custom_call_target="tpu_custom_call" | custom-call | flops 4000000000 | bytes 10000000 | tf_op jit(solution)/shard_map/temporal_back/pallas_call | solution.py:1138
  259.8 3.6 collective-permute-done.59
  263.4 3.5 collective-permute-start.60
  271.7 7.6 %weight_grads.3 = (bf16[4,96,3072]{2,1,0:T(8,128)(2,1)S(1)}, bf16[4,96,3072]{2,1,0:T(8,128)(2,1)}) custom-call(s32[2]{0:T(128)S(1)} %pad_add_fusion.where, bf16[416,768]{1,0:T(8,128)(2,1)S(1)} %copy-done.40, bf16[416,768]{1,0:T(8,128)(2,1)S(1)} %copy-done.30, bf16[416,768]{1,0:T(8,128)(2,1)S(1)} %copy-done.38, bf16[416,2304]{1,0:T(8,128)(2,1)S(1)} %copy-done.22), custom_call_target="tpu_custom_call" | custom-call | flops 2000000000 | bytes 10000000 | tf_op jit(solution)/shard_map/weight_grads/pallas_call | solution.py:1115
  286.4 7.9 %weight_grads.2 = (bf16[4,96,3072]{2,1,0:T(8,128)(2,1)S(1)}, bf16[4,96,3072]{2,1,0:T(8,128)(2,1)}) custom-call(s32[2]{0:T(128)S(1)} %pad_add_fusion.where, bf16[416,768]{1,0:T(8,128)(2,1)S(1)} %copy-done.42, bf16[416,768]{1,0:T(8,128)(2,1)S(1)} %copy-done.28, bf16[400,768]{1,0:T(8,128)(2,1)S(1)} %copy-done.44, bf16[400,2304]{1,0:T(8,128)(2,1)S(1)} %copy-done.32), custom_call_target="tpu_custom_call" | custom-call | flops 2000000000 | bytes 10000000 | tf_op jit(solution)/shard_map/weight_grads/pallas_call | solution.py:1115
  303.7 3.3 convert_add_fusion.1
  321.3 30.2 %collective-permute-done.43 = bf16[2,48,3072]{2,1,0:T(8,128)(2,1)S(1)} collective-permute-done((bf16[2,48,3072]{2,1,0:T(8,128)(2,1)S(1)}, bf16[2,48,3072]{2,1,0:T(8,128)(2,1)S(1)}, u32[]{:S(2)}, u32[]{:S(2)}) %collective-permute-start.43) | collective-permute-done | bytes 589856 | tf_op jit(solution)/shard_map/ppermute | solution.py:860
  354.0 10.2 %collective-permute-done.35 = bf16[2,48,3072]{2,1,0:T(8,128)(2,1)S(1)} collective-permute-done((bf16[2,48,3072]{2,1,0:T(8,128)(2,1)S(1)}, bf16[2,48,3072]{2,1,0:T(8,128)(2,1)S(1)}, u32[]{:S(2)}, u32[]{:S(2)}) %collective-permute-start.35) | collective-permute-done | bytes 589856 | tf_op jit(solution)/shard_map/ppermute | solution.py:860
  366.6 3.9 collective-permute-done.42
  379.1 7.3 %collective-permute-start.46 = (bf16[1,48,3072]{2,1,0:T(8,128)(2,1)S(1)}, bf16[1,48,3072]{2,1,0:T(8,128)(2,1)S(1)}, u32[]{:S(2)}, u32[]{:S(2)}) collective-permute-start(bf16[1,48,3072]{2,1,0:T(8,128)(2,1)S(1)} %add_convert_fusion.3), channel_id=1, source_target_pairs={{0,16},{8,24},{16,0},{24,8},{1,17},{9,25},{17,1},{25,9},{2,18},{10... | collective-permute-start | bytes 884744 | tf_op jit(solution)/shard_map/ppermute | solution.py:860
  390.7 6.4 %collective-permute-done.51 = bf16[2,48,3072]{2,1,0:T(8,128)(2,1)S(1)} collective-permute-done((bf16[2,48,3072]{2,1,0:T(8,128)(2,1)S(1)}, bf16[2,48,3072]{2,1,0:T(8,128)(2,1)S(1)}, u32[]{:S(2)}, u32[]{:S(2)}) %collective-permute-start.51) | collective-permute-done | bytes 589856 | tf_op jit(solution)/shard_map/ppermute | solution.py:860
  397.9 6.0 %collective-permute-done.46 = bf16[1,48,3072]{2,1,0:T(8,128)(2,1)S(1)} collective-permute-done((bf16[1,48,3072]{2,1,0:T(8,128)(2,1)S(1)}, bf16[1,48,3072]{2,1,0:T(8,128)(2,1)S(1)}, u32[]{:S(2)}, u32[]{:S(2)}) %collective-permute-start.46) | collective-permute-done | bytes 294944 | tf_op jit(solution)/shard_map/ppermute | solution.py:860
  410.7 18.5 %collective-permute-done.54 = bf16[2,48,3072]{2,1,0:T(8,128)(2,1)S(1)} collective-permute-done((bf16[2,48,3072]{2,1,0:T(8,128)(2,1)S(1)}, bf16[2,48,3072]{2,1,0:T(8,128)(2,1)S(1)}, u32[]{:S(2)}, u32[]{:S(2)}) %collective-permute-start.54) | collective-permute-done | bytes 589856 | tf_op jit(solution)/shard_map/ppermute | solution.py:860
  431.5 15.6 %collective-permute-done.55 = bf16[2,48,3072]{2,1,0:T(8,128)(2,1)S(1)} collective-permute-done((bf16[2,48,3072]{2,1,0:T(8,128)(2,1)S(1)}, bf16[2,48,3072]{2,1,0:T(8,128)(2,1)S(1)}, u32[]{:S(2)}, u32[]{:S(2)}) %collective-permute-start.55) | collective-permute-done | bytes 589856 | tf_op jit(solution)/shard_map/ppermute | solution.py:860
  449.4 10.2 %collective-permute-done.56 = bf16[2,48,3072]{2,1,0:T(8,128)(2,1)S(1)} collective-permute-done((bf16[2,48,3072]{2,1,0:T(8,128)(2,1)S(1)}, bf16[2,48,3072]{2,1,0:T(8,128)(2,1)S(1)}, u32[]{:S(2)}, u32[]{:S(2)}) %collective-permute-start.56) | collective-permute-done | bytes 589856 | tf_op jit(solution)/shard_map/ppermute | solution.py:860
  (350 shorter events, 123.1 us)
Async XLA Ops:
  7.2 157.9 %all-gather.2.cloned.1.call-start = ((), (), s32[]{:S(2)}) async-start(), calls=%async_computation | async-start | bytes 10616832 | tf_op jit(solution)/shard_map/all_gather | solution.py:936
  14.0 44.8 %collective-permute-start.7 = (bf16[56,2304]{1,0:T(8,128)(2,1)S(1)}, bf16[56,2304]{1,0:T(8,128)(2,1)S(1)}, u32[]{:S(2)}, u32[]{:S(2)}) collective-permute-start(bf16[56,2304]{1,0:T(8,128)(2,1)S(1)} %fusion.14.refs_4_), channel_id=1, source_target_pairs={{0,1},{1,0},{2,3},{3,2},{4,5},{5,4},{6,7},{7,6},{8,9},{9,8},{10,11... | collective-permute-start | bytes 774152 | tf_op jit(solution)/shard_map/ppermute | solution.py:860
  15.0 19.0 %collective-permute-start.16 = (bf16[48,3840]{1,0:T(8,128)(2,1)S(1)}, bf16[48,3840]{1,0:T(8,128)(2,1)S(1)}, u32[]{:S(2)}, u32[]{:S(2)}) collective-permute-start(bf16[48,3840]{1,0:T(8,128)(2,1)S(1)} %get-tuple-element.133.refs_6_), channel_id=1, source_target_pairs={{0,2},{1,3},{2,0},{3,1},{4,6},{5,7},{6,4},{7,5},{8,10},{9,11},{10,... | collective-permute-start | bytes 1105928 | tf_op jit(solution)/shard_map/ppermute | solution.py:860
  19.8 25.6 %collective-permute-start = (bf16[104,768]{1,0:T(8,128)(2,1)S(1)}, bf16[104,768]{1,0:T(8,128)(2,1)S(1)}, u32[]{:S(2)}, u32[]{:S(2)}) collective-permute-start(bf16[104,768]{1,0:T(8,128)(2,1)S(1)} %bitcast.86), channel_id=1, source_target_pairs={{0,8},{8,16},{16,24},{24,0},{1,9},{9,17},{17,25},{25,1},{2,10},{10... | collective-permute-start | bytes 479240 | tf_op jit(solution)/shard_map/ppermute | solution.py:864
  21.8 23.6 %collective-permute-start.1 = (bf16[104,768]{1,0:T(8,128)(2,1)S(1)}, bf16[104,768]{1,0:T(8,128)(2,1)S(1)}, u32[]{:S(2)}, u32[]{:S(2)}) collective-permute-start(bf16[104,768]{1,0:T(8,128)(2,1)S(1)} %bitcast.85), channel_id=1, source_target_pairs={{0,16},{8,24},{16,0},{24,8},{1,17},{9,25},{17,1},{25,9},{2,18},{10... | collective-permute-start | bytes 479240 | tf_op jit(solution)/shard_map/ppermute | solution.py:864
  24.5 22.7 %collective-permute-start.2 = (bf16[104,768]{1,0:T(8,128)(2,1)S(1)}, bf16[104,768]{1,0:T(8,128)(2,1)S(1)}, u32[]{:S(2)}, u32[]{:S(2)}) collective-permute-start(bf16[104,768]{1,0:T(8,128)(2,1)S(1)} %bitcast.84), channel_id=1, source_target_pairs={{0,24},{8,0},{16,8},{24,16},{1,25},{9,1},{17,9},{25,17},{2,26},{10... | collective-permute-start | bytes 479240 | tf_op jit(solution)/shard_map/ppermute | solution.py:864
  45.4 33.3 %collective-permute-start.5 = (bf16[2,56,2304]{2,1,0:T(8,128)(2,1)S(1)}, bf16[2,56,2304]{2,1,0:T(8,128)(2,1)S(1)}, u32[]{:S(2)}, u32[]{:S(2)}) collective-permute-start(bf16[2,56,2304]{2,1,0:T(8,128)(2,1)S(1)} %pad_maximum_fusion.11), channel_id=1, source_target_pairs={{0,4},{1,5},{2,6},{3,7},{4,0},{5,1},{6,2},{7,3},{8,12},{9,13},{10,... | collective-permute-start | bytes 1548296 | tf_op jit(solution)/shard_map/ppermute | solution.py:860
  47.2 55.9 %collective-permute-start.18 = (bf16[2,48,3840]{2,1,0:T(8,128)(2,1)S(1)}, bf16[2,48,3840]{2,1,0:T(8,128)(2,1)S(1)}, u32[]{:S(2)}, u32[]{:S(2)}) collective-permute-start(bf16[2,48,3840]{2,1,0:T(8,128)(2,1)S(1)} %pad_maximum_fusion.5), channel_id=1, source_target_pairs={{0,4},{1,5},{2,6},{3,7},{4,0},{5,1},{6,2},{7,3},{8,12},{9,13},{10,... | collective-permute-start | bytes 2211848 | tf_op jit(solution)/shard_map/ppermute | solution.py:860
  56.6 46.5 %collective-permute-start.19 = (bf16[2,48,3840]{2,1,0:T(8,128)(2,1)S(1)}, bf16[2,48,3840]{2,1,0:T(8,128)(2,1)S(1)}, u32[]{:S(2)}, u32[]{:S(2)}) collective-permute-start(bf16[2,48,3840]{2,1,0:T(8,128)(2,1)S(1)} %pad_maximum_fusion.6), channel_id=1, source_target_pairs={{0,2},{1,3},{2,0},{3,1},{4,6},{5,7},{6,4},{7,5},{8,10},{9,11},{10,... | collective-permute-start | bytes 2211848 | tf_op jit(solution)/shard_map/ppermute | solution.py:860
  57.5 42.9 %collective-permute-start.6 = (bf16[2,48,2304]{2,1,0:T(8,128)(2,1)S(1)}, bf16[2,48,2304]{2,1,0:T(8,128)(2,1)S(1)}, u32[]{:S(2)}, u32[]{:S(2)}) collective-permute-start(bf16[2,48,2304]{2,1,0:T(8,128)(2,1)S(1)} %pad_maximum_fusion.12), channel_id=1, source_target_pairs={{0,2},{1,3},{2,0},{3,1},{4,6},{5,7},{6,4},{7,5},{8,10},{9,11},{10,... | collective-permute-start | bytes 1327112 | tf_op jit(solution)/shard_map/ppermute | solution.py:860
  58.7 20.0 %collective-permute-start.20 = (bf16[48,3840]{1,0:T(8,128)(2,1)S(1)}, bf16[48,3840]{1,0:T(8,128)(2,1)S(1)}, u32[]{:S(2)}, u32[]{:S(2)}) collective-permute-start(bf16[48,3840]{1,0:T(8,128)(2,1)S(1)} %get-tuple-element.133.refs_6_), channel_id=1, source_target_pairs={{0,1},{1,0},{2,3},{3,2},{4,5},{5,4},{6,7},{7,6},{8,9},{9,8},{10,11... | collective-permute-start | bytes 1105928 | tf_op jit(solution)/shard_map/ppermute | solution.py:860
  78.7 25.4 %collective-permute-start.11 = (bf16[2,56,2304]{2,1,0:T(8,128)(2,1)S(1)}, bf16[2,56,2304]{2,1,0:T(8,128)(2,1)S(1)}, u32[]{:S(2)}, u32[]{:S(2)}) collective-permute-start(bf16[2,56,2304]{2,1,0:T(8,128)(2,1)S(1)} %collective-permute-done.5.refs_8_), channel_id=1, source_target_pairs={{0,1},{1,0},{2,3},{3,2},{4,5},{5,4},{6,7},{7,6},{8,9},{9,8},{10,11... | collective-permute-start | bytes 1548296 | tf_op jit(solution)/shard_map/ppermute | solution.py:860
  78.7 21.8 %collective-permute-start.10 = (bf16[48,2304]{1,0:T(8,128)(2,1)S(1)}, bf16[48,2304]{1,0:T(8,128)(2,1)S(1)}, u32[]{:S(2)}, u32[]{:S(2)}) collective-permute-start(bf16[48,2304]{1,0:T(8,128)(2,1)S(1)} %collective-permute-done.4.refs_7_), channel_id=1, source_target_pairs={{0,1},{1,0},{2,3},{3,2},{4,5},{5,4},{6,7},{7,6},{8,9},{9,8},{10,11... | collective-permute-start | bytes 663560 | tf_op jit(solution)/shard_map/ppermute | solution.py:860
  103.1 37.8 %collective-permute-start.24 = (bf16[2,48,3840]{2,1,0:T(8,128)(2,1)S(1)}, bf16[2,48,3840]{2,1,0:T(8,128)(2,1)S(1)}, u32[]{:S(2)}, u32[]{:S(2)}) collective-permute-start(bf16[2,48,3840]{2,1,0:T(8,128)(2,1)S(1)} %collective-permute-done.18.refs_10_), channel_id=1, source_target_pairs={{0,1},{1,0},{2,3},{3,2},{4,5},{5,4},{6,7},{7,6},{8,9},{9,8},{10,11... | collective-permute-start | bytes 2211848 | tf_op jit(solution)/shard_map/ppermute | solution.py:860
  103.1 37.8 %collective-permute-start.25 = (bf16[2,48,3840]{2,1,0:T(8,128)(2,1)S(1)}, bf16[2,48,3840]{2,1,0:T(8,128)(2,1)S(1)}, u32[]{:S(2)}, u32[]{:S(2)}) collective-permute-start(bf16[2,48,3840]{2,1,0:T(8,128)(2,1)S(1)} %collective-permute-done.19.refs_11_), channel_id=1, source_target_pairs={{0,1},{1,0},{2,3},{3,2},{4,5},{5,4},{6,7},{7,6},{8,9},{9,8},{10,11... | collective-permute-start | bytes 2211848 | tf_op jit(solution)/shard_map/ppermute | solution.py:860
  103.6 19.5 %collective-permute-start.21 = (bf16[48,3840]{1,0:T(8,128)(2,1)S(1)}, bf16[48,3840]{1,0:T(8,128)(2,1)S(1)}, u32[]{:S(2)}, u32[]{:S(2)}) collective-permute-start(bf16[48,3840]{1,0:T(8,128)(2,1)S(1)} %get-tuple-element.132.refs_7_), channel_id=1, source_target_pairs={{0,1},{1,0},{2,3},{3,2},{4,5},{5,4},{6,7},{7,6},{8,9},{9,8},{10,11... | collective-permute-start | bytes 1105928 | tf_op jit(solution)/shard_map/ppermute | solution.py:860
  103.7 22.8 %collective-permute-start.22 = (bf16[48,3840]{1,0:T(8,128)(2,1)S(1)}, bf16[48,3840]{1,0:T(8,128)(2,1)S(1)}, u32[]{:S(2)}, u32[]{:S(2)}) collective-permute-start(bf16[48,3840]{1,0:T(8,128)(2,1)S(1)} %collective-permute-done.16.refs_8_), channel_id=1, source_target_pairs={{0,1},{1,0},{2,3},{3,2},{4,5},{5,4},{6,7},{7,6},{8,9},{9,8},{10,11... | collective-permute-start | bytes 1105928 | tf_op jit(solution)/shard_map/ppermute | solution.py:860
  104.1 22.4 %collective-permute-start.23 = (bf16[48,3840]{1,0:T(8,128)(2,1)S(1)}, bf16[48,3840]{1,0:T(8,128)(2,1)S(1)}, u32[]{:S(2)}, u32[]{:S(2)}) collective-permute-start(bf16[48,3840]{1,0:T(8,128)(2,1)S(1)} %collective-permute-done.17.refs_9_), channel_id=1, source_target_pairs={{0,1},{1,0},{2,3},{3,2},{4,5},{5,4},{6,7},{7,6},{8,9},{9,8},{10,11... | collective-permute-start | bytes 1105928 | tf_op jit(solution)/shard_map/ppermute | solution.py:860
  196.9 106.8 %collective-permute-start.48 = (bf16[4,96,3072]{2,1,0:T(8,128)(2,1)}, bf16[4,96,3072]{2,1,0:T(8,128)(2,1)}, u32[]{:S(2)}, u32[]{:S(2)}) collective-permute-start(bf16[4,96,3072]{2,1,0:T(8,128)(2,1)} %get-tuple-element.96), channel_id=1, source_target_pairs={{0,1},{1,0},{2,3},{3,2},{4,5},{5,4},{6,7},{7,6},{8,9},{9,8},{10,11... | collective-permute-start | bytes 7077896 | tf_op jit(solution)/shard_map/ppermute | solution.py:860
  197.0 110.1 %collective-permute-start.49 = (bf16[4,96,3072]{2,1,0:T(8,128)(2,1)}, bf16[4,96,3072]{2,1,0:T(8,128)(2,1)}, u32[]{:S(2)}, u32[]{:S(2)}) collective-permute-start(bf16[4,96,3072]{2,1,0:T(8,128)(2,1)} %get-tuple-element.98), channel_id=1, source_target_pairs={{0,1},{1,0},{2,3},{3,2},{4,5},{5,4},{6,7},{7,6},{8,9},{9,8},{10,11... | collective-permute-start | bytes 7077896 | tf_op jit(solution)/shard_map/ppermute | solution.py:860
  263.4 21.0 %collective-permute-start.60 = (f32[16,768]{1,0:T(8,128)S(1)}, f32[16,768]{1,0:T(8,128)S(1)}, u32[]{:S(2)}, u32[]{:S(2)}) collective-permute-start(f32[16,768]{1,0:T(8,128)S(1)} %add.235), channel_id=1, source_target_pairs={{0,8},{8,0},{16,24},{24,16},{1,9},{9,1},{17,25},{25,17},{2,10},{10... | collective-permute-start | bytes 147464 | tf_op jit(solution)/shard_map/ppermute | solution.py:860
  296.8 20.4 %collective-permute-start.32 = (bf16[4,96,3072]{2,1,0:T(8,128)(2,1)}, bf16[4,96,3072]{2,1,0:T(8,128)(2,1)}, u32[]{:S(2)}, u32[]{:S(2)}) collective-permute-start(bf16[4,96,3072]{2,1,0:T(8,128)(2,1)} %get-tuple-element.90), channel_id=1, source_target_pairs={{0,1},{1,0},{2,3},{3,2},{4,5},{5,4},{6,7},{7,6},{8,9},{9,8},{10,11... | collective-permute-start | bytes 7077896 | tf_op jit(solution)/shard_map/ppermute | solution.py:860
  310.0 76.3 %collective-permute-start.52 = (bf16[4,48,3072]{2,1,0:T(8,128)(2,1)S(1)}, bf16[4,48,3072]{2,1,0:T(8,128)(2,1)S(1)}, u32[]{:S(2)}, u32[]{:S(2)}) collective-permute-start(bf16[4,48,3072]{2,1,0:T(8,128)(2,1)S(1)} %pad_maximum_fusion.3), channel_id=1, source_target_pairs={{0,2},{1,3},{2,0},{3,1},{4,6},{5,7},{6,4},{7,5},{8,10},{9,11},{10,... | collective-permute-start | bytes 3538952 | tf_op jit(solution)/shard_map/ppermute | solution.py:860
  311.5 75.1 %collective-permute-start.50 = (bf16[4,48,3072]{2,1,0:T(8,128)(2,1)S(1)}, bf16[4,48,3072]{2,1,0:T(8,128)(2,1)S(1)}, u32[]{:S(2)}, u32[]{:S(2)}) collective-permute-start(bf16[4,48,3072]{2,1,0:T(8,128)(2,1)S(1)} %pad_maximum_fusion.1), channel_id=1, source_target_pairs={{0,4},{1,5},{2,6},{3,7},{4,0},{5,1},{6,2},{7,3},{8,12},{9,13},{10,... | collective-permute-start | bytes 3538952 | tf_op jit(solution)/shard_map/ppermute | solution.py:860
  315.0 36.6 %collective-permute-start.43 = (bf16[2,48,3072]{2,1,0:T(8,128)(2,1)S(1)}, bf16[2,48,3072]{2,1,0:T(8,128)(2,1)S(1)}, u32[]{:S(2)}, u32[]{:S(2)}) collective-permute-start(bf16[2,48,3072]{2,1,0:T(8,128)(2,1)S(1)} %pad_maximum_fusion.8), channel_id=1, source_target_pairs={{0,2},{1,3},{2,0},{3,1},{4,6},{5,7},{6,4},{7,5},{8,10},{9,11},{10,... | collective-permute-start | bytes 1769480 | tf_op jit(solution)/shard_map/ppermute | solution.py:860
  315.9 36.3 %collective-permute-start.41 = (bf16[2,48,3072]{2,1,0:T(8,128)(2,1)S(1)}, bf16[2,48,3072]{2,1,0:T(8,128)(2,1)S(1)}, u32[]{:S(2)}, u32[]{:S(2)}) collective-permute-start(bf16[2,48,3072]{2,1,0:T(8,128)(2,1)S(1)} %stack.124), channel_id=1, source_target_pairs={{0,4},{1,5},{2,6},{3,7},{4,0},{5,1},{6,2},{7,3},{8,12},{9,13},{10,... | collective-permute-start | bytes 1769480 | tf_op jit(solution)/shard_map/ppermute | solution.py:860
  319.9 44.3 %collective-permute-start.35 = (bf16[2,48,3072]{2,1,0:T(8,128)(2,1)S(1)}, bf16[2,48,3072]{2,1,0:T(8,128)(2,1)S(1)}, u32[]{:S(2)}, u32[]{:S(2)}) collective-permute-start(bf16[2,48,3072]{2,1,0:T(8,128)(2,1)S(1)} %pad_maximum_fusion.7), channel_id=1, source_target_pairs={{0,2},{1,3},{2,0},{3,1},{4,6},{5,7},{6,4},{7,5},{8,10},{9,11},{10,... | collective-permute-start | bytes 1769480 | tf_op jit(solution)/shard_map/ppermute | solution.py:860
  379.1 24.9 %collective-permute-start.46 = (bf16[1,48,3072]{2,1,0:T(8,128)(2,1)S(1)}, bf16[1,48,3072]{2,1,0:T(8,128)(2,1)S(1)}, u32[]{:S(2)}, u32[]{:S(2)}) collective-permute-start(bf16[1,48,3072]{2,1,0:T(8,128)(2,1)S(1)} %add_convert_fusion.3), channel_id=1, source_target_pairs={{0,16},{8,24},{16,0},{24,8},{1,17},{9,25},{17,1},{25,9},{2,18},{10... | collective-permute-start | bytes 884744 | tf_op jit(solution)/shard_map/ppermute | solution.py:860
  388.8 21.8 %collective-permute-start.38 = (bf16[1,48,3072]{2,1,0:T(8,128)(2,1)S(1)}, bf16[1,48,3072]{2,1,0:T(8,128)(2,1)S(1)}, u32[]{:S(2)}, u32[]{:S(2)}) collective-permute-start(bf16[1,48,3072]{2,1,0:T(8,128)(2,1)S(1)} %add_convert_fusion.5), channel_id=1, source_target_pairs={{0,16},{8,24},{16,0},{24,8},{1,17},{9,25},{17,1},{25,9},{2,18},{10... | collective-permute-start | bytes 884744 | tf_op jit(solution)/shard_map/ppermute | solution.py:860
  404.0 25.6 %collective-permute-start.47 = (bf16[1,48,3072]{2,1,0:T(8,128)(2,1)S(1)}, bf16[1,48,3072]{2,1,0:T(8,128)(2,1)S(1)}, u32[]{:S(2)}, u32[]{:S(2)}) collective-permute-start(bf16[1,48,3072]{2,1,0:T(8,128)(2,1)S(1)} %add_convert_fusion.2), channel_id=1, source_target_pairs={{0,8},{8,0},{16,24},{24,16},{1,9},{9,1},{17,25},{25,17},{2,10},{10... | collective-permute-start | bytes 884744 | tf_op jit(solution)/shard_map/ppermute | solution.py:860
  408.0 21.2 %collective-permute-start.54 = (bf16[2,48,3072]{2,1,0:T(8,128)(2,1)S(1)}, bf16[2,48,3072]{2,1,0:T(8,128)(2,1)S(1)}, u32[]{:S(2)}, u32[]{:S(2)}) collective-permute-start(bf16[2,48,3072]{2,1,0:T(8,128)(2,1)S(1)} %select_convert_fusion), channel_id=1, source_target_pairs={{0,8},{8,0},{16,24},{24,16},{1,9},{9,1},{17,25},{25,17},{2,10},{10... | collective-permute-start | bytes 1769480 | tf_op jit(solution)/shard_map/ppermute | solution.py:860
  410.7 36.8 %collective-permute-start.39 = (bf16[1,48,3072]{2,1,0:T(8,128)(2,1)S(1)}, bf16[1,48,3072]{2,1,0:T(8,128)(2,1)S(1)}, u32[]{:S(2)}, u32[]{:S(2)}) collective-permute-start(bf16[1,48,3072]{2,1,0:T(8,128)(2,1)S(1)} %add_convert_fusion.4), channel_id=1, source_target_pairs={{0,8},{8,0},{16,24},{24,16},{1,9},{9,1},{17,25},{25,17},{2,10},{10... | collective-permute-start | bytes 884744 | tf_op jit(solution)/shard_map/ppermute | solution.py:860
  (101 other events, 968.2 us)
Sparse Core Ops, SparseCore 0:
  10.5 92.8 all-gather.1

commit v2 on v0

--- a/solution.py
+++ b/solution.py
@@ -1,6 +1,10 @@
+import functools
+
 import jax
 import jax.numpy as jnp
 from jax import lax
+from jax.experimental import pallas as pl
+from jax.experimental.pallas import tpu as pltpu
 from jax.sharding import PartitionSpec as P
 
 HEADS = 12
@@ -125,7 +129,7 @@
     return stacked.reshape(packed.shape).astype(jnp.bfloat16)
 
 
-def body(
+def general_body(
     video,
     temporal_entry,
     temporal_exit,
@@ -355,6 +359,1060 @@
     )
 
 
+BF = jnp.bfloat16
+F32 = jnp.float32
+D = 768
+FRAME_ROWS = 208
+PLACES = 196
+HERE = 49
+PIECE = 104
+ROWS = 416
+SPOTS = 400
+GROUP = 80
+SHARD = 96
+HALF = 48
+WIDE = 3072
+NEG = -1e30
+HBM = pl.BlockSpec(memory_space=pl.ANY)
+KEPT = pl.BlockSpec(memory_space=pltpu.HBM)
+VMEM = pl.BlockSpec(memory_space=pltpu.VMEM)
+
+
+def nn(a, b):
+    return jnp.dot(a, b, preferred_element_type=F32)
+
+
+def nt(a, b):
+    return lax.dot_general(a, b, (((1,), (1,)), ((), ())), preferred_element_type=F32)
+
+
+def tn(a, b):
+    return lax.dot_general(a, b, (((0,), (0,)), ((), ())), preferred_element_type=F32)
+
+
+def normalised(values):
+    average = jnp.mean(values, axis=-1, keepdims=True)
+    centred = values - average
+    variance = jnp.mean(centred * centred, axis=-1, keepdims=True)
+    scale = lax.rsqrt(variance + norm_eps)
+    return centred * scale, scale
+
+
+def norm_back(grad, unit, scale, gain):
+    moved = grad * gain
+    inner = scale * (
+        moved
+        - jnp.mean(moved, axis=-1, keepdims=True)
+        - unit * jnp.mean(moved * unit, axis=-1, keepdims=True)
+    )
+    return (
+        inner,
+        jnp.sum(grad * unit, axis=0, keepdims=True),
+        jnp.sum(grad, axis=0, keepdims=True),
+    )
+
+
+def picks(target, columns):
+    lanes = lax.broadcasted_iota(jnp.int32, (target.shape[0], columns), 1)
+    return jnp.where(lanes == target, 1.0, 0.0).astype(BF)
+
+
+def row_index(rows):
+    return lax.broadcasted_iota(jnp.int32, (rows, 1), 0)
+
+
+def at_least(value, limit):
+    return jnp.where(value >= limit, 1, 0)
+
+
+def place_from_piece():
+    r = row_index(SPOTS)
+    col = ((r >> 1) & 3) * PIECE + (r & 1) * HERE + (r >> 3)
+    return picks(jnp.where(r < 8 * HERE, col, -1), ROWS)
+
+
+def piece_parts():
+    c = row_index(ROWS)
+    k = at_least(c, PIECE) + at_least(c, 2 * PIECE) + at_least(c, 3 * PIECE)
+    rem = c - PIECE * k
+    f = at_least(rem, HERE)
+    return k, f, rem - HERE * f, rem < 2 * HERE
+
+
+def piece_from_place():
+    k, f, p, valid = piece_parts()
+    return picks(jnp.where(valid, p * 8 + k * 2 + f, -1), SPOTS)
+
+
+def frame_from_piece(me):
+    r = row_index(ROWS)
+    f = at_least(r, FRAME_ROWS)
+    spot = r - FRAME_ROWS * f
+    q = at_least(spot, HERE) + at_least(spot, 2 * HERE) + at_least(spot, 3 * HERE)
+    col = (q ^ me) * PIECE + f * HERE + spot - HERE * q
+    return picks(jnp.where(spot < PLACES, col, -1), ROWS)
+
+
+def piece_from_frame(me):
+    k, f, p, valid = piece_parts()
+    return picks(jnp.where(valid, f * FRAME_ROWS + HERE * (me ^ k) + p, -1), ROWS)
+
+
+def split_pieces(rows, refs):
+    for k, ref in enumerate(refs):
+        ref[...] = rows[k * PIECE : (k + 1) * PIECE]
+
+
+def stack_pieces(refs, stack):
+    for k, ref in enumerate(refs):
+        stack[k * PIECE : (k + 1) * PIECE, :] = ref[...]
+
+
+def small_row(params, index, width=D):
+    block = index // 8
+    return params[index % 8 : index % 8 + 1, block * D : block * D + width]
+
+
+def two_heads(value, factor=1.0):
+    lane = lax.broadcasted_iota(jnp.int32, (1, 128), 1)
+    low = jnp.where(lane < 64, factor, 0.0).astype(BF)
+    high = jnp.where(lane < 64, 0.0, factor).astype(BF)
+    return jnp.concatenate([value * low, value * high], axis=0)
+
+
+def joined(value):
+    rows = value.shape[0] // 2
+    lane = lax.broadcasted_iota(jnp.int32, (rows, 128), 1)
+    return jnp.where(lane < 64, value[:rows], value[rows:])
+
+
+def attend_block(q, k, v, keep):
+    scores = jnp.where(keep, nt(two_heads(q, 0.125), k), NEG)
+    raised = jnp.exp(scores - jnp.max(scores, axis=-1, keepdims=True))
+    weight = raised * (1.0 / jnp.sum(raised, axis=-1, keepdims=True))
+    return joined(nn(weight.astype(BF), v)).astype(BF)
+
+
+def attend_block_back(q, k, v, do, keep):
+    scores = jnp.where(keep, nt(k, two_heads(q, 0.125)), NEG)
+    raised = jnp.exp(scores - jnp.max(scores, axis=0, keepdims=True))
+    weight = raised * (1.0 / jnp.sum(raised, axis=0, keepdims=True))
+    both = two_heads(do)
+    dv = nn(weight.astype(BF), both)
+    dweight = nt(v, both)
+    delta = jnp.sum(dweight * weight, axis=0, keepdims=True)
+    dscore = (weight * (dweight - delta)).astype(BF)
+    dq = joined(tn(dscore, k)) * 0.125
+    dk = nn(dscore, two_heads(q, 0.125))
+    return dq.astype(BF), dk.astype(BF), dv.astype(BF)
+
+
+def spot_mask(rows, columns):
+    r = lax.broadcasted_iota(jnp.int32, (rows, columns), 0)
+    c = lax.broadcasted_iota(jnp.int32, (rows, columns), 1)
+    wrap = lambda i, n: i - jnp.where(i >= GROUP, GROUP, 0) if n > GROUP else i
+    return (wrap(r, rows) >> 3) == (wrap(c, columns) >> 3)
+
+
+def wide_product(a_ref, w_ref, out_ref, columns, step, w_offset=0):
+    def body(i, carry):
+        at = pl.multiple_of(i * step, 128)
+        out_ref[:, pl.ds(at, step)] = nn(
+            a_ref[...], w_ref[:, pl.ds(at + w_offset, step)]
+        ).astype(BF)
+        return carry
+
+    lax.fori_loop(0, columns // step, body, 0)
+
+
+ENTRY_PIECES = (
+    ((0, 0, 0, 0), (1, 0, 0, 1), (2, 0, 2, 0), (3, 0, 4, 1))
+    + ((4, 0, 4, 0), (4, 56, 6, 0), (5, 0, 2, 1), (5, 48, 6, 1))
+    + ((6, 0, 1, 0), (6, 56, 1, 1), (6, 104, 3, 0), (6, 160, 5, 1))
+    + ((6, 208, 5, 0), (6, 264, 7, 0), (6, 320, 3, 1), (6, 368, 7, 1))
+)
+PLANE_PIECES = (
+    ((0, 0, 0, 0), (0, 48, 0, 1), (2, 96, 2, 0), (1, 112, 4, 1))
+    + ((3, 0, 4, 0), (3, 48, 6, 0), (4, 0, 2, 1), (4, 48, 6, 1))
+    + ((5, 0, 1, 0), (5, 48, 1, 1), (5, 96, 3, 0), (5, 144, 5, 1))
+    + ((5, 192, 5, 0), (5, 240, 7, 0), (5, 288, 3, 1), (5, 336, 7, 1))
+)
+EXPAND_PIECES = ((0, 0), (6, 0), (2, 96), (6, 192), (4, 0), (7, 0), (4, 96), (7, 96))
+CONTRACT_PIECES = ((1, 0), (6, 96), (5, 0), (8, 0), (3, 96), (6, 288), (5, 96), (8, 96))
+
+
+def piece_copies(refs, table, own, weights, extra, sems):
+    copies = []
+    for array, at, relative, half in table:
+        rows = pl.ds(pl.multiple_of((own ^ relative) * SHARD + half * HALF, 16), HALF)
+        pairs = [(refs[array].at[pl.ds(at, HALF)], weights.at[rows])]
+        if half == 0 and extra is not None:
+            pairs.append((refs[array].at[pl.ds(at + HALF, 8)], extra.at[relative]))
+        for source, target in pairs:
+            copies.append(pltpu.make_async_copy(source, target, sems.at[len(copies)]))
+    return copies
+
+
+def arrange_parameters(where, bias, *refs):
+    sources, (first, second), held, sems = refs[:5], refs[5:7], refs[7:12], refs[12]
+    copies = [
+        pltpu.make_async_copy(source, target, sems.at[i])
+        for i, (source, target) in enumerate(zip(sources, held, strict=True))
+    ]
+    for c in copies:
+        c.start()
+    entry, leave, gains, shifts, biases = held
+    own = where[0]
+    lane = lax.broadcasted_iota(jnp.int32, (SHARD, D), 1)
+    spread = jnp.where(lane == own * SHARD + row_index(SHARD), 1.0, 0.0).astype(BF)
+    lane = lax.broadcasted_iota(jnp.int32, (384, D), 1)
+    wide = jnp.where(lane == (own & 1) * 384 + row_index(384), 1.0, 0.0).astype(BF)
+    four = lax.broadcasted_iota(jnp.int32, (4, D), 0)
+    bias_rows = jnp.where(four == own // 2, nn(bias[...], wide), 0.0)
+    for c in copies:
+        c.wait()
+    rows = jnp.concatenate(
+        [nn(gains[...], spread), nn(shifts[...], spread), nn(biases[...], spread), bias_rows], axis=0
+    )
+    rows = jnp.concatenate([rows, jnp.zeros((3, D), F32)], axis=0)
+    first[0:HALF, : 3 * D] = entry[0:HALF]
+    first[0:HALF, 3 * D :] = leave[0:HALF]
+    first[HALF:, :D] = rows[0:8].astype(BF)
+    first[HALF:, D : 2 * D] = rows[8:16].astype(BF)
+    first[HALF:, 2 * D :] = jnp.zeros((8, 2 * D), BF)
+    second[:, : 3 * D] = entry[HALF:]
+    second[:, 3 * D :] = leave[HALF:]
+
+
+def arrange_tokens(where, video, cotangent, tokens, cot, *pieces):
+    for source, target in ((video, tokens), (cotangent, cot)):
+        for f in range(2):
+            target[f * FRAME_ROWS : f * FRAME_ROWS + PLACES, :] = source[0, f]
+            target[f * FRAME_ROWS + PLACES : (f + 1) * FRAME_ROWS, :] = jnp.zeros(
+                (FRAME_ROWS - PLACES, D), BF
+            )
+    split_pieces(nn(piece_from_frame(where[1]), tokens[...]).astype(BF), pieces)
+
+
+def temporal_forward(*refs):
+    video, pieces, refs = refs[:4], refs[4:11], refs[11:]
+    out, refs = refs[:4], refs[4:]
+    (normed_out, packed_out, weight_out, leave_out, params_out, bias_out), refs = refs[:6], refs[6:]
+    weights, extra, stack, normed_ref, packed_ref, blended, sems, out_sems = refs
+    own = lax.axis_index("fsdp")
+    copies = piece_copies(pieces, ENTRY_PIECES, own, weights, extra, sems)
+    for c in copies:
+        c.start()
+    stack_pieces(video, stack)
+    unit, _ = normalised(stack[...].astype(F32))
+    for c in copies:
+        c.wait()
+    outs = [
+        pltpu.make_async_copy(weights.at[:, pl.ds(0, 3 * D)], weight_out, out_sems.at[0]),
+        pltpu.make_async_copy(normed_ref, normed_out, out_sems.at[1]),
+        pltpu.make_async_copy(packed_ref, packed_out, out_sems.at[2]),
+        pltpu.make_async_copy(weights.at[:, pl.ds(3 * D, D)], leave_out, out_sems.at[3]),
+    ]
+    outs[0].start()
+    outs[3].start()
+    params = extra[0].astype(F32)
+    for k in range(1, 8):
+        params = params + extra[k].astype(F32)
+    params_out[...] = params
+    for r in range(4):
+        bias_out[r : r + 1, :] = small_row(params, 9 + r)
+    normed = (unit * small_row(params, 0) + small_row(params, 3)).astype(BF)
+    normed_ref[...] = nn(place_from_piece(), normed).astype(BF)
+    outs[1].start()
+    wide_product(normed_ref, weights, packed_ref, 3 * D, D)
+    outs[2].start()
+    keep = spot_mask(2 * GROUP, GROUP)
+
+    def heads(i, carry):
+        at = pl.multiple_of(i * 128, 128)
+        for t in range(SPOTS // GROUP):
+            rows = pl.ds(t * GROUP, GROUP)
+            blended[rows, pl.ds(at, 128)] = attend_block(
+                packed_ref[rows, pl.ds(at, 128)],
+                packed_ref[rows, pl.ds(at + D, 128)],
+                packed_ref[rows, pl.ds(at + 2 * D, 128)],
+                keep,
+            )
+        return carry
+
+    lax.fori_loop(0, HEADS // 2, heads, 0)
+    split_pieces(nn(piece_from_place(), blended[...]).astype(BF), out)
+    for c in outs:
+        c.wait()
+
+
+def spatial_forward(*refs):
+    (tokens, params_ref, w_exit), places, pieces, refs = refs[:3], refs[3:7], refs[7:13], refs[13:]
+    after_two, normed_three = refs[:2]
+    held, refs = refs[2:9], refs[9:]
+    weights, stack, after_ref, normed_ref, packed_ref, blended, blended_time, sems, out_sems = refs
+    own = lax.axis_index("fsdp")
+    me = lax.axis_index("frame")
+    copies = piece_copies(pieces, PLANE_PIECES, own, weights, None, sems)
+    for c in copies:
+        c.start()
+    params = params_ref[...]
+    stack_pieces(places, stack)
+    blended_time[...] = nn(frame_from_piece(me), stack[...]).astype(BF)
+    for c in copies:
+        c.wait()
+    outs = [
+        pltpu.make_async_copy(src, dst, out_sems.at[i])
+        for i, (src, dst) in enumerate(
+            zip(
+                (
+                    weights.at[:, pl.ds(0, 3 * D)],
+                    weights.at[:, pl.ds(3 * D, D)],
+                    blended_time,
+                    after_ref,
+                    normed_ref,
+                    packed_ref,
+                    blended,
+                ),
+                held,
+                strict=True,
+            )
+        )
+    ]
+    for c in outs[:3]:
+        c.start()
+    after_time = (
+        tokens[...].astype(F32)
+        + nn(blended_time[...], w_exit[...])
+        + small_row(params, 6)
+    )
+    after_ref[...] = after_time
+    outs[3].start()
+    unit, _ = normalised(after_time)
+    normed_ref[...] = (unit * small_row(params, 1) + small_row(params, 4)).astype(BF)
+    outs[4].start()
+    wide_product(normed_ref, weights, packed_ref, 3 * D, D)
+    outs[5].start()
+    keep = lax.broadcasted_iota(jnp.int32, (2 * FRAME_ROWS, FRAME_ROWS), 1) < PLACES
+
+    def heads(i, carry):
+        at = pl.multiple_of(i * 128, 128)
+        for f in range(2):
+            rows = pl.ds(f * FRAME_ROWS, FRAME_ROWS)
+            blended[rows, pl.ds(at, 128)] = attend_block(
+                packed_ref[rows, pl.ds(at, 128)],
+                packed_ref[rows, pl.ds(at + D, 128)],
+                packed_ref[rows, pl.ds(at + 2 * D, 128)],
+                keep,
+            )
+        return carry
+
+    lax.fori_loop(0, HEADS // 2, heads, 0)
+    outs[6].start()
+    last = after_ref[...] + nn(blended[...], weights[:, 3 * D :]) + small_row(params, 7)
+    after_two[...] = last
+    unit, _ = normalised(last)
+    normed_three[...] = (unit * small_row(params, 2) + small_row(params, 5)).astype(BF)
+    for c in outs:
+        c.wait()
+
+
+def feed_forward(where, normed, after_ref, cot, params_ref, bias, *refs):
+    pieces, refs = refs[:9], refs[9:]
+    (output, grad_after, branch, keep_we, send_we, keep_wc, send_wc, small), refs = refs[:8], refs[8:]
+    w_in, w_out, normed_own, total, grad_normed, shuffle, sems = refs
+    own = where[0]
+    parity = own & 1
+    first_copies, later = [], []
+    for k, (array, at) in enumerate(EXPAND_PIECES):
+        source = pieces[array].at[pl.ds(at, SHARD)]
+        first_copies.append(
+            pltpu.make_async_copy(source, w_in.at[pl.ds(k * SHARD, SHARD)], sems.at[k])
+        )
+    for k, (array, at) in enumerate(CONTRACT_PIECES):
+        for c in range(4):
+            source = pieces[array].at[pl.ds(at, SHARD), pl.ds(c * D, D)]
+            spot = (k // 2) * D + (parity ^ (k & 1)) * 384 + c * SHARD
+            target = w_out.at[pl.ds(pl.multiple_of(spot, 32), SHARD)]
+            later.append(pltpu.make_async_copy(source, target, sems.at[8 + len(later)]))
+    for c in first_copies + later:
+        c.start()
+
+    column = lax.broadcasted_iota(jnp.int32, (1, D), 1)
+    block = (column * 683) >> 16
+    order = (own ^ block) * SHARD + column - block * SHARD
+    chosen = jnp.where(
+        lax.broadcasted_iota(jnp.int32, (D, D), 0) == order, jnp.ones((), F32), jnp.zeros((), F32)
+    ).astype(BF)
+    normed_own[...] = nn(normed[...], chosen).astype(BF)
+    total[...] = jnp.zeros_like(total)
+    grad_normed[...] = jnp.zeros_like(grad_normed)
+    small[...] = jnp.zeros_like(small)
+    for c in first_copies + later:
+        c.wait()
+
+    def step(p, carry):
+        chip = (own >> 1) ^ p
+        at = pl.ds(pl.multiple_of(chip * D, D), D)
+        rows = pl.ds(pl.multiple_of(p * D, D), D)
+        hidden = nn(normed_own[...], w_in[:, at]) + bias[pl.ds(chip, 1), :]
+        area = 0.5 + 0.5 * lax.erf(hidden * 0.7071067811865476)
+        slope = area + hidden * (0.3989422804014327 * jnp.exp(-0.5 * hidden * hidden))
+        active = (hidden * area).astype(BF)
+        total[...] += nn(active, w_out[rows, :])
+        grad_hidden = (nt(cot[...], w_out[rows, :]) * slope).astype(BF)
+        grad_normed[...] += nt(grad_hidden, w_in[:, at])
+        small[pl.ds(9 + chip, 1), :] = jnp.sum(grad_hidden.astype(F32), axis=0, keepdims=True)
+        shuffle[...] = tn(active, cot[...])
+        for kind, ref in ((parity, keep_wc), (1 - parity, send_wc)):
+            for c in range(4):
+                part = shuffle[pl.ds(pl.multiple_of(kind * 384 + c * SHARD, 32), SHARD), :]
+                ref[p, :, c * D : (c + 1) * D] = part.astype(BF)
+        moved = tn(normed_own[...], grad_hidden).astype(BF)
+        for j in range(4):
+            keep_we[j, :, at] = moved[2 * j * SHARD : (2 * j + 1) * SHARD]
+            send_we[j, :, at] = moved[(2 * j + 1) * SHARD : (2 * j + 2) * SHARD]
+        return carry
+
+    lax.fori_loop(0, 4, step, 0)
+    params = params_ref[...]
+    values = after_ref[...]
+    result = (values + (total[...] + small_row(params, 8))).astype(BF)
+    for f in range(2):
+        output[0, f] = result[f * FRAME_ROWS : f * FRAME_ROWS + PLACES]
+    unit, scale = normalised(values)
+    dn = nt(grad_normed[...].astype(BF), chosen)
+    inner, dgain, dshift = norm_back(dn, unit, scale, small_row(params, 2))
+    top = cot[...].astype(F32)
+    dafter = top + inner
+    grad_after[...] = dafter
+    branch[...] = dafter.astype(BF)
+    small[2:3, :] = dgain
+    small[5:6, :] = dshift
+    small[8:9, :] = jnp.sum(top, axis=0, keepdims=True)
+
+
+def spatial_back(branch, packed, w_last, grad_packed, grad_blended):
+    grad_blended[...] = nt(branch[...], w_last[...]).astype(BF)
+    keep = lax.broadcasted_iota(jnp.int32, (FRAME_ROWS, 2 * FRAME_ROWS), 0) < PLACES
+
+    def heads(i, carry):
+        at = pl.multiple_of(i * 128, 128)
+        for f in range(2):
+            rows = pl.ds(f * FRAME_ROWS, FRAME_ROWS)
+            dq, dk, dv = attend_block_back(
+                packed[rows, pl.ds(at, 128)],
+                packed[rows, pl.ds(at + D, 128)],
+                packed[rows, pl.ds(at + 2 * D, 128)],
+                grad_blended[rows, pl.ds(at, 128)],
+                keep,
+            )
+            grad_packed[rows, pl.ds(at, 128)] = dq
+            grad_packed[rows, pl.ds(at + D, 128)] = dk
+            grad_packed[rows, pl.ds(at + 2 * D, 128)] = dv
+        return carry
+
+    lax.fori_loop(0, HEADS // 2, heads, 0)
+
+
+def spatial_back_norm(where, *refs):
+    grad_packed, branch, grad_after, after_ref, params_ref, small_in, w_entry, w_exit = refs[:8]
+    grad_first, branch_first, small, *pieces = refs[8:]
+    params = params_ref[...]
+    dn = nt(grad_packed[...], w_entry[...]).astype(BF).astype(F32)
+    unit, scale = normalised(after_ref[...])
+    inner, dgain, dshift = norm_back(dn, unit, scale, small_row(params, 1))
+    first = grad_after[...] + inner
+    grad_first[...] = first
+    low = first.astype(BF)
+    branch_first[...] = low
+    back = nt(low, w_exit[...]).astype(BF)
+    split_pieces(nn(piece_from_frame(where[1]), back).astype(BF), pieces)
+    small[...] = small_in[...]
+    small[1:2, :] = dgain
+    small[4:5, :] = dshift
+    small[6:7, :] = jnp.sum(low.astype(F32), axis=0, keepdims=True)
+    small[7:8, :] = jnp.sum(branch[...].astype(F32), axis=0, keepdims=True)
+
+
+def temporal_back(*refs):
+    video, pieces, (packed, small_in, weights), refs = refs[:4], refs[4:8], refs[8:11], refs[11:]
+    (grad_packed, small), out, (stack, grads) = refs[:2], refs[2:6], refs[6:]
+    stack_pieces(pieces, stack)
+    grads[...] = nn(place_from_piece(), stack[...]).astype(BF)
+    keep = spot_mask(GROUP, 2 * GROUP)
+
+    def heads(i, carry):
+        at = pl.multiple_of(i * 128, 128)
+        for t in range(SPOTS // GROUP):
+            rows = pl.ds(t * GROUP, GROUP)
+            dq, dk, dv = attend_block_back(
+                packed[rows, pl.ds(at, 128)],
+                packed[rows, pl.ds(at + D, 128)],
+                packed[rows, pl.ds(at + 2 * D, 128)],
+                grads[rows, pl.ds(at, 128)],
+                keep,
+            )
+            grad_packed[rows, pl.ds(at, 128)] = dq
+            grad_packed[rows, pl.ds(at + D, 128)] = dk
+            grad_packed[rows, pl.ds(at + 2 * D, 128)] = dv
+        return carry
+
+    lax.fori_loop(0, HEADS // 2, heads, 0)
+    dn = nt(grad_packed[...], weights[...]).astype(BF)
+    moved = nn(piece_from_place(), dn)
+    split_pieces(moved.astype(BF), out)
+    stack_pieces(video, stack)
+    unit, _ = normalised(stack[...].astype(F32))
+    small[...] = small_in[...]
+    small[0:1, :] = jnp.sum(moved * unit, axis=0, keepdims=True)
+    small[3:4, :] = jnp.sum(moved, axis=0, keepdims=True)
+
+
+def input_back(where, tokens, grad_first, params_ref, *refs):
+    pieces, (out, stack) = refs[:4], refs[4:]
+    stack_pieces(pieces, stack)
+    dn = nn(frame_from_piece(where[1]), stack[...])
+    unit, scale = normalised(tokens[...].astype(F32))
+    moved = dn * small_row(params_ref[...], 0)
+    inner = scale * (
+        moved
+        - jnp.mean(moved, axis=-1, keepdims=True)
+        - unit * jnp.mean(moved * unit, axis=-1, keepdims=True)
+    )
+    total = grad_first[...] + inner
+    for f in range(2):
+        out[0, f] = total[f * FRAME_ROWS : f * FRAME_ROWS + PLACES]
+
+
+def weight_grads(where, *refs, tiles):
+    step = pl.program_id(0)
+    own = where[0]
+    pairs, (keep, send, shuffle) = refs[: 2 * len(tiles)], refs[2 * len(tiles) :]
+    first = 0
+    for i, count in enumerate(tiles):
+
+        @pl.when((step >= first) & (step < first + count))
+        def _(i=i):
+            shuffle[...] = tn(pairs[2 * i][...], pairs[2 * i + 1][...])
+
+        first += count
+    for j in range(4):
+        for parity, ref in ((0, keep), (1, send)):
+            rows = pl.ds(pl.multiple_of((own ^ (2 * j + parity)) * SHARD, 8), SHARD)
+            ref[j] = shuffle[rows, :].astype(BF)
+
+
+def by_columns(width, step):
+    def run(i, carry):
+        step(pl.ds(pl.multiple_of(i * 384, 128), 384))
+        return carry
+
+    lax.fori_loop(0, width // 384, run, 0)
+
+
+def plane_one_sums(*refs, count):
+    keeps, gots, (for_x, for_y, held) = refs[:count], refs[count : 2 * count], refs[2 * count :]
+
+    def step(at):
+        for i, (keep, got) in enumerate(zip(keeps, gots, strict=True)):
+            total = [keep[j, :, at].astype(F32) + got[j, :, at].astype(F32) for j in range(4)]
+            for_x[2 * i, :, at] = total[1][:HALF].astype(BF)
+            for_x[2 * i + 1, :, at] = total[3][:HALF].astype(BF)
+            for_y[2 * i, :, at] = total[2][HALF:].astype(BF)
+            for_y[2 * i + 1, :, at] = total[3][HALF:].astype(BF)
+            held[i, 0, :, at] = total[0][:HALF]
+            held[i, 1, :, at] = total[0][HALF:]
+            held[i, 2, :, at] = total[2][:HALF]
+            held[i, 3, :, at] = total[1][HALF:]
+
+    by_columns(keeps[0].shape[-1], step)
+
+
+def plane_two_sums(held, from_x, from_y, next_y, next_x, left):
+    def step(at):
+        for i in range(held.shape[0]):
+            next_y[i, :, at] = (held[i, 2, :, at] + from_x[2 * i + 1, :, at].astype(F32)).astype(BF)
+            next_x[i, :, at] = (held[i, 3, :, at] + from_y[2 * i + 1, :, at].astype(F32)).astype(BF)
+            left[i, 0, :, at] = held[i, 0, :, at] + from_x[2 * i, :, at].astype(F32)
+            left[i, 1, :, at] = held[i, 1, :, at] + from_y[2 * i, :, at].astype(F32)
+
+    by_columns(held.shape[-1], step)
+
+
+def line_one_sums(where, left, got_y, got_x, out, stays):
+    odd = where[1] & 1
+
+    def step(at):
+        for i in range(left.shape[0]):
+            first = left[i, 0, :, at] + got_y[i, :, at].astype(F32)
+            second = left[i, 1, :, at] + got_x[i, :, at].astype(F32)
+            out[i, :, at] = jnp.where(odd == 1, first, second).astype(BF)
+            stays[i, :, at] = jnp.where(odd == 1, second, first)
+
+    by_columns(left.shape[-1], step)
+
+
+def pair_sums(one, two, out):
+    def step(at):
+        for i in range(out.shape[0]):
+            out[i, :, at] = (one[i, :, at].astype(F32) + two[i, :, at].astype(F32)).astype(BF)
+
+    by_columns(out.shape[-1], step)
+
+
+def line_result(where, full, other, *outs, parts):
+    odd = where[1] & 1
+    for out, (i, first, columns) in zip(outs, parts, strict=True):
+        for block in range(columns // D):
+            at = slice(first + block * D, first + (block + 1) * D)
+            one, two = full[i, :, at].astype(F32), other[i, :, at].astype(F32)
+            low = jnp.where(odd == 1, two, one)
+            high = jnp.where(odd == 1, one, two)
+            if out.shape[1] == D:
+                out[block * SHARD : block * SHARD + HALF, :] = low
+                out[block * SHARD + HALF : (block + 1) * SHARD, :] = high
+            else:
+                out[:HALF, block * D : (block + 1) * D] = low
+                out[HALF:, block * D : (block + 1) * D] = high
+
+
+def shape(*dims, dtype=BF):
+    return jax.ShapeDtypeStruct(dims, dtype)
+
+
+def kept(*dims, dtype=BF):
+    return pltpu.HBM(dims, dtype)
+
+
+NO_COST = pl.CostEstimate(flops=1000, bytes_accessed=1000, transcendentals=0)
+
+
+def limit(mebibytes):
+    return pltpu.CompilerParams(vmem_limit_bytes=mebibytes << 20)
+
+
+def whole_call(kernel, name, outs, *ins, mebibytes=16, scalars=0, scratch=(), **options):
+    specs = [pl.BlockSpec(memory_space=pltpu.SMEM)] * scalars + [VMEM] * (len(ins) - scalars)
+    single = not isinstance(outs, (list, tuple))
+    return pl.pallas_call(
+        functools.partial(kernel, **options),
+        name=name,
+        out_shape=outs,
+        in_specs=specs,
+        out_specs=VMEM if single else [VMEM] * len(outs),
+        scratch_shapes=scratch,
+        compiler_params=limit(mebibytes),
+        cost_estimate=NO_COST,
+    )(*ins)
+
+
+CORE = [(i, i ^ 1) for i in range(8)]
+ACROSS = [(i, i ^ 2) for i in range(8)]
+UP = [(i, i ^ 4) for i in range(8)]
+NEAR = [(i, i ^ 1) for i in range(4)]
+FAR = [(i, i ^ 2) for i in range(4)]
+
+
+def swap(value, pairs, axis="fsdp"):
+    return lax.ppermute(value, axis, pairs)
+
+
+def shift(pieces):
+    moved = [lax.ppermute(pieces[k], "frame", [(i, i ^ k) for i in range(4)]) for k in (1, 2, 3)]
+    return [pieces[0], *moved]
+
+
+def after(value, *earlier):
+    return lax.optimization_barrier((value, *earlier))[0]
+
+
+class Reduction:
+    def __init__(self, where, keep, send):
+        self.where, self.keep, self.count, self.width = where, keep, len(keep), keep[0].shape[-1]
+        self.got = [swap(v, CORE) for v in send]
+
+    def shape(self, *dims, dtype=BF):
+        return shape(*dims, HALF, self.width, dtype=dtype)
+
+    def plane_one(self, *earlier):
+        got = [after(g, *earlier) for g in self.got] if earlier else self.got
+        n = self.count
+        for_x, for_y, self.held = whole_call(
+            plane_one_sums,
+            "plane_one",
+            [self.shape(2 * n), self.shape(2 * n), self.shape(n, 4, dtype=F32)],
+            *self.keep,
+            *got,
+            count=n,
+            mebibytes=24,
+        )
+        self.from_x = swap(for_x, ACROSS)
+        self.from_y = swap(for_y, UP)
+        return for_x, for_y
+
+    def plane_two(self, *earlier):
+        n = self.count
+        next_y, next_x, self.left = whole_call(
+            plane_two_sums,
+            "plane_two",
+            [self.shape(n), self.shape(n), self.shape(n, 2, dtype=F32)],
+            self.held,
+            after(self.from_x, *earlier),
+            after(self.from_y, *earlier),
+        )
+        self.got_y = swap(next_y, UP)
+        self.got_x = swap(next_x, ACROSS)
+        return next_y, next_x
+
+    def line_one(self, *earlier):
+        n = self.count
+        out, self.stays = whole_call(
+            line_one_sums,
+            "line_one",
+            [self.shape(n), self.shape(n, dtype=F32)],
+            self.where,
+            self.left,
+            after(self.got_y, *earlier),
+            after(self.got_x, *earlier),
+            scalars=1,
+        )
+        self.near = swap(out, NEAR, "frame")
+        return (out,)
+
+    def line_two(self, *earlier):
+        self.pair = whole_call(
+            pair_sums, "line_two", self.shape(self.count), self.stays, after(self.near, *earlier)
+        )
+        self.far = swap(self.pair, FAR, "frame")
+        return (self.pair,)
+
+    def line_three(self, *earlier):
+        self.full = whole_call(
+            pair_sums, "line_three", self.shape(self.count), self.pair, after(self.far, *earlier)
+        )
+        self.other = swap(self.full, NEAR, "frame")
+        return (self.full,)
+
+    def result(self, parts, outs):
+        return whole_call(
+            line_result, "line_result", outs, self.where, self.full, self.other, scalars=1, parts=parts
+        )
+
+
+def reduce_small(small):
+    for pairs in (CORE, ACROSS, UP):
+        small = small + swap(small, pairs)
+    for pairs in (NEAR, FAR):
+        small = small + swap(small, pairs, "frame")
+    return small
+
+
+def body(
+    video,
+    temporal_entry,
+    temporal_exit,
+    spatial_entry,
+    spatial_exit,
+    expand_weight,
+    contract_weight,
+    layer_gains,
+    layer_shifts,
+    branch_biases,
+    expand_bias,
+    cotangent,
+):
+    own = lax.axis_index("fsdp")
+    where = jnp.stack([own, lax.axis_index("frame")]).astype(jnp.int32)
+    rows = lambda *parts: jnp.concatenate(parts, axis=0)
+
+    sources = (temporal_entry, temporal_exit, layer_gains, layer_shifts, branch_biases)
+    g1a, g1b = pl.pallas_call(
+        arrange_parameters,
+        name="arrange_parameters",
+        out_shape=[shape(HALF + 8, WIDE), shape(HALF, WIDE)],
+        in_specs=[pl.BlockSpec(memory_space=pltpu.SMEM), VMEM] + [HBM] * 5,
+        out_specs=[VMEM] * 2,
+        scratch_shapes=[pltpu.VMEM(v.shape, BF) for v in sources] + [pltpu.SemaphoreType.DMA((5,))],
+        compiler_params=limit(8),
+        cost_estimate=NO_COST,
+    )(
+        where,
+        expand_bias.reshape(1, 384),
+        *(pltpu.with_memory_space_constraint(v, pltpu.HBM) for v in sources),
+    )
+    x1, y1 = swap(g1a, ACROSS), swap(g1b, UP)
+
+    tokens, cot, *video_pieces = whole_call(
+        arrange_tokens,
+        "arrange_tokens",
+        [shape(ROWS, D), shape(ROWS, D)] + [shape(PIECE, D)] * 4,
+        where,
+        after(video, g1a),
+        cotangent,
+        scalars=1,
+    )
+    video_pieces = shift(video_pieces)
+
+    plane = jnp.concatenate([spatial_entry, spatial_exit], axis=1)
+    contract = jnp.concatenate([contract_weight[c * SHARD : (c + 1) * SHARD] for c in range(4)], axis=1)
+    x1, y1, plane, contract, *_ = lax.optimization_barrier((x1, y1, plane, contract, tokens))
+    to_y = rows(g1a, x1, plane[HALF:])
+    to_x = rows(g1b, y1, plane[:HALF])
+    r2y, r2x = swap(to_y, UP), swap(to_x, ACROSS)
+    c1 = swap(rows(g1a, g1b, x1, y1, r2y[:112], r2x[:96]), CORE)
+    to_y = after(rows(plane[:HALF], r2x[96:], contract), *video_pieces[1:])
+    to_x = after(rows(plane[HALF:], r2y[112:], expand_weight), *video_pieces[1:])
+    r3y, r3x = swap(to_y, UP), swap(to_x, ACROSS)
+
+    *places, normed_place, packed_place, entry_full, exit_full, params, bias_full = pl.pallas_call(
+        temporal_forward,
+        name="temporal_forward",
+        out_shape=[shape(PIECE, D)] * 4
+        + [
+            kept(SPOTS, D),
+            kept(SPOTS, 3 * D),
+            kept(D, 3 * D),
+            kept(D, D),
+            shape(8, WIDE, dtype=F32),
+            shape(8, D, dtype=F32),
+        ],
+        in_specs=[VMEM] * 4 + [HBM] * 7,
+        out_specs=[VMEM] * 4 + [KEPT] * 4 + [VMEM] * 2,
+        scratch_shapes=[
+            pltpu.VMEM((D, WIDE), BF),
+            pltpu.VMEM((8, 8, WIDE), BF),
+            pltpu.VMEM((ROWS, D), BF),
+            pltpu.VMEM((SPOTS, D), BF),
+            pltpu.VMEM((SPOTS, 3 * D), BF),
+            pltpu.VMEM((SPOTS, D), BF),
+            pltpu.SemaphoreType.DMA((24,)),
+            pltpu.SemaphoreType.DMA((4,)),
+        ],
+        compiler_params=limit(24),
+        cost_estimate=NO_COST,
+    )(after(video_pieces[0], to_y, to_x), *video_pieces[1:], g1a, g1b, x1, y1, r2y, r2x, c1)
+    places = shift(places)
+
+    r3y, r3x = after(r3y, *places[1:]), after(r3x, *places[1:])
+    c2 = swap(rows(plane, r2x[96:], r2y[112:], r3y[:96], r3x[:96]), CORE)
+    to_y = rows(expand_weight, r3x[96:])
+    to_x = rows(contract, r3y[96:])
+    r4y, r4x = swap(to_y, UP), swap(to_x, ACROSS)
+    (
+        after_space,
+        normed_three,
+        space_full,
+        last_full,
+        blended_time,
+        after_time,
+        normed_two,
+        packed_space,
+        blended_space,
+    ) = pl.pallas_call(
+        spatial_forward,
+        name="spatial_forward",
+        out_shape=[
+            shape(ROWS, D, dtype=F32),
+            shape(ROWS, D),
+            kept(D, 3 * D),
+            kept(D, D),
+            kept(ROWS, D),
+            kept(ROWS, D, dtype=F32),
+            kept(ROWS, D),
+            kept(ROWS, 3 * D),
+            kept(ROWS, D),
+        ],
+        in_specs=[VMEM] * 7 + [HBM] * 6,
+        out_specs=[VMEM] * 2 + [KEPT] * 7,
+        scratch_shapes=[
+            pltpu.VMEM((D, WIDE), BF),
+            pltpu.VMEM((ROWS, D), BF),
+            pltpu.VMEM((ROWS, D), F32),
+            pltpu.VMEM((ROWS, D), BF),
+            pltpu.VMEM((ROWS, 3 * D), BF),
+            pltpu.VMEM((ROWS, D), BF),
+            pltpu.VMEM((ROWS, D), BF),
+            pltpu.SemaphoreType.DMA((16,)),
+            pltpu.SemaphoreType.DMA((7,)),
+        ],
+        compiler_params=limit(24),
+        cost_estimate=NO_COST,
+    )(after(tokens, to_y, to_x), params, exit_full, *places, plane, r2y, r2x, r3y, r3x, c2)
+
+    c3 = swap(after(rows(expand_weight, contract, r3x[96:], r3y[96:]), normed_three), CORE)
+    c4, c5 = swap(r4y, CORE), swap(r4x, CORE)
+    output, grad_after, branch_last, keep_we, send_we, keep_wc, send_wc, small = pl.pallas_call(
+        feed_forward,
+        name="feed_forward",
+        out_shape=[
+            shape(*video.shape),
+            shape(ROWS, D, dtype=F32),
+            shape(ROWS, D),
+            shape(4, SHARD, WIDE),
+            shape(4, SHARD, WIDE),
+            shape(4, SHARD, WIDE),
+            shape(4, SHARD, WIDE),
+            shape(16, D, dtype=F32),
+        ],
+        in_specs=[pl.BlockSpec(memory_space=pltpu.SMEM)] + [VMEM] * 5 + [HBM] * 9,
+        out_specs=[VMEM] * 8,
+        scratch_shapes=[
+            pltpu.VMEM((D, WIDE), BF),
+            pltpu.VMEM((WIDE, D), BF),
+            pltpu.VMEM((ROWS, D), BF),
+            pltpu.VMEM((ROWS, D), F32),
+            pltpu.VMEM((ROWS, D), F32),
+            pltpu.VMEM((D, D), F32),
+            pltpu.SemaphoreType.DMA((40,)),
+        ],
+        compiler_params=limit(28),
+        cost_estimate=NO_COST,
+    )(
+        *(where, normed_three, after_space, cot, params, bias_full),
+        *(expand_weight, contract, r3x, r3y, r4y, r4x, c3, c4, c5),
+    )
+    forward_sum = Reduction(where, [keep_we, keep_wc], [send_we, send_wc])
+
+    grad_packed = pl.pallas_call(
+        spatial_back,
+        name="spatial_back",
+        out_shape=shape(ROWS, 3 * D),
+        in_specs=[VMEM] * 3,
+        out_specs=VMEM,
+        scratch_shapes=[pltpu.VMEM((ROWS, D), BF)],
+        compiler_params=limit(16),
+        cost_estimate=NO_COST,
+    )(branch_last, packed_space, last_full)
+    placed = forward_sum.plane_one(grad_packed)
+    grad_first, branch_first, small, *grad_pieces = whole_call(
+        spatial_back_norm,
+        "spatial_back_norm",
+        [shape(ROWS, D, dtype=F32), shape(ROWS, D), shape(16, D, dtype=F32)] + [shape(PIECE, D)] * 4,
+        where,
+        grad_packed,
+        branch_last,
+        grad_after,
+        after_time,
+        params,
+        after(small, *placed),
+        space_full,
+        exit_full,
+        mebibytes=20,
+        scalars=1,
+    )
+    grad_pieces = shift(grad_pieces)
+
+    whole = lambda *dims: pl.BlockSpec(dims, lambda i, w: (0,) * len(dims))
+
+    def grads(*pairs):
+        tiles = tuple(b.shape[1] // D for _, b in pairs)
+        specs, first = [], 0
+        for (a, b), count in zip(pairs, tiles, strict=True):
+            at = lambda i, w, first=first, count=count: (0, jnp.clip(i - first, 0, count - 1))
+            specs += [whole(*a.shape), pl.BlockSpec((b.shape[0], D), at)]
+            first += count
+        return pl.pallas_call(
+            functools.partial(weight_grads, tiles=tiles),
+            name="weight_grads",
+            out_shape=[shape(4, SHARD, D * first)] * 2,
+            grid_spec=pltpu.PrefetchScalarGridSpec(
+                num_scalar_prefetch=1,
+                grid=(first,),
+                in_specs=specs,
+                out_specs=[pl.BlockSpec((4, SHARD, D), lambda i, w: (0, 0, i))] * 2,
+                scratch_shapes=[pltpu.VMEM((D, D), F32)],
+            ),
+            compiler_params=limit(16),
+            cost_estimate=NO_COST,
+        )(where, *(v for pair in pairs for v in pair))
+
+    keep_space, send_space = grads(
+        (blended_time, branch_first), (normed_two, grad_packed), (blended_space, branch_last)
+    )
+    output = after(jnp.swapaxes(output, 1, 2), send_space)
+
+    grad_place, small, *normed_back = pl.pallas_call(
+        temporal_back,
+        name="temporal_back",
+        out_shape=[shape(SPOTS, 3 * D), shape(16, D, dtype=F32)] + [shape(PIECE, D)] * 4,
+        in_specs=[VMEM] * 11,
+        out_specs=[VMEM] * 6,
+        scratch_shapes=[pltpu.VMEM((ROWS, D), BF), pltpu.VMEM((SPOTS, D), BF)],
+        compiler_params=limit(20),
+        cost_estimate=NO_COST,
+    )(*video_pieces, after(grad_pieces[0], output), *grad_pieces[1:], packed_place, small, entry_full)
+
+    step = lambda total, pairs, *axis: (total, swap(total, pairs, *axis))
+    join = lambda both, *earlier: both[0] + after(both[1], *earlier)
+    placed = forward_sum.plane_two(small)
+    space_sum = Reduction(where, [keep_space], [after(send_space, *placed)])
+    near = swap(after(jnp.stack([normed_back[1], normed_back[3]]), *placed), NEAR, "frame")
+    keep_time, send_time = grads((after(normed_place, *placed), grad_place))
+    placed = space_sum.plane_one(send_time)
+    time_sum = Reduction(where, [keep_time], [after(send_time, near, *placed)])
+    placed = forward_sum.line_one(*placed, near)
+    far = swap(after(jnp.stack([normed_back[2], near[1]]), *placed), FAR, "frame")
+    small = step(join(step(after(small, *placed), CORE)), ACROSS)
+    placed = forward_sum.line_two(*placed, far)
+    small = join(small, *placed)
+    placed = space_sum.plane_two(*placed, small)
+    placed = time_sum.plane_one(*placed)
+    input_grad = whole_call(
+        input_back,
+        "input_back",
+        shape(*video.shape, dtype=F32),
+        where,
+        after(tokens, *placed),
+        grad_first,
+        params,
+        *(normed_back[0], near[0], far[0], far[1]),
+        scalars=1,
+        scratch=[pltpu.VMEM((ROWS, D), BF)],
+    )
+    placed = space_sum.line_one(*placed, input_grad)
+    placed = time_sum.plane_two(*placed)
+    small = step(after(small, *placed), UP)
+    placed = forward_sum.line_three(*placed)
+    small = join(small, *placed)
+    placed = time_sum.line_one(*placed, small)
+    small = step(after(small, *placed), NEAR, "frame")
+    placed = space_sum.line_two(*placed)
+    small = join(small, *placed)
+    placed = time_sum.line_two(*placed, small)
+    small = step(after(small, *placed), FAR, "frame")
+    wide = lambda rows, columns: shape(rows, columns, dtype=F32)
+    grad_expand, grad_contract = forward_sum.result(
+        ((0, 0, WIDE), (1, 0, WIDE)), [wide(SHARD, WIDE), wide(4 * SHARD, D)]
+    )
+    placed = space_sum.line_three(*placed)
+    small = join(small, *placed)
+    placed = time_sum.line_three(*placed, grad_contract, small)
+    input_grad = jnp.swapaxes(input_grad, 1, 2)
+    grad_exit_time, grad_entry_space, grad_exit_space = space_sum.result(
+        ((0, 0, D), (0, D, 3 * D), (0, 4 * D, D)),
+        [wide(SHARD, D), wide(SHARD, 3 * D), wide(SHARD, D)],
+    )
+    time_sum.other = after(time_sum.other, grad_exit_space)
+    (grad_entry_time,) = time_sum.result(((0, 0, 3 * D),), [wide(SHARD, 3 * D)])
+
+    mine = lax.dynamic_slice_in_dim(small[:9], own * SHARD, SHARD, axis=1)
+    return (
+        jnp.swapaxes(output, 1, 2),
+        jnp.swapaxes(input_grad, 1, 2),
+        grad_entry_time,
+        grad_exit_time,
+        grad_entry_space,
+        grad_exit_space,
+        grad_expand,
+        grad_contract,
+        mine[0:3],
+        mine[3:6],
+        mine[6:9],
+        lax.dynamic_slice_in_dim(small[9:13].reshape(WIDE), own * 384, 384),
+    )
+
+
 def solution(mesh):
     placed = (
         P("fsdp", "frame", None, None),
@@ -370,8 +1428,9 @@
         P("fsdp"),
         P("fsdp", "frame", None, None),
     )
+    special = mesh.shape["fsdp"] == 8 and mesh.shape["frame"] == 4
     return jax.shard_map(
-        body,
+        body if special else general_body,
         mesh=mesh,
         in_specs=placed,
         out_specs=(

time: 905 us -> 313 us (0.35)
  blocking collectives: 259 us -> 0 us
  waiting for transfers between devices: 339 us -> 136 us
  matrix products: 114 us -> 0 us
  local copies, waits for them, and re-layouts: 116 us -> 7.91 us
  Pallas kernels: 0 us -> 98.6 us
  starting transfers between devices: 13.4 us -> 68.2 us
  other arithmetic: 37.4 us -> 0.86 us
  between operations: 18.5 us -> 1.28 us
    reduce_scatter x12 -> x0, waiting for transfers between devices: 199 us -> none  [the longest x1 74.1 us: body(): lax.psum_scatter(grad_expand, 'fsdp', scatter_dimension=0, tiled=True)]
    all_gather x13 -> x0, blocking collectives: 165 us -> none  [the longest x1 20.6 us: body(): lax.all_gather(shares[4].astype(jnp.bfloat16), 'frame', axis=0, tiled=True)]
    ppermute x0 -> x54, waiting for transfers between devices: none -> 136 us  [the longest x45 129 us: swap(): return lax.ppermute(value, axis, pairs)]
    dot_general x30 -> x0, matrix products: 114 us -> none  [the longest x6 37.5 us: dense(): return jnp.dot(first_op, second_op, preferred_element_type=jnp.float32)]
    pallas_call x0 -> x29, Pallas kernels: none -> 98.6 us  [the longest x1 21.2 us: body(): pl.pallas_call(feed_forward, name='feed_forward', out_shape=[shape(*video...]
    ppermute x0 -> x54, starting transfers between devices: none -> 68.2 us  [the longest x45 53.3 us: swap(): return lax.ppermute(value, axis, pairs)]
    all_to_all x3 -> x0, waiting for transfers between devices: 60.1 us -> none  [the longest x1 44.6 us: body(): lax.all_to_all(grad_packed_place, 'frame', split_axis=1, concat_axis=2, t...]
    unnamed x24 -> x0, waiting for transfers between devices: 60 us -> none
  transfers between devices with their start and end apart: 24 -> 54, of which waited for: 15 -> 27; matrix products, arithmetic and copies ran while one was open for 26% -> 2% of each run, Pallas kernels for 0% -> 23%
where the time goes in v2:
time: 313 us; the launch traced here: 312 us
  waiting for transfers between devices  136 us (43%)
  Pallas kernels  98.6 us (32%)
  starting transfers between devices  68.2 us (22%)
  local copies, waits for them, and re-layouts  7.91 us (3%)
    ppermute x45, waiting for transfers between devices, swap(): return lax.ppermute(value, axis, pairs)  129 us
    ppermute x45, starting transfers between devices, swap(): return lax.ppermute(value, axis, pairs)  53.3 us
    pallas_call x1, Pallas kernels, body(): pl.pallas_call(feed_forward, name='feed_forward', out_shape=[shape(*video...  21.2 us
    pallas_call x21, Pallas kernels, whole_call(): pl.pallas_call(functools.partial(kernel, **options), name=name, out_shape...  19.1 us
    ppermute x9, starting transfers between devices, shift(): lax.ppermute(pieces[k], 'frame', [(i, i ^ k) for i in range(4)])  14.9 us
    pallas_call x1, Pallas kernels, body(): pl.pallas_call(temporal_back, name='temporal_back', out_shape=[shape(SPOT...  13.6 us
    pallas_call x1, Pallas kernels, body(): pl.pallas_call(spatial_forward, name='spatial_forward', out_shape=[shape(...  12.5 us
    pallas_call x1, Pallas kernels, body(): pl.pallas_call(temporal_forward, name='temporal_forward', out_shape=[shap...  10.2 us
  transfers between devices with their start and end apart: 54, of which 27 were waited for; matrix products, arithmetic and copies ran while one was open for 2% of the time, Pallas kernels for 23%

profile of v2, /device:TPU:0, one launch (start us, length us, event | category | flops | bytes accessed | tf_op | source)
XLA Modules:
  0.0 312.4 jit_solution(5967374847931247411)
XLA Ops:
  3.4 3.0 collective-permute-start
  13.0 2.6 collective-permute-start.4
  19.7 20.0 %collective-permute-done.2.refs_8_ = bf16[160,3072]{1,0:T(8,128)(2,1)S(1)} collective-permute-done((bf16[160,3072]{1,0:T(8,128)(2,1)S(1)}, bf16[160,3072]{1,0:T(8,128)(2,1)S(1)}, u32[]{:S(2)}, u32[]{:S(2)}) %collective-permute-start.2) | collective-permute-done | bytes 983072 | tf_op jit(solution)/shard_map/ppermute | solution.py:1018
  42.4 2.3 collective-permute-done.8.refs_10_
  44.7 10.2 %temporal_forward.1 = (bf16[104,768]{1,0:T(8,128)(2,1)S(1)}, bf16[104,768]{1,0:T(8,128)(2,1)S(1)}, bf16[104,768]{1,0:T(8,128)(2,1)S(1)}, bf16[104,768]{1,0:T(8,1...) custom-call(bf16[104,768]{1,0:T(8,128)(2,1)S(1)} %get-tuple-element., ...), custom_call_target="tpu_custom_call" | custom-call | flops 1000 | bytes 1000 | tf_op jit(solution)/shard_map/temporal_forward/pallas_call | solution.py:1168
  54.9 2.7 collective-permute-start.10
  59.2 9.4 %collective-permute-done.6.refs_11_.refs_2_ = bf16[192,3072]{1,0:T(8,128)(2,1)S(1)} collective-permute-done((bf16[192,3072]{1,0:T(8,128)(2,1)S(1)}, bf16[192,3072]{1,0:T(8,128)(2,1)S(1)}, u32[]{:S(2)}, u32[]{:S(2)}) %collective-permute-start.6) | collective-permute-done | bytes 1179680 | tf_op jit(solution)/shard_map/ppermute | solution.py:1018
  75.1 12.5 %spatial_forward.1 = (f32[416,768]{1,0:T(8,128)S(1)}, bf16[416,768]{1,0:T(8,128)(2,1)S(1)}, bf16[768,2304]{1,0:T(8,128)(2,1)}, bf16[768,768]{1,0:T(8,128)(2,1)},...) custom-call(bf16[416,768]{1,0:T(8,128)(2,1)S(1)} %get-tuple-element., ...), custom_call_target="tpu_custom_call" | custom-call | flops 1000 | bytes 1000 | tf_op jit(solution)/shard_map/spatial_forward/pallas_call | solution.py:1212
  87.8 11.3 %collective-permute-done.15.refs_5_ = bf16[192,3072]{1,0:T(8,128)(2,1)S(1)} collective-permute-done((bf16[192,3072]{1,0:T(8,128)(2,1)S(1)}, bf16[192,3072]{1,0:T(8,128)(2,1)S(1)}, u32[]{:S(2)}, u32[]{:S(2)}) %collective-permute-start.15) | collective-permute-done | bytes 1179680 | tf_op jit(solution)/shard_map/ppermute | solution.py:1018
  99.6 2.3 collective-permute-done.18.refs_8_
  103.6 21.2 %feed_forward.1 = (bf16[1,2,196,768]{3,2,1,0:T(8,128)(2,1)S(1)}, f32[416,768]{1,0:T(8,128)S(1)}, bf16[416,768]{1,0:T(8,128)(2,1)S(1)}, bf16[4,96,3072]{2,1,0:T(8...) custom-call(s32[2]{0:T(128)S(1)} %pad_add_fusion.where, ...), custom_call_target="tpu_custom_call" | custom-call | flops 1000 | bytes 1000 | tf_op jit(solution)/shard_map/feed_forward/pallas_call | solution.py:1245
  125.4 9.9 %spatial_back.1.refs_0_.refs_3_ = bf16[416,2304]{1,0:T(8,128)(2,1)S(1)} custom-call(bf16[416,768]{1,0:T(8,128)(2,1)S(1)} %get-tuple-element.176.branch.refs_1_.refs_5_, bf16[416,2304]{1,0:T(8,128)(2,1)S(1)} %copy-done.4, bf16[768,768]{1,0:T(8,128)(2,1)S(1)} %copy-done.7), custom_call_target="tpu_custom_call" | custom-call | flops 1000 | bytes 1000 | tf_op jit(solution)/shard_map/spatial_back/pallas_call | solution.py:1277
  138.8 4.5 %spatial_back_norm.1 = (f32[416,768]{1,0:T(8,128)S(1)}, bf16[416,768]{1,0:T(8,128)(2,1)S(1)}, f32[16,768]{1,0:T(8,128)S(1)}, bf16[104,768]{1,0:T(8,128)(2,1)S(1)...) custom-call(s32[2]{0:T(128)S(1)} %pad_add_fusion.where, ...), custom_call_target="tpu_custom_call" | custom-call | flops 1000 | bytes 1000 | tf_op jit(solution)/shard_map/spatial_back_norm/pallas_call | solution.py:998
  143.3 2.8 collective-permute-start.22
  149.5 6.3 %weight_grads.2 = (bf16[4,96,3840]{2,1,0:T(8,128)(2,1)S(1)}, bf16[4,96,3840]{2,1,0:T(8,128)(2,1)S(1)}) custom-call(s32[2]{0:T(128)S(1)} %pad_add_fusion.where, bf16[416,768]{1,0:T(8,128)(2,1)S(1)} %copy-done.8, bf16[416,768]{1,0:T(8,128)(2,1)S(1)} %get-tuple-element.192.refs_1_, bf16[416,768]{1,0:T(8,128)(2,1)S(1)} %copy-done.9, ...), custom_call_target="tpu_custom_call" | custom-call | flops 1000 | bytes 1000 | tf_op jit(solution)/shard_map/weight_grads/pallas_call | solution.py:1315
  155.8 4.8 %collective-permute-done.23.refs_6_ = bf16[104,768]{1,0:T(8,128)(2,1)S(1)} collective-permute-done((bf16[104,768]{1,0:T(8,128)(2,1)S(1)}, bf16[104,768]{1,0:T(8,128)(2,1)S(1)}, u32[]{:S(2)}, u32[]{:S(2)}) %collective-permute-start.23) | collective-permute-done | bytes 159776 | tf_op jit(solution)/shard_map/ppermute | solution.py:1022
  160.6 13.6 %temporal_back.1 = (bf16[400,2304]{1,0:T(8,128)(2,1)S(1)}, f32[16,768]{1,0:T(8,128)S(1)}, bf16[104,768]{1,0:T(8,128)(2,1)S(1)}, bf16[104,768]{1,0:T(8,128)(2,1)S...) custom-call(bf16[104,768]{1,0:T(8,128)(2,1)S(1)} %get-tuple-element.159.refs_0_, ...), custom_call_target="tpu_custom_call" | custom-call | flops 1000 | bytes 1000 | tf_op jit(solution)/shard_map/temporal_back/pallas_call | solution.py:1335
  174.9 2.7 collective-permute-start.26
  177.6 3.9 %weight_grads.3 = (bf16[4,96,2304]{2,1,0:T(8,128)(2,1)S(1)}, bf16[4,96,2304]{2,1,0:T(8,128)(2,1)S(1)}) custom-call(s32[2]{0:T(128)S(1)} %pad_add_fusion.where, bf16[400,768]{1,0:T(8,128)(2,1)S(1)} %copy-done.11, bf16[400,2304]{1,0:T(8,128)(2,1)S(1)} %get-tuple-element.213.refs_1_), custom_call_target="tpu_custom_call" | custom-call | flops 1000 | bytes 1000 | tf_op jit(solution)/shard_map/weight_grads/pallas_call | solution.py:1315
  182.2 3.6 %collective-permute-done.26 = bf16[2,104,768]{2,1,0:T(8,128)(2,1)S(1)} collective-permute-done((bf16[2,104,768]{2,1,0:T(8,128)(2,1)S(1)}, bf16[2,104,768]{2,1,0:T(8,128)(2,1)S(1)}, u32[]{:S(2)}, u32[]{:S(2)}) %collective-permute-start.26) | collective-permute-done | bytes 319520 | tf_op jit(solution)/shard_map/ppermute | solution.py:1018
  189.9 12.1 %collective-permute-done.31.got_x = bf16[2,48,3072]{2,1,0:T(8,128)(2,1)S(1)} collective-permute-done((bf16[2,48,3072]{2,1,0:T(8,128)(2,1)S(1)}, bf16[2,48,3072]{2,1,0:T(8,128)(2,1)S(1)}, u32[]{:S(2)}, u32[]{:S(2)}) %collective-permute-start.31) | collective-permute-done | bytes 589856 | tf_op jit(solution)/shard_map/ppermute | solution.py:1018
  209.6 14.9 %collective-permute-done.33 = bf16[2,104,768]{2,1,0:T(8,128)(2,1)S(1)} collective-permute-done((bf16[2,104,768]{2,1,0:T(8,128)(2,1)S(1)}, bf16[2,104,768]{2,1,0:T(8,128)(2,1)S(1)}, u32[]{:S(2)}, u32[]{:S(2)}) %collective-permute-start.33) | collective-permute-done | bytes 319520 | tf_op jit(solution)/shard_map/ppermute | solution.py:1018
  225.4 3.4 %collective-permute-done.35 = f32[16,768]{1,0:T(8,128)S(1)} collective-permute-done((f32[16,768]{1,0:T(8,128)S(1)}, f32[16,768]{1,0:T(8,128)S(1)}, u32[]{:S(2)}, u32[]{:S(2)}) %collective-permute-start.35) | collective-permute-done | bytes 49184 | tf_op jit(solution)/shard_map/ppermute | solution.py:1018
  233.7 3.5 %collective-permute-start.42 = (bf16[2,48,3072]{2,1,0:T(8,128)(2,1)S(1)}, bf16[2,48,3072]{2,1,0:T(8,128)(2,1)S(1)}, u32[]{:S(2)}, u32[]{:S(2)}) collective-permute-start(bf16[2,48,3072]{2,1,0:T(8,128)(2,1)S(1)} %line_two.3.one), channel_id=1, source_target_pairs={{0,16},{8,24},{16,0},{24,8},{1,17},{9,25},{17,1},{25,9},{2,18},{10... | collective-permute-start | bytes 1769480 | tf_op jit(solution)/shard_map/ppermute | solution.py:1018
  242.1 4.3 %collective-permute-start.46 = (bf16[1,48,3840]{2,1,0:T(8,128)(2,1)S(1)}, bf16[1,48,3840]{2,1,0:T(8,128)(2,1)S(1)}, u32[]{:S(2)}, u32[]{:S(2)}) collective-permute-start(bf16[1,48,3840]{2,1,0:T(8,128)(2,1)S(1)} %get-tuple-element.250), channel_id=1, source_target_pairs={{0,8},{8,0},{16,24},{24,16},{1,9},{9,1},{17,25},{25,17},{2,10},{10... | collective-permute-start | bytes 1105928 | tf_op jit(solution)/shard_map/ppermute | solution.py:1018
  249.2 9.5 %collective-permute-done.42.two = bf16[2,48,3072]{2,1,0:T(8,128)(2,1)S(1)} collective-permute-done((bf16[2,48,3072]{2,1,0:T(8,128)(2,1)S(1)}, bf16[2,48,3072]{2,1,0:T(8,128)(2,1)S(1)}, u32[]{:S(2)}, u32[]{:S(2)}) %collective-permute-start.42) | collective-permute-done | bytes 589856 | tf_op jit(solution)/shard_map/ppermute | solution.py:1018
  259.8 3.6 %collective-permute-done.43 = f32[16,768]{1,0:T(8,128)S(1)} collective-permute-done((f32[16,768]{1,0:T(8,128)S(1)}, f32[16,768]{1,0:T(8,128)S(1)}, u32[]{:S(2)}, u32[]{:S(2)}) %collective-permute-start.43) | collective-permute-done | bytes 49184 | tf_op jit(solution)/shard_map/ppermute | solution.py:1018
  264.3 3.5 %collective-permute-start.49 = (bf16[1,48,3840]{2,1,0:T(8,128)(2,1)S(1)}, bf16[1,48,3840]{2,1,0:T(8,128)(2,1)S(1)}, u32[]{:S(2)}, u32[]{:S(2)}) collective-permute-start(bf16[1,48,3840]{2,1,0:T(8,128)(2,1)S(1)} %line_two.4.one), channel_id=1, source_target_pairs={{0,16},{8,24},{16,0},{24,8},{1,17},{9,25},{17,1},{25,9},{2,18},{10... | collective-permute-start | bytes 1105928 | tf_op jit(solution)/shard_map/ppermute | solution.py:1018
  269.8 16.3 %collective-permute-done.47 = f32[16,768]{1,0:T(8,128)S(1)} collective-permute-done((f32[16,768]{1,0:T(8,128)S(1)}, f32[16,768]{1,0:T(8,128)S(1)}, u32[]{:S(2)}, u32[]{:S(2)}) %collective-permute-start.47) | collective-permute-done | bytes 49184 | tf_op jit(solution)/shard_map/ppermute | solution.py:1018
  286.2 3.4 %collective-permute-start.48 = (bf16[1,48,2304]{2,1,0:T(8,128)(2,1)S(1)}, bf16[1,48,2304]{2,1,0:T(8,128)(2,1)S(1)}, u32[]{:S(2)}, u32[]{:S(2)}) collective-permute-start(bf16[1,48,2304]{2,1,0:T(8,128)(2,1)S(1)} %line_two.5.one), channel_id=1, source_target_pairs={{0,16},{8,24},{16,0},{24,8},{1,17},{9,25},{17,1},{25,9},{2,18},{10... | collective-permute-start | bytes 663560 | tf_op jit(solution)/shard_map/ppermute | solution.py:1018
  293.7 8.8 %collective-permute-done.51 = f32[16,768]{1,0:T(8,128)S(1)} collective-permute-done((f32[16,768]{1,0:T(8,128)S(1)}, f32[16,768]{1,0:T(8,128)S(1)}, u32[]{:S(2)}, u32[]{:S(2)}) %collective-permute-start.51) | collective-permute-done | bytes 49184 | tf_op jit(solution)/shard_map/ppermute | solution.py:1018
  302.7 2.2 collective-permute-start.52
  (175 shorter events, 76.0 us)
Async XLA Ops:
  11.4 28.7 %collective-permute-start.3 = (bf16[104,768]{1,0:T(8,128)(2,1)S(1)}, bf16[104,768]{1,0:T(8,128)(2,1)S(1)}, u32[]{:S(2)}, u32[]{:S(2)}) collective-permute-start(bf16[104,768]{1,0:T(8,128)(2,1)S(1)} %get-tuple-element.151), channel_id=1, source_target_pairs={{0,8},{8,0},{16,24},{24,16},{1,9},{9,1},{17,25},{25,17},{2,10},{10... | collective-permute-start | bytes 479240 | tf_op jit(solution)/shard_map/ppermute | solution.py:1022
  13.0 27.1 %collective-permute-start.4 = (bf16[104,768]{1,0:T(8,128)(2,1)S(1)}, bf16[104,768]{1,0:T(8,128)(2,1)S(1)}, u32[]{:S(2)}, u32[]{:S(2)}) collective-permute-start(bf16[104,768]{1,0:T(8,128)(2,1)S(1)} %get-tuple-element.152), channel_id=1, source_target_pairs={{0,16},{8,24},{16,0},{24,8},{1,17},{9,25},{17,1},{25,9},{2,18},{10... | collective-permute-start | bytes 479240 | tf_op jit(solution)/shard_map/ppermute | solution.py:1022
  15.6 24.5 %collective-permute-start.5 = (bf16[104,768]{1,0:T(8,128)(2,1)S(1)}, bf16[104,768]{1,0:T(8,128)(2,1)S(1)}, u32[]{:S(2)}, u32[]{:S(2)}) collective-permute-start(bf16[104,768]{1,0:T(8,128)(2,1)S(1)} %get-tuple-element.153), channel_id=1, source_target_pairs={{0,24},{8,16},{16,8},{24,0},{1,25},{9,17},{17,9},{25,1},{2,26},{10... | collective-permute-start | bytes 479240 | tf_op jit(solution)/shard_map/ppermute | solution.py:1022
  17.3 22.4 %collective-permute-start.2 = (bf16[160,3072]{1,0:T(8,128)(2,1)S(1)}, bf16[160,3072]{1,0:T(8,128)(2,1)S(1)}, u32[]{:S(2)}, u32[]{:S(2)}) collective-permute-start(bf16[160,3072]{1,0:T(8,128)(2,1)S(1)} %pad_maximum_fusion.5), channel_id=1, source_target_pairs={{0,4},{1,5},{2,6},{3,7},{4,0},{5,1},{6,2},{7,3},{8,12},{9,13},{10,... | collective-permute-start | bytes 2949128 | tf_op jit(solution)/shard_map/ppermute | solution.py:1018
  19.0 20.8 %collective-permute-start.7 = (bf16[144,3072]{1,0:T(8,128)(2,1)S(1)}, bf16[144,3072]{1,0:T(8,128)(2,1)S(1)}, u32[]{:S(2)}, u32[]{:S(2)}) collective-permute-start(bf16[144,3072]{1,0:T(8,128)(2,1)S(1)} %pad_maximum_fusion.6), channel_id=1, source_target_pairs={{0,2},{1,3},{2,0},{3,1},{4,6},{5,7},{6,4},{7,5},{8,10},{9,11},{10,... | collective-permute-start | bytes 2654216 | tf_op jit(solution)/shard_map/ppermute | solution.py:1018
  40.1 28.4 %collective-permute-start.6 = (bf16[192,3072]{1,0:T(8,128)(2,1)S(1)}, bf16[192,3072]{1,0:T(8,128)(2,1)S(1)}, u32[]{:S(2)}, u32[]{:S(2)}) collective-permute-start(bf16[192,3072]{1,0:T(8,128)(2,1)S(1)} %pad_maximum_fusion.1), channel_id=1, source_target_pairs={{0,2},{1,3},{2,0},{3,1},{4,6},{5,7},{6,4},{7,5},{8,10},{9,11},{10,... | collective-permute-start | bytes 3538952 | tf_op jit(solution)/shard_map/ppermute | solution.py:1018
  40.9 29.3 %collective-permute-start.12 = (bf16[192,3072]{1,0:T(8,128)(2,1)S(1)}, bf16[192,3072]{1,0:T(8,128)(2,1)S(1)}, u32[]{:S(2)}, u32[]{:S(2)}) collective-permute-start(bf16[192,3072]{1,0:T(8,128)(2,1)S(1)} %pad_maximum_fusion.2), channel_id=1, source_target_pairs={{0,4},{1,5},{2,6},{3,7},{4,0},{5,1},{6,2},{7,3},{8,12},{9,13},{10,... | collective-permute-start | bytes 3538952 | tf_op jit(solution)/shard_map/ppermute | solution.py:1018
  54.9 14.8 %collective-permute-start.10 = (bf16[104,768]{1,0:T(8,128)(2,1)S(1)}, bf16[104,768]{1,0:T(8,128)(2,1)S(1)}, u32[]{:S(2)}, u32[]{:S(2)}) collective-permute-start(bf16[104,768]{1,0:T(8,128)(2,1)S(1)} %get-tuple-element.161), channel_id=1, source_target_pairs={{0,16},{8,24},{16,0},{24,8},{1,17},{9,25},{17,1},{25,9},{2,18},{10... | collective-permute-start | bytes 479240 | tf_op jit(solution)/shard_map/ppermute | solution.py:1022
  70.6 28.4 %collective-permute-start.15 = (bf16[192,3072]{1,0:T(8,128)(2,1)S(1)}, bf16[192,3072]{1,0:T(8,128)(2,1)S(1)}, u32[]{:S(2)}, u32[]{:S(2)}) collective-permute-start(bf16[192,3072]{1,0:T(8,128)(2,1)S(1)} %pad_maximum_fusion.4), channel_id=1, source_target_pairs={{0,2},{1,3},{2,0},{3,1},{4,6},{5,7},{6,4},{7,5},{8,10},{9,11},{10,... | collective-permute-start | bytes 3538952 | tf_op jit(solution)/shard_map/ppermute | solution.py:1018
  71.5 28.2 %collective-permute-start.14 = (bf16[192,3072]{1,0:T(8,128)(2,1)S(1)}, bf16[192,3072]{1,0:T(8,128)(2,1)S(1)}, u32[]{:S(2)}, u32[]{:S(2)}) collective-permute-start(bf16[192,3072]{1,0:T(8,128)(2,1)S(1)} %pad_maximum_fusion.3), channel_id=1, source_target_pairs={{0,4},{1,5},{2,6},{3,7},{4,0},{5,1},{6,2},{7,3},{8,12},{9,13},{10,... | collective-permute-start | bytes 3538952 | tf_op jit(solution)/shard_map/ppermute | solution.py:1018
  87.6 16.0 %collective-permute-start.16 = (bf16[384,3072]{1,0:T(8,128)(2,1)S(1)}, bf16[384,3072]{1,0:T(8,128)(2,1)S(1)}, u32[]{:S(2)}, u32[]{:S(2)}) collective-permute-start(bf16[384,3072]{1,0:T(8,128)(2,1)S(1)} %pad_maximum_fusion), channel_id=1, source_target_pairs={{0,1},{1,0},{2,3},{3,2},{4,5},{5,4},{6,7},{7,6},{8,9},{9,8},{10,11... | collective-permute-start | bytes 7077896 | tf_op jit(solution)/shard_map/ppermute | solution.py:1018
  136.6 37.6 %collective-permute-start.25 = (bf16[4,48,3072]{2,1,0:T(8,128)(2,1)S(1)}, bf16[4,48,3072]{2,1,0:T(8,128)(2,1)S(1)}, u32[]{:S(2)}, u32[]{:S(2)}) collective-permute-start(bf16[4,48,3072]{2,1,0:T(8,128)(2,1)S(1)} %get-tuple-element.189), channel_id=1, source_target_pairs={{0,4},{1,5},{2,6},{3,7},{4,0},{5,1},{6,2},{7,3},{8,12},{9,13},{10,... | collective-permute-start | bytes 3538952 | tf_op jit(solution)/shard_map/ppermute | solution.py:1018
  138.2 36.0 %collective-permute-start.21 = (bf16[4,48,3072]{2,1,0:T(8,128)(2,1)S(1)}, bf16[4,48,3072]{2,1,0:T(8,128)(2,1)S(1)}, u32[]{:S(2)}, u32[]{:S(2)}) collective-permute-start(bf16[4,48,3072]{2,1,0:T(8,128)(2,1)S(1)} %get-tuple-element.188), channel_id=1, source_target_pairs={{0,2},{1,3},{2,0},{3,1},{4,6},{5,7},{6,4},{7,5},{8,10},{9,11},{10,... | collective-permute-start | bytes 3538952 | tf_op jit(solution)/shard_map/ppermute | solution.py:1018
  185.8 45.0 %collective-permute-start.28 = (bf16[4,96,2304]{2,1,0:T(8,128)(2,1)S(1)}, bf16[4,96,2304]{2,1,0:T(8,128)(2,1)S(1)}, u32[]{:S(2)}, u32[]{:S(2)}) collective-permute-start(bf16[4,96,2304]{2,1,0:T(8,128)(2,1)S(1)} %get-tuple-element.224), channel_id=1, source_target_pairs={{0,1},{1,0},{2,3},{3,2},{4,5},{5,4},{6,7},{7,6},{8,9},{9,8},{10,11... | collective-permute-start | bytes 5308424 | tf_op jit(solution)/shard_map/ppermute | solution.py:1018
  185.8 16.1 %collective-permute-start.31 = (bf16[2,48,3072]{2,1,0:T(8,128)(2,1)S(1)}, bf16[2,48,3072]{2,1,0:T(8,128)(2,1)S(1)}, u32[]{:S(2)}, u32[]{:S(2)}) collective-permute-start(bf16[2,48,3072]{2,1,0:T(8,128)(2,1)S(1)} %get-tuple-element.211), channel_id=1, source_target_pairs={{0,2},{1,3},{2,0},{3,1},{4,6},{5,7},{6,4},{7,5},{8,10},{9,11},{10,... | collective-permute-start | bytes 1769480 | tf_op jit(solution)/shard_map/ppermute | solution.py:1018
  187.3 16.2 %collective-permute-start.30 = (bf16[2,48,3072]{2,1,0:T(8,128)(2,1)S(1)}, bf16[2,48,3072]{2,1,0:T(8,128)(2,1)S(1)}, u32[]{:S(2)}, u32[]{:S(2)}) collective-permute-start(bf16[2,48,3072]{2,1,0:T(8,128)(2,1)S(1)} %get-tuple-element.210), channel_id=1, source_target_pairs={{0,4},{1,5},{2,6},{3,7},{4,0},{5,1},{6,2},{7,3},{8,12},{9,13},{10,... | collective-permute-start | bytes 1769480 | tf_op jit(solution)/shard_map/ppermute | solution.py:1018
  187.8 41.0 %collective-permute-start.36 = (bf16[2,48,3840]{2,1,0:T(8,128)(2,1)S(1)}, bf16[2,48,3840]{2,1,0:T(8,128)(2,1)S(1)}, u32[]{:S(2)}, u32[]{:S(2)}) collective-permute-start(bf16[2,48,3840]{2,1,0:T(8,128)(2,1)S(1)} %get-tuple-element.223), channel_id=1, source_target_pairs={{0,4},{1,5},{2,6},{3,7},{4,0},{5,1},{6,2},{7,3},{8,12},{9,13},{10,... | collective-permute-start | bytes 2211848 | tf_op jit(solution)/shard_map/ppermute | solution.py:1018
  189.3 39.4 %collective-permute-start.29 = (bf16[2,48,3840]{2,1,0:T(8,128)(2,1)S(1)}, bf16[2,48,3840]{2,1,0:T(8,128)(2,1)S(1)}, u32[]{:S(2)}, u32[]{:S(2)}) collective-permute-start(bf16[2,48,3840]{2,1,0:T(8,128)(2,1)S(1)} %get-tuple-element.222), channel_id=1, source_target_pairs={{0,2},{1,3},{2,0},{3,1},{4,6},{5,7},{6,4},{7,5},{8,10},{9,11},{10,... | collective-permute-start | bytes 2211848 | tf_op jit(solution)/shard_map/ppermute | solution.py:1018
  204.4 20.9 %collective-permute-start.32 = (bf16[2,48,3072]{2,1,0:T(8,128)(2,1)S(1)}, bf16[2,48,3072]{2,1,0:T(8,128)(2,1)S(1)}, u32[]{:S(2)}, u32[]{:S(2)}) collective-permute-start(bf16[2,48,3072]{2,1,0:T(8,128)(2,1)S(1)} %get-tuple-element.230), channel_id=1, source_target_pairs={{0,8},{8,0},{16,24},{24,16},{1,9},{9,1},{17,25},{25,17},{2,10},{10... | collective-permute-start | bytes 1769480 | tf_op jit(solution)/shard_map/ppermute | solution.py:1018
  207.5 17.0 %collective-permute-start.33 = (bf16[2,104,768]{2,1,0:T(8,128)(2,1)S(1)}, bf16[2,104,768]{2,1,0:T(8,128)(2,1)S(1)}, u32[]{:S(2)}, u32[]{:S(2)}) collective-permute-start(bf16[2,104,768]{2,1,0:T(8,128)(2,1)S(1)} %pad_maximum_fusion.10), channel_id=1, source_target_pairs={{0,16},{8,24},{16,0},{24,8},{1,17},{9,25},{17,1},{25,9},{2,18},{10... | collective-permute-start | bytes 958472 | tf_op jit(solution)/shard_map/ppermute | solution.py:1018
  231.2 15.4 %collective-permute-start.40 = (bf16[2,48,2304]{2,1,0:T(8,128)(2,1)S(1)}, bf16[2,48,2304]{2,1,0:T(8,128)(2,1)S(1)}, u32[]{:S(2)}, u32[]{:S(2)}) collective-permute-start(bf16[2,48,2304]{2,1,0:T(8,128)(2,1)S(1)} %get-tuple-element.242), channel_id=1, source_target_pairs={{0,4},{1,5},{2,6},{3,7},{4,0},{5,1},{6,2},{7,3},{8,12},{9,13},{10,... | collective-permute-start | bytes 1327112 | tf_op jit(solution)/shard_map/ppermute | solution.py:1018
  232.3 14.8 %collective-permute-start.37 = (bf16[2,48,2304]{2,1,0:T(8,128)(2,1)S(1)}, bf16[2,48,2304]{2,1,0:T(8,128)(2,1)S(1)}, u32[]{:S(2)}, u32[]{:S(2)}) collective-permute-start(bf16[2,48,2304]{2,1,0:T(8,128)(2,1)S(1)} %get-tuple-element.241), channel_id=1, source_target_pairs={{0,2},{1,3},{2,0},{3,1},{4,6},{5,7},{6,4},{7,5},{8,10},{9,11},{10,... | collective-permute-start | bytes 1327112 | tf_op jit(solution)/shard_map/ppermute | solution.py:1018
  233.7 24.9 %collective-permute-start.42 = (bf16[2,48,3072]{2,1,0:T(8,128)(2,1)S(1)}, bf16[2,48,3072]{2,1,0:T(8,128)(2,1)S(1)}, u32[]{:S(2)}, u32[]{:S(2)}) collective-permute-start(bf16[2,48,3072]{2,1,0:T(8,128)(2,1)S(1)} %line_two.3.one), channel_id=1, source_target_pairs={{0,16},{8,24},{16,0},{24,8},{1,17},{9,25},{17,1},{25,9},{2,18},{10... | collective-permute-start | bytes 1769480 | tf_op jit(solution)/shard_map/ppermute | solution.py:1018
  242.1 22.0 %collective-permute-start.46 = (bf16[1,48,3840]{2,1,0:T(8,128)(2,1)S(1)}, bf16[1,48,3840]{2,1,0:T(8,128)(2,1)S(1)}, u32[]{:S(2)}, u32[]{:S(2)}) collective-permute-start(bf16[1,48,3840]{2,1,0:T(8,128)(2,1)S(1)} %get-tuple-element.250), channel_id=1, source_target_pairs={{0,8},{8,0},{16,24},{24,16},{1,9},{9,1},{17,25},{25,17},{2,10},{10... | collective-permute-start | bytes 1105928 | tf_op jit(solution)/shard_map/ppermute | solution.py:1018
  247.4 16.0 %collective-permute-start.44 = (bf16[1,48,2304]{2,1,0:T(8,128)(2,1)S(1)}, bf16[1,48,2304]{2,1,0:T(8,128)(2,1)S(1)}, u32[]{:S(2)}, u32[]{:S(2)}) collective-permute-start(bf16[1,48,2304]{2,1,0:T(8,128)(2,1)S(1)} %get-tuple-element.255), channel_id=1, source_target_pairs={{0,2},{1,3},{2,0},{3,1},{4,6},{5,7},{6,4},{7,5},{8,10},{9,11},{10,... | collective-permute-start | bytes 663560 | tf_op jit(solution)/shard_map/ppermute | solution.py:1018
  248.8 14.6 %collective-permute-start.41 = (bf16[1,48,2304]{2,1,0:T(8,128)(2,1)S(1)}, bf16[1,48,2304]{2,1,0:T(8,128)(2,1)S(1)}, u32[]{:S(2)}, u32[]{:S(2)}) collective-permute-start(bf16[1,48,2304]{2,1,0:T(8,128)(2,1)S(1)} %get-tuple-element.254), channel_id=1, source_target_pairs={{0,4},{1,5},{2,6},{3,7},{4,0},{5,1},{6,2},{7,3},{8,12},{9,13},{10,... | collective-permute-start | bytes 663560 | tf_op jit(solution)/shard_map/ppermute | solution.py:1018
  258.9 32.8 %collective-permute-start.50 = (bf16[2,48,3072]{2,1,0:T(8,128)(2,1)S(1)}, bf16[2,48,3072]{2,1,0:T(8,128)(2,1)S(1)}, u32[]{:S(2)}, u32[]{:S(2)}) collective-permute-start(bf16[2,48,3072]{2,1,0:T(8,128)(2,1)S(1)} %line_three.3.full), channel_id=1, source_target_pairs={{0,8},{8,0},{16,24},{24,16},{1,9},{9,1},{17,25},{25,17},{2,10},{10... | collective-permute-start | bytes 1769480 | tf_op jit(solution)/shard_map/ppermute | solution.py:1018
  264.3 25.4 %collective-permute-start.49 = (bf16[1,48,3840]{2,1,0:T(8,128)(2,1)S(1)}, bf16[1,48,3840]{2,1,0:T(8,128)(2,1)S(1)}, u32[]{:S(2)}, u32[]{:S(2)}) collective-permute-start(bf16[1,48,3840]{2,1,0:T(8,128)(2,1)S(1)} %line_two.4.one), channel_id=1, source_target_pairs={{0,16},{8,24},{16,0},{24,8},{1,17},{9,25},{17,1},{25,9},{2,18},{10... | collective-permute-start | bytes 1105928 | tf_op jit(solution)/shard_map/ppermute | solution.py:1018
  267.8 18.4 %collective-permute-start.45 = (bf16[1,48,2304]{2,1,0:T(8,128)(2,1)S(1)}, bf16[1,48,2304]{2,1,0:T(8,128)(2,1)S(1)}, u32[]{:S(2)}, u32[]{:S(2)}) collective-permute-start(bf16[1,48,2304]{2,1,0:T(8,128)(2,1)S(1)} %get-tuple-element.262), channel_id=1, source_target_pairs={{0,8},{8,0},{16,24},{24,16},{1,9},{9,1},{17,25},{25,17},{2,10},{10... | collective-permute-start | bytes 663560 | tf_op jit(solution)/shard_map/ppermute | solution.py:1018
  267.9 18.3 %collective-permute-start.47 = (f32[16,768]{1,0:T(8,128)S(1)}, f32[16,768]{1,0:T(8,128)S(1)}, u32[]{:S(2)}, u32[]{:S(2)}) collective-permute-start(f32[16,768]{1,0:T(8,128)S(1)} %add.23), channel_id=1, source_target_pairs={{0,8},{8,0},{16,24},{24,16},{1,9},{9,1},{17,25},{25,17},{2,10},{10... | collective-permute-start | bytes 147464 | tf_op jit(solution)/shard_map/ppermute | solution.py:1018
  286.2 16.3 %collective-permute-start.48 = (bf16[1,48,2304]{2,1,0:T(8,128)(2,1)S(1)}, bf16[1,48,2304]{2,1,0:T(8,128)(2,1)S(1)}, u32[]{:S(2)}, u32[]{:S(2)}) collective-permute-start(bf16[1,48,2304]{2,1,0:T(8,128)(2,1)S(1)} %line_two.5.one), channel_id=1, source_target_pairs={{0,16},{8,24},{16,0},{24,8},{1,17},{9,25},{17,1},{25,9},{2,18},{10... | collective-permute-start | bytes 663560 | tf_op jit(solution)/shard_map/ppermute | solution.py:1018
  289.8 19.3 %collective-permute-start.53 = (bf16[1,48,3840]{2,1,0:T(8,128)(2,1)S(1)}, bf16[1,48,3840]{2,1,0:T(8,128)(2,1)S(1)}, u32[]{:S(2)}, u32[]{:S(2)}) collective-permute-start(bf16[1,48,3840]{2,1,0:T(8,128)(2,1)S(1)} %line_three.4.full), channel_id=1, source_target_pairs={{0,8},{8,0},{16,24},{24,16},{1,9},{9,1},{17,25},{25,17},{2,10},{10... | collective-permute-start | bytes 1105928 | tf_op jit(solution)/shard_map/ppermute | solution.py:1018
  (37 other events, 374.9 us)

commit v3 on v2

--- a/solution.py
+++ b/solution.py
@@ -977,6 +977,103 @@
                 out[HALF:, block * D : (block + 1) * D] = high
 
 
+def chain_start(left, got_y, got_x, *outs):
+    def step(at):
+        for i, out in enumerate(outs):
+            out[0, :HALF, at] = (left[i, 0, :, at] + got_y[i, :, at].astype(F32)).astype(BF)
+            out[0, HALF:, at] = (left[i, 1, :, at] + got_x[i, :, at].astype(F32)).astype(BF)
+
+    by_columns(left.shape[-1], step)
+
+
+def chain_result(where, *refs):
+    inner = (where[1] == 1) | (where[1] == 2)
+    count = len(refs) // 3
+    for total, got, out in zip(refs[:count], refs[count : 2 * count], refs[2 * count :], strict=True):
+        for block in range(total.shape[-1] // D):
+            at = slice(block * D, (block + 1) * D)
+            value = jnp.where(inner, total[0, :, at].astype(F32), got[0, :, at].astype(F32))
+            if out.shape[1] == D:
+                out[block * SHARD : (block + 1) * SHARD, :] = value
+            else:
+                out[:, at] = value
+
+
+def put_small(target, at, value):
+    target[at : at + 8, :D] = value[:8]
+    target[at : at + 8, D : 2 * D] = value[8:]
+    target[at : at + 8, 2 * D :] = jnp.zeros((8, target.shape[1] - 2 * D), BF)
+
+
+def add_small(kept, source, at):
+    got = source[at : at + 8, : 2 * D].astype(F32)
+    return kept[...].astype(F32) + jnp.concatenate([got[:, :D], got[:, D:]], axis=0)
+
+
+def plane_one_both(keep, got, small, small_got, for_x, for_y, held, kept):
+    def step(at):
+        total = [keep[j, :, at].astype(F32) + got[j, :, at].astype(F32) for j in range(4)]
+        for_x[:HALF, at] = total[1][:HALF].astype(BF)
+        for_x[HALF:SHARD, at] = total[3][:HALF].astype(BF)
+        for_y[:HALF, at] = total[2][HALF:].astype(BF)
+        for_y[HALF:, at] = total[3][HALF:].astype(BF)
+        held[0, :, at] = total[0][:HALF]
+        held[1, :, at] = total[0][HALF:]
+        held[2, :, at] = total[2][:HALF]
+        held[3, :, at] = total[1][HALF:]
+
+    by_columns(keep.shape[-1], step)
+    value = (small[...] + small_got[...]).astype(BF)
+    kept[...] = value
+    put_small(for_x, SHARD, value)
+
+
+def plane_two_both(held, from_x, from_y, kept, next_y, next_x, left, kept_next):
+    def step(at):
+        next_y[:HALF, at] = (held[2, :, at] + from_x[HALF:SHARD, at].astype(F32)).astype(BF)
+        next_x[:, at] = (held[3, :, at] + from_y[HALF:, at].astype(F32)).astype(BF)
+        left[0, :, at] = held[0, :, at] + from_x[:HALF, at].astype(F32)
+        left[1, :, at] = held[1, :, at] + from_y[:HALF, at].astype(F32)
+
+    by_columns(held.shape[-1], step)
+    value = add_small(kept, from_x, SHARD).astype(BF)
+    kept_next[...] = value
+    put_small(next_y, HALF, value)
+
+
+def line_one_both(where, left, got_y, got_x, kept, out, stays, kept_next):
+    odd = where[1] & 1
+
+    def step(at):
+        first = left[0, :, at] + got_y[:HALF, at].astype(F32)
+        second = left[1, :, at] + got_x[:, at].astype(F32)
+        out[:HALF, at] = jnp.where(odd == 1, first, second).astype(BF)
+        stays[:, at] = jnp.where(odd == 1, second, first)
+
+    by_columns(left.shape[-1], step)
+    value = add_small(kept, got_y, HALF).astype(BF)
+    kept_next[...] = value
+    put_small(out, HALF, value)
+
+
+def line_two_both(stays, near, kept, pair, kept_next):
+    def step(at):
+        pair[:HALF, at] = (stays[:, at] + near[:HALF, at].astype(F32)).astype(BF)
+
+    by_columns(stays.shape[-1], step)
+    value = add_small(kept, near, HALF).astype(BF)
+    kept_next[...] = value
+    put_small(pair, HALF, value)
+
+
+def line_three_both(pair, far, kept, full, small):
+    def step(at):
+        full[0, :, at] = (pair[:HALF, at].astype(F32) + far[:HALF, at].astype(F32)).astype(BF)
+
+    by_columns(full.shape[-1], step)
+    small[...] = add_small(kept, far, HALF)
+
+
 def shape(*dims, dtype=BF):
     return jax.ShapeDtypeStruct(dims, dtype)
 
@@ -1100,12 +1197,118 @@
         )
 
 
-def reduce_small(small):
-    for pairs in (CORE, ACROSS, UP):
-        small = small + swap(small, pairs)
-    for pairs in (NEAR, FAR):
-        small = small + swap(small, pairs, "frame")
-    return small
+class ReductionChain(Reduction):
+    def chain_one(self, *earlier):
+        self.mine = whole_call(
+            chain_start,
+            "chain_start",
+            [shape(1, SHARD, self.width)] * self.count,
+            self.left,
+            after(self.got_y, *earlier),
+            after(self.got_x, *earlier),
+        )
+        self.inward = [swap(v, [(0, 1), (3, 2)], "frame") for v in self.mine]
+        self.pair, self.across = [None] * self.count, [None] * self.count
+        self.total, self.outward = [None] * self.count, [None] * self.count
+        return tuple(self.mine)
+
+    def chain_two(self, i, *earlier):
+        out = shape(1, SHARD, self.width)
+        self.pair[i] = whole_call(
+            pair_sums, "chain_two", out, self.mine[i], after(self.inward[i], *earlier)
+        )
+        self.across[i] = swap(self.pair[i], [(1, 2), (2, 1)], "frame")
+        return (self.pair[i],)
+
+    def chain_three(self, i, *earlier):
+        out = shape(1, SHARD, self.width)
+        self.total[i] = whole_call(
+            pair_sums, "chain_three", out, self.pair[i], after(self.across[i], *earlier)
+        )
+        self.outward[i] = swap(self.total[i], [(1, 0), (2, 3)], "frame")
+        return (self.total[i],)
+
+    def chain_result(self, i, out, *earlier):
+        got = after(self.outward[i], *earlier)
+        return whole_call(
+            chain_result, "chain_result", [out], self.where, self.total[i], got, scalars=1
+        )[0]
+
+
+class ReductionBoth(Reduction):
+    def __init__(self, where, keep, send, small):
+        super().__init__(where, [keep], [send])
+        self.small, self.small_got = small, swap(small, CORE)
+
+    def flat(self, rows, dtype=BF):
+        return shape(rows, self.width, dtype=dtype)
+
+    def plane_one(self, *earlier):
+        kept = shape(16, D)
+        for_x, for_y, self.held, self.kept = whole_call(
+            plane_one_both,
+            "plane_one_both",
+            [self.flat(SHARD + 8), self.flat(SHARD), self.shape(4, dtype=F32), kept],
+            self.keep[0],
+            after(self.got[0], *earlier),
+            self.small,
+            self.small_got,
+            mebibytes=24,
+        )
+        self.from_x, self.from_y = swap(for_x, ACROSS), swap(for_y, UP)
+        return for_x, for_y
+
+    def plane_two(self, *earlier):
+        next_y, next_x, self.left, self.kept = whole_call(
+            plane_two_both,
+            "plane_two_both",
+            [self.flat(HALF + 8), self.flat(HALF), self.shape(2, dtype=F32), shape(16, D)],
+            self.held,
+            after(self.from_x, *earlier),
+            after(self.from_y, *earlier),
+            self.kept,
+        )
+        self.got_y, self.got_x = swap(next_y, UP), swap(next_x, ACROSS)
+        return next_y, next_x
+
+    def line_one(self, *earlier):
+        out, self.stays, self.kept = whole_call(
+            line_one_both,
+            "line_one_both",
+            [self.flat(HALF + 8), self.flat(HALF, F32), shape(16, D)],
+            self.where,
+            self.left,
+            after(self.got_y, *earlier),
+            after(self.got_x, *earlier),
+            self.kept,
+            scalars=1,
+        )
+        self.near = swap(out, NEAR, "frame")
+        return (out,)
+
+    def line_two(self, *earlier):
+        self.pair, self.kept = whole_call(
+            line_two_both,
+            "line_two_both",
+            [self.flat(HALF + 8), shape(16, D)],
+            self.stays,
+            after(self.near, *earlier),
+            self.kept,
+        )
+        self.far = swap(self.pair, FAR, "frame")
+        return (self.pair,)
+
+    def line_three(self, *earlier):
+        self.full, self.small = whole_call(
+            line_three_both,
+            "line_three_both",
+            [self.shape(1), shape(16, D, dtype=F32)],
+            self.pair,
+            after(self.far, *earlier),
+            self.kept,
+        )
+        self.other = swap(self.full, NEAR, "frame")
+        return (self.full,)
 
 
 def body(
@@ -1272,7 +1475,7 @@
         *(where, normed_three, after_space, cot, params, bias_full),
         *(expand_weight, contract, r3x, r3y, r4y, r4x, c3, c4, c5),
     )
-    forward_sum = Reduction(where, [keep_we, keep_wc], [send_we, send_wc])
+    forward_sum = ReductionChain(where, [keep_we, keep_wc], [send_we, send_wc])
 
     grad_packed = pl.pallas_call(
         spatial_back,
@@ -1343,21 +1546,13 @@
         cost_estimate=NO_COST,
     )(*video_pieces, after(grad_pieces[0], output), *grad_pieces[1:], packed_place, small, entry_full)
 
-    step = lambda total, pairs, *axis: (total, swap(total, pairs, *axis))
-    join = lambda both, *earlier: both[0] + after(both[1], *earlier)
     placed = forward_sum.plane_two(small)
-    space_sum = Reduction(where, [keep_space], [after(send_space, *placed)])
-    near = swap(after(jnp.stack([normed_back[1], normed_back[3]]), *placed), NEAR, "frame")
+    space_sum = ReductionBoth(where, keep_space, after(send_space, *placed), after(small, *placed))
+    normed_back = shift([after(v, *placed) for v in normed_back])
     keep_time, send_time = grads((after(normed_place, *placed), grad_place))
     placed = space_sum.plane_one(send_time)
-    time_sum = Reduction(where, [keep_time], [after(send_time, near, *placed)])
-    placed = forward_sum.line_one(*placed, near)
-    far = swap(after(jnp.stack([normed_back[2], near[1]]), *placed), FAR, "frame")
-    small = step(join(step(after(small, *placed), CORE)), ACROSS)
-    placed = forward_sum.line_two(*placed, far)
-    small = join(small, *placed)
-    placed = space_sum.plane_two(*placed, small)
-    placed = time_sum.plane_one(*placed)
+    placed = forward_sum.chain_one(*placed, *normed_back[1:])
+    time_sum = Reduction(where, [keep_time], [after(send_time, *placed)])
     input_grad = whole_call(
         input_back,
         "input_back",
@@ -1366,28 +1561,27 @@
         after(tokens, *placed),
         grad_first,
         params,
-        *(normed_back[0], near[0], far[0], far[1]),
+        *normed_back,
         scalars=1,
         scratch=[pltpu.VMEM((ROWS, D), BF)],
     )
-    placed = space_sum.line_one(*placed, input_grad)
-    placed = time_sum.plane_two(*placed)
-    small = step(after(small, *placed), UP)
-    placed = forward_sum.line_three(*placed)
-    small = join(small, *placed)
-    placed = time_sum.line_one(*placed, small)
-    small = step(after(small, *placed), NEAR, "frame")
+    placed = forward_sum.chain_two(0, *placed, input_grad)
+    placed = space_sum.plane_two(*placed)
+    placed = forward_sum.chain_two(1, *placed)
+    placed = forward_sum.chain_three(0, *placed)
+    placed = space_sum.line_one(*placed)
+    placed = time_sum.plane_one(*placed)
+    placed = forward_sum.chain_three(1, *placed)
+    wide = lambda rows, columns: shape(rows, columns, dtype=F32)
+    grad_expand = forward_sum.chain_result(0, wide(SHARD, WIDE), *placed)
+    placed = time_sum.plane_two(*placed, grad_expand)
     placed = space_sum.line_two(*placed)
-    small = join(small, *placed)
-    placed = time_sum.line_two(*placed, small)
-    small = step(after(small, *placed), FAR, "frame")
-    wide = lambda rows, columns: shape(rows, columns, dtype=F32)
-    grad_expand, grad_contract = forward_sum.result(
-        ((0, 0, WIDE), (1, 0, WIDE)), [wide(SHARD, WIDE), wide(4 * SHARD, D)]
-    )
+    placed = time_sum.line_one(*placed)
+    placed = time_sum.line_two(*placed)
+    grad_contract = forward_sum.chain_result(1, wide(4 * SHARD, D), *placed)
     placed = space_sum.line_three(*placed)
-    small = join(small, *placed)
-    placed = time_sum.line_three(*placed, grad_contract, small)
+    small = space_sum.small
+    placed = time_sum.line_three(*placed, grad_contract)
     input_grad = jnp.swapaxes(input_grad, 1, 2)
     grad_exit_time, grad_entry_space, grad_exit_space = space_sum.result(
         ((0, 0, D), (0, D, 3 * D), (0, 4 * D, D)),

time: 313 us -> 301 us (0.962)
  waiting for transfers between devices: 136 us -> 128 us
  starting transfers between devices: 68.2 us -> 63.5 us
    ppermute x45 -> x42, waiting for transfers between devices: 129 us -> 115 us  [swap(): return lax.ppermute(value, axis, pairs)]
    ppermute x45 -> x42, starting transfers between devices: 53.3 us -> 41.3 us  [swap(): return lax.ppermute(value, axis, pairs)]
    ppermute x9 -> x12, starting transfers between devices: 14.9 us -> 22.1 us  [shift(): lax.ppermute(pieces[k], 'frame', [(i, i ^ k) for i in range(4)])]
    ppermute x9 -> x12, waiting for transfers between devices: 6.56 us -> 12.7 us  [shift(): lax.ppermute(pieces[k], 'frame', [(i, i ^ k) for i in range(4)])]
    pallas_call x21 -> x24, Pallas kernels: 19.1 us -> 20.2 us  [whole_call(): pl.pallas_call(functools.partial(kernel, **options), name=name, out_shape...]
  transfers between devices with their start and end apart: 54 -> 54, of which waited for: 27 -> 26; matrix products, arithmetic and copies ran while one was open for 2% -> 3% of each run, Pallas kernels for 23% -> 24%
where the time goes in v3:
time: 301 us
  waiting for transfers between devices  128 us (43%)
  Pallas kernels  99.7 us (33%)
  starting transfers between devices  63.5 us (21%)
  local copies, waits for them, and re-layouts  7.87 us (3%)
    ppermute x42, waiting for transfers between devices, swap(): return lax.ppermute(value, axis, pairs)  115 us
    ppermute x42, starting transfers between devices, swap(): return lax.ppermute(value, axis, pairs)  41.3 us
    ppermute x12, starting transfers between devices, shift(): lax.ppermute(pieces[k], 'frame', [(i, i ^ k) for i in range(4)])  22.1 us
    pallas_call x1, Pallas kernels, body(): pl.pallas_call(feed_forward, name='feed_forward', out_shape=[shape(*video...  21.2 us
    pallas_call x24, Pallas kernels, whole_call(): pl.pallas_call(functools.partial(kernel, **options), name=name, out_shape...  20.2 us
    pallas_call x1, Pallas kernels, body(): pl.pallas_call(temporal_back, name='temporal_back', out_shape=[shape(SPOT...  13.6 us
    ppermute x12, waiting for transfers between devices, shift(): lax.ppermute(pieces[k], 'frame', [(i, i ^ k) for i in range(4)])  12.7 us
    pallas_call x1, Pallas kernels, body(): pl.pallas_call(spatial_forward, name='spatial_forward', out_shape=[shape(...  12.5 us
  transfers between devices with their start and end apart: 54, of which 26 were waited for; matrix products, arithmetic and copies ran while one was open for 3% of the time, Pallas kernels for 24%

profile of v3, /device:TPU:0, one launch (start us, length us, event | category | flops | bytes accessed | tf_op | source)
XLA Modules:
  0.0 300.8 jit_solution(15408048447208354234)
XLA Ops:
  3.4 3.0 collective-permute-start
  13.0 2.6 collective-permute-start.4
  19.7 20.0 %collective-permute-done.2.refs_8_ = bf16[160,3072]{1,0:T(8,128)(2,1)S(1)} collective-permute-done((bf16[160,3072]{1,0:T(8,128)(2,1)S(1)}, bf16[160,3072]{1,0:T(8,128)(2,1)S(1)}, u32[]{:S(2)}, u32[]{:S(2)}) %collective-permute-start.2) | collective-permute-done | bytes 983072 | tf_op jit(solution)/shard_map/ppermute | solution.py:1115
  42.4 2.3 collective-permute-done.8.refs_10_
  44.7 10.2 %temporal_forward.1 = (bf16[104,768]{1,0:T(8,128)(2,1)S(1)}, bf16[104,768]{1,0:T(8,128)(2,1)S(1)}, bf16[104,768]{1,0:T(8,128)(2,1)S(1)}, bf16[104,768]{1,0:T(8,1...) custom-call(bf16[104,768]{1,0:T(8,128)(2,1)S(1)} %get-tuple-element., ...), custom_call_target="tpu_custom_call" | custom-call | flops 1000 | bytes 1000 | tf_op jit(solution)/shard_map/temporal_forward/pallas_call | solution.py:1371
  54.9 2.7 collective-permute-start.10
  59.2 9.4 %collective-permute-done.6.refs_11_.refs_2_ = bf16[192,3072]{1,0:T(8,128)(2,1)S(1)} collective-permute-done((bf16[192,3072]{1,0:T(8,128)(2,1)S(1)}, bf16[192,3072]{1,0:T(8,128)(2,1)S(1)}, u32[]{:S(2)}, u32[]{:S(2)}) %collective-permute-start.6) | collective-permute-done | bytes 1179680 | tf_op jit(solution)/shard_map/ppermute | solution.py:1115
  75.1 12.5 %spatial_forward.1 = (f32[416,768]{1,0:T(8,128)S(1)}, bf16[416,768]{1,0:T(8,128)(2,1)S(1)}, bf16[768,2304]{1,0:T(8,128)(2,1)}, bf16[768,768]{1,0:T(8,128)(2,1)},...) custom-call(bf16[416,768]{1,0:T(8,128)(2,1)S(1)} %get-tuple-element., ...), custom_call_target="tpu_custom_call" | custom-call | flops 1000 | bytes 1000 | tf_op jit(solution)/shard_map/spatial_forward/pallas_call | solution.py:1415
  87.8 11.3 %collective-permute-done.15.refs_5_ = bf16[192,3072]{1,0:T(8,128)(2,1)S(1)} collective-permute-done((bf16[192,3072]{1,0:T(8,128)(2,1)S(1)}, bf16[192,3072]{1,0:T(8,128)(2,1)S(1)}, u32[]{:S(2)}, u32[]{:S(2)}) %collective-permute-start.15) | collective-permute-done | bytes 1179680 | tf_op jit(solution)/shard_map/ppermute | solution.py:1115
  99.6 2.3 collective-permute-done.18.refs_8_
  103.6 21.2 %feed_forward.1 = (bf16[1,2,196,768]{3,2,1,0:T(8,128)(2,1)S(1)}, f32[416,768]{1,0:T(8,128)S(1)}, bf16[416,768]{1,0:T(8,128)(2,1)S(1)}, bf16[4,96,3072]{2,1,0:T(8...) custom-call(s32[2]{0:T(128)S(1)} %pad_add_fusion.where, ...), custom_call_target="tpu_custom_call" | custom-call | flops 1000 | bytes 1000 | tf_op jit(solution)/shard_map/feed_forward/pallas_call | solution.py:1448
  125.4 9.9 %spatial_back.1.refs_0_.refs_3_ = bf16[416,2304]{1,0:T(8,128)(2,1)S(1)} custom-call(bf16[416,768]{1,0:T(8,128)(2,1)S(1)} %get-tuple-element.180.branch.refs_1_.refs_5_, bf16[416,2304]{1,0:T(8,128)(2,1)S(1)} %copy-done.4, bf16[768,768]{1,0:T(8,128)(2,1)S(1)} %copy-done.7), custom_call_target="tpu_custom_call" | custom-call | flops 1000 | bytes 1000 | tf_op jit(solution)/shard_map/spatial_back/pallas_call | solution.py:1480
  138.8 4.5 %spatial_back_norm.1 = (f32[416,768]{1,0:T(8,128)S(1)}, bf16[416,768]{1,0:T(8,128)(2,1)S(1)}, f32[16,768]{1,0:T(8,128)S(1)}, bf16[104,768]{1,0:T(8,128)(2,1)S(1)...) custom-call(s32[2]{0:T(128)S(1)} %pad_add_fusion.where, ...), custom_call_target="tpu_custom_call" | custom-call | flops 1000 | bytes 1000 | tf_op jit(solution)/shard_map/spatial_back_norm/pallas_call | solution.py:1095
  143.3 2.8 collective-permute-start.22
  149.5 6.3 %weight_grads.2 = (bf16[4,96,3840]{2,1,0:T(8,128)(2,1)S(1)}, bf16[4,96,3840]{2,1,0:T(8,128)(2,1)S(1)}) custom-call(s32[2]{0:T(128)S(1)} %pad_add_fusion.where, bf16[416,768]{1,0:T(8,128)(2,1)S(1)} %copy-done.8, bf16[416,768]{1,0:T(8,128)(2,1)S(1)} %get-tuple-element.196.refs_1_, bf16[416,768]{1,0:T(8,128)(2,1)S(1)} %copy-done.9, ...), custom_call_target="tpu_custom_call" | custom-call | flops 1000 | bytes 1000 | tf_op jit(solution)/shard_map/weight_grads/pallas_call | solution.py:1518
  155.8 4.8 %collective-permute-done.23.refs_6_ = bf16[104,768]{1,0:T(8,128)(2,1)S(1)} collective-permute-done((bf16[104,768]{1,0:T(8,128)(2,1)S(1)}, bf16[104,768]{1,0:T(8,128)(2,1)S(1)}, u32[]{:S(2)}, u32[]{:S(2)}) %collective-permute-start.23) | collective-permute-done | bytes 159776 | tf_op jit(solution)/shard_map/ppermute | solution.py:1119
  160.6 13.6 %temporal_back.1 = (bf16[400,2304]{1,0:T(8,128)(2,1)S(1)}, f32[16,768]{1,0:T(8,128)S(1)}, bf16[104,768]{1,0:T(8,128)(2,1)S(1)}, bf16[104,768]{1,0:T(8,128)(2,1)S...) custom-call(bf16[104,768]{1,0:T(8,128)(2,1)S(1)} %get-tuple-element.163.refs_0_, ...), custom_call_target="tpu_custom_call" | custom-call | flops 1000 | bytes 1000 | tf_op jit(solution)/shard_map/temporal_back/pallas_call | solution.py:1538
  176.9 2.8 collective-permute-start.31
  180.3 4.4 %collective-permute-start.30 = (bf16[104,768]{1,0:T(8,128)(2,1)S(1)}, bf16[104,768]{1,0:T(8,128)(2,1)S(1)}, u32[]{:S(2)}, u32[]{:S(2)}) collective-permute-start(bf16[104,768]{1,0:T(8,128)(2,1)S(1)} %get-tuple-element.229), channel_id=1, source_target_pairs={{0,16},{8,24},{16,0},{24,8},{1,17},{9,25},{17,1},{25,9},{2,18},{10... | collective-permute-start | bytes 479240 | tf_op jit(solution)/shard_map/ppermute | solution.py:1119
  184.7 3.9 %weight_grads.3 = (bf16[4,96,2304]{2,1,0:T(8,128)(2,1)S(1)}, bf16[4,96,2304]{2,1,0:T(8,128)(2,1)S(1)}) custom-call(s32[2]{0:T(128)S(1)} %pad_add_fusion.where, bf16[400,768]{1,0:T(8,128)(2,1)S(1)} %copy-done.11, bf16[400,2304]{1,0:T(8,128)(2,1)S(1)} %get-tuple-element.220.refs_1_), custom_call_target="tpu_custom_call" | custom-call | flops 1000 | bytes 1000 | tf_op jit(solution)/shard_map/weight_grads/pallas_call | solution.py:1518
  189.4 6.1 %collective-permute-done.30.refs_2_ = bf16[104,768]{1,0:T(8,128)(2,1)S(1)} collective-permute-done((bf16[104,768]{1,0:T(8,128)(2,1)S(1)}, bf16[104,768]{1,0:T(8,128)(2,1)S(1)}, u32[]{:S(2)}, u32[]{:S(2)}) %collective-permute-start.30) | collective-permute-done | bytes 159776 | tf_op jit(solution)/shard_map/ppermute | solution.py:1119
  202.9 8.6 %collective-permute-done.35.two = bf16[1,96,3072]{2,1,0:T(8,128)(2,1)S(1)} collective-permute-done((bf16[1,96,3072]{2,1,0:T(8,128)(2,1)S(1)}, bf16[1,96,3072]{2,1,0:T(8,128)(2,1)S(1)}, u32[]{:S(2)}, u32[]{:S(2)}) %collective-permute-start.35) | collective-permute-done | bytes 589856 | tf_op jit(solution)/shard_map/ppermute | solution.py:1115
  212.3 4.9 %collective-permute-done.36.from_y = bf16[96,3840]{1,0:T(8,128)(2,1)S(1)} collective-permute-done((bf16[96,3840]{1,0:T(8,128)(2,1)S(1)}, bf16[96,3840]{1,0:T(8,128)(2,1)S(1)}, u32[]{:S(2)}, u32[]{:S(2)}) %collective-permute-start.36) | collective-permute-done | bytes 737312 | tf_op jit(solution)/shard_map/ppermute | solution.py:1115
  220.3 3.4 %collective-permute-done.39.two = bf16[1,96,3072]{2,1,0:T(8,128)(2,1)S(1)} collective-permute-done((bf16[1,96,3072]{2,1,0:T(8,128)(2,1)S(1)}, bf16[1,96,3072]{2,1,0:T(8,128)(2,1)S(1)}, u32[]{:S(2)}, u32[]{:S(2)}) %collective-permute-start.39) | collective-permute-done | bytes 589856 | tf_op jit(solution)/shard_map/ppermute | solution.py:1115
  226.1 3.3 %collective-permute-done.40.got_x = bf16[48,3840]{1,0:T(8,128)(2,1)S(1)} collective-permute-done((bf16[48,3840]{1,0:T(8,128)(2,1)S(1)}, bf16[48,3840]{1,0:T(8,128)(2,1)S(1)}, u32[]{:S(2)}, u32[]{:S(2)}) %collective-permute-start.40) | collective-permute-done | bytes 368672 | tf_op jit(solution)/shard_map/ppermute | solution.py:1115
  232.8 2.6 collective-permute-start.46
  235.6 10.6 %collective-permute-done.43.refs_1_ = bf16[1,96,3072]{2,1,0:T(8,128)(2,1)S(1)} collective-permute-done((bf16[1,96,3072]{2,1,0:T(8,128)(2,1)S(1)}, bf16[1,96,3072]{2,1,0:T(8,128)(2,1)S(1)}, u32[]{:S(2)}, u32[]{:S(2)}) %collective-permute-start.43) | collective-permute-done | bytes 589856 | tf_op jit(solution)/shard_map/ppermute | solution.py:1115
  251.5 3.9 %collective-permute-done.46.near = bf16[56,3840]{1,0:T(8,128)(2,1)S(1)} collective-permute-done((bf16[56,3840]{1,0:T(8,128)(2,1)S(1)}, bf16[56,3840]{1,0:T(8,128)(2,1)S(1)}, u32[]{:S(2)}, u32[]{:S(2)}) %collective-permute-start.46) | collective-permute-done | bytes 430112 | tf_op jit(solution)/shard_map/ppermute | solution.py:1115
  257.0 2.6 collective-permute-start.48
  259.6 20.5 %collective-permute-done.48.two = bf16[1,48,2304]{2,1,0:T(8,128)(2,1)S(1)} collective-permute-done((bf16[1,48,2304]{2,1,0:T(8,128)(2,1)S(1)}, bf16[1,48,2304]{2,1,0:T(8,128)(2,1)S(1)}, u32[]{:S(2)}, u32[]{:S(2)}) %collective-permute-start.48) | collective-permute-done | bytes 221216 | tf_op jit(solution)/shard_map/ppermute | solution.py:1115
  281.0 2.5 collective-permute-start.53
  285.2 5.7 %collective-permute-done.49.two = bf16[1,48,2304]{2,1,0:T(8,128)(2,1)S(1)} collective-permute-done((bf16[1,48,2304]{2,1,0:T(8,128)(2,1)S(1)}, bf16[1,48,2304]{2,1,0:T(8,128)(2,1)S(1)}, u32[]{:S(2)}, u32[]{:S(2)}) %collective-permute-start.49) | collective-permute-done | bytes 221216 | tf_op jit(solution)/shard_map/ppermute | solution.py:1115
  (169 shorter events, 74.2 us)
Async XLA Ops:
  3.4 13.8 %collective-permute-start = (bf16[56,3072]{1,0:T(8,128)(2,1)S(1)}, bf16[56,3072]{1,0:T(8,128)(2,1)S(1)}, u32[]{:S(2)}, u32[]{:S(2)}) collective-permute-start(bf16[56,3072]{1,0:T(8,128)(2,1)S(1)} %get-tuple-element.149.refs_4_), channel_id=1, source_target_pairs={{0,2},{1,3},{2,0},{3,1},{4,6},{5,7},{6,4},{7,5},{8,10},{9,11},{10,... | collective-permute-start | bytes 1032200 | tf_op jit(solution)/shard_map/ppermute | solution.py:1115
  11.4 28.7 %collective-permute-start.3 = (bf16[104,768]{1,0:T(8,128)(2,1)S(1)}, bf16[104,768]{1,0:T(8,128)(2,1)S(1)}, u32[]{:S(2)}, u32[]{:S(2)}) collective-permute-start(bf16[104,768]{1,0:T(8,128)(2,1)S(1)} %get-tuple-element.155), channel_id=1, source_target_pairs={{0,8},{8,0},{16,24},{24,16},{1,9},{9,1},{17,25},{25,17},{2,10},{10... | collective-permute-start | bytes 479240 | tf_op jit(solution)/shard_map/ppermute | solution.py:1119
  13.0 27.1 %collective-permute-start.4 = (bf16[104,768]{1,0:T(8,128)(2,1)S(1)}, bf16[104,768]{1,0:T(8,128)(2,1)S(1)}, u32[]{:S(2)}, u32[]{:S(2)}) collective-permute-start(bf16[104,768]{1,0:T(8,128)(2,1)S(1)} %get-tuple-element.156), channel_id=1, source_target_pairs={{0,16},{8,24},{16,0},{24,8},{1,17},{9,25},{17,1},{25,9},{2,18},{10... | collective-permute-start | bytes 479240 | tf_op jit(solution)/shard_map/ppermute | solution.py:1119
  15.6 24.5 %collective-permute-start.5 = (bf16[104,768]{1,0:T(8,128)(2,1)S(1)}, bf16[104,768]{1,0:T(8,128)(2,1)S(1)}, u32[]{:S(2)}, u32[]{:S(2)}) collective-permute-start(bf16[104,768]{1,0:T(8,128)(2,1)S(1)} %get-tuple-element.157), channel_id=1, source_target_pairs={{0,24},{8,16},{16,8},{24,0},{1,25},{9,17},{17,9},{25,1},{2,26},{10... | collective-permute-start | bytes 479240 | tf_op jit(solution)/shard_map/ppermute | solution.py:1119
  17.3 22.4 %collective-permute-start.2 = (bf16[160,3072]{1,0:T(8,128)(2,1)S(1)}, bf16[160,3072]{1,0:T(8,128)(2,1)S(1)}, u32[]{:S(2)}, u32[]{:S(2)}) collective-permute-start(bf16[160,3072]{1,0:T(8,128)(2,1)S(1)} %pad_maximum_fusion.5), channel_id=1, source_target_pairs={{0,4},{1,5},{2,6},{3,7},{4,0},{5,1},{6,2},{7,3},{8,12},{9,13},{10,... | collective-permute-start | bytes 2949128 | tf_op jit(solution)/shard_map/ppermute | solution.py:1115
  19.0 20.8 %collective-permute-start.7 = (bf16[144,3072]{1,0:T(8,128)(2,1)S(1)}, bf16[144,3072]{1,0:T(8,128)(2,1)S(1)}, u32[]{:S(2)}, u32[]{:S(2)}) collective-permute-start(bf16[144,3072]{1,0:T(8,128)(2,1)S(1)} %pad_maximum_fusion.6), channel_id=1, source_target_pairs={{0,2},{1,3},{2,0},{3,1},{4,6},{5,7},{6,4},{7,5},{8,10},{9,11},{10,... | collective-permute-start | bytes 2654216 | tf_op jit(solution)/shard_map/ppermute | solution.py:1115
  40.1 28.4 %collective-permute-start.6 = (bf16[192,3072]{1,0:T(8,128)(2,1)S(1)}, bf16[192,3072]{1,0:T(8,128)(2,1)S(1)}, u32[]{:S(2)}, u32[]{:S(2)}) collective-permute-start(bf16[192,3072]{1,0:T(8,128)(2,1)S(1)} %pad_maximum_fusion.1), channel_id=1, source_target_pairs={{0,2},{1,3},{2,0},{3,1},{4,6},{5,7},{6,4},{7,5},{8,10},{9,11},{10,... | collective-permute-start | bytes 3538952 | tf_op jit(solution)/shard_map/ppermute | solution.py:1115
  40.9 29.3 %collective-permute-start.12 = (bf16[192,3072]{1,0:T(8,128)(2,1)S(1)}, bf16[192,3072]{1,0:T(8,128)(2,1)S(1)}, u32[]{:S(2)}, u32[]{:S(2)}) collective-permute-start(bf16[192,3072]{1,0:T(8,128)(2,1)S(1)} %pad_maximum_fusion.2), channel_id=1, source_target_pairs={{0,4},{1,5},{2,6},{3,7},{4,0},{5,1},{6,2},{7,3},{8,12},{9,13},{10,... | collective-permute-start | bytes 3538952 | tf_op jit(solution)/shard_map/ppermute | solution.py:1115
  54.9 14.8 %collective-permute-start.10 = (bf16[104,768]{1,0:T(8,128)(2,1)S(1)}, bf16[104,768]{1,0:T(8,128)(2,1)S(1)}, u32[]{:S(2)}, u32[]{:S(2)}) collective-permute-start(bf16[104,768]{1,0:T(8,128)(2,1)S(1)} %get-tuple-element.165), channel_id=1, source_target_pairs={{0,16},{8,24},{16,0},{24,8},{1,17},{9,25},{17,1},{25,9},{2,18},{10... | collective-permute-start | bytes 479240 | tf_op jit(solution)/shard_map/ppermute | solution.py:1119
  70.6 28.4 %collective-permute-start.15 = (bf16[192,3072]{1,0:T(8,128)(2,1)S(1)}, bf16[192,3072]{1,0:T(8,128)(2,1)S(1)}, u32[]{:S(2)}, u32[]{:S(2)}) collective-permute-start(bf16[192,3072]{1,0:T(8,128)(2,1)S(1)} %pad_maximum_fusion.4), channel_id=1, source_target_pairs={{0,2},{1,3},{2,0},{3,1},{4,6},{5,7},{6,4},{7,5},{8,10},{9,11},{10,... | collective-permute-start | bytes 3538952 | tf_op jit(solution)/shard_map/ppermute | solution.py:1115
  71.5 28.2 %collective-permute-start.14 = (bf16[192,3072]{1,0:T(8,128)(2,1)S(1)}, bf16[192,3072]{1,0:T(8,128)(2,1)S(1)}, u32[]{:S(2)}, u32[]{:S(2)}) collective-permute-start(bf16[192,3072]{1,0:T(8,128)(2,1)S(1)} %pad_maximum_fusion.3), channel_id=1, source_target_pairs={{0,4},{1,5},{2,6},{3,7},{4,0},{5,1},{6,2},{7,3},{8,12},{9,13},{10,... | collective-permute-start | bytes 3538952 | tf_op jit(solution)/shard_map/ppermute | solution.py:1115
  87.6 16.0 %collective-permute-start.16 = (bf16[384,3072]{1,0:T(8,128)(2,1)S(1)}, bf16[384,3072]{1,0:T(8,128)(2,1)S(1)}, u32[]{:S(2)}, u32[]{:S(2)}) collective-permute-start(bf16[384,3072]{1,0:T(8,128)(2,1)S(1)} %pad_maximum_fusion), channel_id=1, source_target_pairs={{0,1},{1,0},{2,3},{3,2},{4,5},{5,4},{6,7},{7,6},{8,9},{9,8},{10,11... | collective-permute-start | bytes 7077896 | tf_op jit(solution)/shard_map/ppermute | solution.py:1115
  136.6 37.6 %collective-permute-start.25 = (bf16[4,48,3072]{2,1,0:T(8,128)(2,1)S(1)}, bf16[4,48,3072]{2,1,0:T(8,128)(2,1)S(1)}, u32[]{:S(2)}, u32[]{:S(2)}) collective-permute-start(bf16[4,48,3072]{2,1,0:T(8,128)(2,1)S(1)} %get-tuple-element.193), channel_id=1, source_target_pairs={{0,4},{1,5},{2,6},{3,7},{4,0},{5,1},{6,2},{7,3},{8,12},{9,13},{10,... | collective-permute-start | bytes 3538952 | tf_op jit(solution)/shard_map/ppermute | solution.py:1115
  138.2 36.0 %collective-permute-start.21 = (bf16[4,48,3072]{2,1,0:T(8,128)(2,1)S(1)}, bf16[4,48,3072]{2,1,0:T(8,128)(2,1)S(1)}, u32[]{:S(2)}, u32[]{:S(2)}) collective-permute-start(bf16[4,48,3072]{2,1,0:T(8,128)(2,1)S(1)} %get-tuple-element.192), channel_id=1, source_target_pairs={{0,2},{1,3},{2,0},{3,1},{4,6},{5,7},{6,4},{7,5},{8,10},{9,11},{10,... | collective-permute-start | bytes 3538952 | tf_op jit(solution)/shard_map/ppermute | solution.py:1115
  146.1 14.5 %collective-permute-start.23 = (bf16[104,768]{1,0:T(8,128)(2,1)S(1)}, bf16[104,768]{1,0:T(8,128)(2,1)S(1)}, u32[]{:S(2)}, u32[]{:S(2)}) collective-permute-start(bf16[104,768]{1,0:T(8,128)(2,1)S(1)} %get-tuple-element.205), channel_id=1, source_target_pairs={{0,16},{8,24},{16,0},{24,8},{1,17},{9,25},{17,1},{25,9},{2,18},{10... | collective-permute-start | bytes 479240 | tf_op jit(solution)/shard_map/ppermute | solution.py:1119
  174.8 20.7 %collective-permute-start.32 = (bf16[2,48,3072]{2,1,0:T(8,128)(2,1)S(1)}, bf16[2,48,3072]{2,1,0:T(8,128)(2,1)S(1)}, u32[]{:S(2)}, u32[]{:S(2)}) collective-permute-start(bf16[2,48,3072]{2,1,0:T(8,128)(2,1)S(1)} %get-tuple-element.216), channel_id=1, source_target_pairs={{0,2},{1,3},{2,0},{3,1},{4,6},{5,7},{6,4},{7,5},{8,10},{9,11},{10,... | collective-permute-start | bytes 1769480 | tf_op jit(solution)/shard_map/ppermute | solution.py:1115
  176.4 19.1 %collective-permute-start.26 = (bf16[2,48,3072]{2,1,0:T(8,128)(2,1)S(1)}, bf16[2,48,3072]{2,1,0:T(8,128)(2,1)S(1)}, u32[]{:S(2)}, u32[]{:S(2)}) collective-permute-start(bf16[2,48,3072]{2,1,0:T(8,128)(2,1)S(1)} %get-tuple-element.214), channel_id=1, source_target_pairs={{0,4},{1,5},{2,6},{3,7},{4,0},{5,1},{6,2},{7,3},{8,12},{9,13},{10,... | collective-permute-start | bytes 1769480 | tf_op jit(solution)/shard_map/ppermute | solution.py:1115
  180.3 15.2 %collective-permute-start.30 = (bf16[104,768]{1,0:T(8,128)(2,1)S(1)}, bf16[104,768]{1,0:T(8,128)(2,1)S(1)}, u32[]{:S(2)}, u32[]{:S(2)}) collective-permute-start(bf16[104,768]{1,0:T(8,128)(2,1)S(1)} %get-tuple-element.229), channel_id=1, source_target_pairs={{0,16},{8,24},{16,0},{24,8},{1,17},{9,25},{17,1},{25,9},{2,18},{10... | collective-permute-start | bytes 479240 | tf_op jit(solution)/shard_map/ppermute | solution.py:1119
  195.8 34.4 %collective-permute-start.33 = (bf16[4,96,2304]{2,1,0:T(8,128)(2,1)S(1)}, bf16[4,96,2304]{2,1,0:T(8,128)(2,1)S(1)}, u32[]{:S(2)}, u32[]{:S(2)}) collective-permute-start(bf16[4,96,2304]{2,1,0:T(8,128)(2,1)S(1)} %get-tuple-element.241), channel_id=1, source_target_pairs={{0,1},{1,0},{2,3},{3,2},{4,5},{5,4},{6,7},{7,6},{8,9},{9,8},{10,11... | collective-permute-start | bytes 5308424 | tf_op jit(solution)/shard_map/ppermute | solution.py:1115
  196.0 15.5 %collective-permute-start.35 = (bf16[1,96,3072]{2,1,0:T(8,128)(2,1)S(1)}, bf16[1,96,3072]{2,1,0:T(8,128)(2,1)S(1)}, u32[]{:S(2)}, u32[]{:S(2)}) collective-permute-start(bf16[1,96,3072]{2,1,0:T(8,128)(2,1)S(1)} %get-tuple-element.234.one), channel_id=1, source_target_pairs={{0,8},{24,16},{1,9},{25,17},{2,10},{26,18},{3,11},{27,19},{4,12},{... | collective-permute-start | bytes 1769480 | tf_op jit(solution)/shard_map/ppermute | solution.py:1115
  197.9 20.0 %collective-permute-start.34 = (bf16[104,3840]{1,0:T(8,128)(2,1)S(1)}, bf16[104,3840]{1,0:T(8,128)(2,1)S(1)}, u32[]{:S(2)}, u32[]{:S(2)}) collective-permute-start(bf16[104,3840]{1,0:T(8,128)(2,1)S(1)} %get-tuple-element.224), channel_id=1, source_target_pairs={{0,2},{1,3},{2,0},{3,1},{4,6},{5,7},{6,4},{7,5},{8,10},{9,11},{10,... | collective-permute-start | bytes 2396168 | tf_op jit(solution)/shard_map/ppermute | solution.py:1115
  199.0 18.3 %collective-permute-start.36 = (bf16[96,3840]{1,0:T(8,128)(2,1)S(1)}, bf16[96,3840]{1,0:T(8,128)(2,1)S(1)}, u32[]{:S(2)}, u32[]{:S(2)}) collective-permute-start(bf16[96,3840]{1,0:T(8,128)(2,1)S(1)} %get-tuple-element.225), channel_id=1, source_target_pairs={{0,4},{1,5},{2,6},{3,7},{4,0},{5,1},{6,2},{7,3},{8,12},{9,13},{10,... | collective-permute-start | bytes 2211848 | tf_op jit(solution)/shard_map/ppermute | solution.py:1115
  200.0 23.7 %collective-permute-start.39 = (bf16[1,96,3072]{2,1,0:T(8,128)(2,1)S(1)}, bf16[1,96,3072]{2,1,0:T(8,128)(2,1)S(1)}, u32[]{:S(2)}, u32[]{:S(2)}) collective-permute-start(bf16[1,96,3072]{2,1,0:T(8,128)(2,1)S(1)} %get-tuple-element.235.one), channel_id=1, source_target_pairs={{0,8},{24,16},{1,9},{25,17},{2,10},{26,18},{3,11},{27,19},{4,12},{... | collective-permute-start | bytes 1769480 | tf_op jit(solution)/shard_map/ppermute | solution.py:1115
  211.6 12.9 %collective-permute-start.38 = (bf16[1,96,3072]{2,1,0:T(8,128)(2,1)S(1)}, bf16[1,96,3072]{2,1,0:T(8,128)(2,1)S(1)}, u32[]{:S(2)}, u32[]{:S(2)}) collective-permute-start(bf16[1,96,3072]{2,1,0:T(8,128)(2,1)S(1)} %chain_two.2.one), channel_id=1, source_target_pairs={{8,16},{16,8},{9,17},{17,9},{10,18},{18,10},{11,19},{19,11},{12,20... | collective-permute-start | bytes 1769480 | tf_op jit(solution)/shard_map/ppermute | solution.py:1115
  224.8 21.5 %collective-permute-start.43 = (bf16[1,96,3072]{2,1,0:T(8,128)(2,1)S(1)}, bf16[1,96,3072]{2,1,0:T(8,128)(2,1)S(1)}, u32[]{:S(2)}, u32[]{:S(2)}) collective-permute-start(bf16[1,96,3072]{2,1,0:T(8,128)(2,1)S(1)} %chain_three.2.refs_0_), channel_id=1, source_target_pairs={{8,0},{16,24},{9,1},{17,25},{10,2},{18,26},{11,3},{19,27},{12,4},{... | collective-permute-start | bytes 1769480 | tf_op jit(solution)/shard_map/ppermute | solution.py:1115
  230.7 17.2 %collective-permute-start.44 = (bf16[2,48,2304]{2,1,0:T(8,128)(2,1)S(1)}, bf16[2,48,2304]{2,1,0:T(8,128)(2,1)S(1)}, u32[]{:S(2)}, u32[]{:S(2)}) collective-permute-start(bf16[2,48,2304]{2,1,0:T(8,128)(2,1)S(1)} %get-tuple-element.259), channel_id=1, source_target_pairs={{0,4},{1,5},{2,6},{3,7},{4,0},{5,1},{6,2},{7,3},{8,12},{9,13},{10,... | collective-permute-start | bytes 1327112 | tf_op jit(solution)/shard_map/ppermute | solution.py:1115
  232.3 15.6 %collective-permute-start.41 = (bf16[2,48,2304]{2,1,0:T(8,128)(2,1)S(1)}, bf16[2,48,2304]{2,1,0:T(8,128)(2,1)S(1)}, u32[]{:S(2)}, u32[]{:S(2)}) collective-permute-start(bf16[2,48,2304]{2,1,0:T(8,128)(2,1)S(1)} %get-tuple-element.258), channel_id=1, source_target_pairs={{0,2},{1,3},{2,0},{3,1},{4,6},{5,7},{6,4},{7,5},{8,10},{9,11},{10,... | collective-permute-start | bytes 1327112 | tf_op jit(solution)/shard_map/ppermute | solution.py:1115
  232.8 22.6 %collective-permute-start.46 = (bf16[56,3840]{1,0:T(8,128)(2,1)S(1)}, bf16[56,3840]{1,0:T(8,128)(2,1)S(1)}, u32[]{:S(2)}, u32[]{:S(2)}) collective-permute-start(bf16[56,3840]{1,0:T(8,128)(2,1)S(1)} %get-tuple-element.255), channel_id=1, source_target_pairs={{0,8},{8,0},{16,24},{24,16},{1,9},{9,1},{17,25},{25,17},{2,10},{10... | collective-permute-start | bytes 1290248 | tf_op jit(solution)/shard_map/ppermute | solution.py:1115
  250.2 33.3 %collective-permute-start.51 = (bf16[1,96,3072]{2,1,0:T(8,128)(2,1)S(1)}, bf16[1,96,3072]{2,1,0:T(8,128)(2,1)S(1)}, u32[]{:S(2)}, u32[]{:S(2)}) collective-permute-start(bf16[1,96,3072]{2,1,0:T(8,128)(2,1)S(1)} %chain_three.3.refs_0_), channel_id=1, source_target_pairs={{8,0},{16,24},{9,1},{17,25},{10,2},{18,26},{11,3},{19,27},{12,4},{... | collective-permute-start | bytes 1769480 | tf_op jit(solution)/shard_map/ppermute | solution.py:1115
  255.6 25.3 %collective-permute-start.50 = (bf16[56,3840]{1,0:T(8,128)(2,1)S(1)}, bf16[56,3840]{1,0:T(8,128)(2,1)S(1)}, u32[]{:S(2)}, u32[]{:S(2)}) collective-permute-start(bf16[56,3840]{1,0:T(8,128)(2,1)S(1)} %get-tuple-element.270.pair), channel_id=1, source_target_pairs={{0,16},{8,24},{16,0},{24,8},{1,17},{9,25},{17,1},{25,9},{2,18},{10... | collective-permute-start | bytes 1290248 | tf_op jit(solution)/shard_map/ppermute | solution.py:1115
  257.0 23.1 %collective-permute-start.48 = (bf16[1,48,2304]{2,1,0:T(8,128)(2,1)S(1)}, bf16[1,48,2304]{2,1,0:T(8,128)(2,1)S(1)}, u32[]{:S(2)}, u32[]{:S(2)}) collective-permute-start(bf16[1,48,2304]{2,1,0:T(8,128)(2,1)S(1)} %get-tuple-element.274), channel_id=1, source_target_pairs={{0,8},{8,0},{16,24},{24,16},{1,9},{9,1},{17,25},{25,17},{2,10},{10... | collective-permute-start | bytes 663560 | tf_op jit(solution)/shard_map/ppermute | solution.py:1115
  281.0 15.1 %collective-permute-start.53 = (bf16[1,48,3840]{2,1,0:T(8,128)(2,1)S(1)}, bf16[1,48,3840]{2,1,0:T(8,128)(2,1)S(1)}, u32[]{:S(2)}, u32[]{:S(2)}) collective-permute-start(bf16[1,48,3840]{2,1,0:T(8,128)(2,1)S(1)} %get-tuple-element.278.full), channel_id=1, source_target_pairs={{0,8},{8,0},{16,24},{24,16},{1,9},{9,1},{17,25},{25,17},{2,10},{10... | collective-permute-start | bytes 1105928 | tf_op jit(solution)/shard_map/ppermute | solution.py:1115
  (37 other events, 387.5 us)

commit v4 on v3

--- a/solution.py
+++ b/solution.py
@@ -584,13 +584,16 @@
     second[:, 3 * D :] = leave[HALF:]
 
 
-def arrange_tokens(where, video, cotangent, tokens, cot, *pieces):
-    for source, target in ((video, tokens), (cotangent, cot)):
-        for f in range(2):
-            target[f * FRAME_ROWS : f * FRAME_ROWS + PLACES, :] = source[0, f]
-            target[f * FRAME_ROWS + PLACES : (f + 1) * FRAME_ROWS, :] = jnp.zeros(
-                (FRAME_ROWS - PLACES, D), BF
-            )
+def pad_frames(source, target):
+    for f in range(2):
+        target[f * FRAME_ROWS : f * FRAME_ROWS + PLACES, :] = source[0, f]
+        target[f * FRAME_ROWS + PLACES : (f + 1) * FRAME_ROWS, :] = jnp.zeros(
+            (FRAME_ROWS - PLACES, D), BF
+        )
+
+
+def arrange_tokens(where, video, tokens, *pieces):
+    pad_frames(video, tokens)
     split_pieces(nn(piece_from_frame(where[1]), tokens[...]).astype(BF), pieces)
 
 
@@ -763,11 +766,11 @@
         grad_hidden = (nt(cot[...], w_out[rows, :]) * slope).astype(BF)
         grad_normed[...] += nt(grad_hidden, w_in[:, at])
         small[pl.ds(9 + chip, 1), :] = jnp.sum(grad_hidden.astype(F32), axis=0, keepdims=True)
-        shuffle[...] = tn(active, cot[...])
+        shuffle[...] = tn(active, cot[...]).astype(BF)
         for kind, ref in ((parity, keep_wc), (1 - parity, send_wc)):
             for c in range(4):
-                part = shuffle[pl.ds(pl.multiple_of(kind * 384 + c * SHARD, 32), SHARD), :]
-                ref[p, :, c * D : (c + 1) * D] = part.astype(BF)
+                rows = pl.ds(pl.multiple_of(kind * 384 + c * SHARD, 32), SHARD)
+                ref[p, :, c * D : (c + 1) * D] = shuffle[rows, :]
         moved = tn(normed_own[...], grad_hidden).astype(BF)
         for j in range(4):
             keep_we[j, :, at] = moved[2 * j * SHARD : (2 * j + 1) * SHARD]
@@ -894,13 +897,13 @@
 
         @pl.when((step >= first) & (step < first + count))
         def _(i=i):
-            shuffle[...] = tn(pairs[2 * i][...], pairs[2 * i + 1][...])
+            shuffle[...] = tn(pairs[2 * i][...], pairs[2 * i + 1][...]).astype(BF)
 
         first += count
     for j in range(4):
         for parity, ref in ((0, keep), (1, send)):
-            rows = pl.ds(pl.multiple_of((own ^ (2 * j + parity)) * SHARD, 8), SHARD)
-            ref[j] = shuffle[rows, :].astype(BF)
+            rows = pl.ds(pl.multiple_of((own ^ (2 * j + parity)) * SHARD, 32), SHARD)
+            ref[j] = shuffle[rows, :]
 
 
 def by_columns(width, step):
@@ -1236,8 +1239,7 @@
 
 
 class ReductionBoth(Reduction):
-    def __init__(self, where, keep, send, small):
-        super().__init__(where, [keep], [send])
+    def join(self, small):
         self.small, self.small_got = small, swap(small, CORE)
 
     def flat(self, rows, dtype=BF):
@@ -1346,13 +1348,12 @@
     )
     x1, y1 = swap(g1a, ACROSS), swap(g1b, UP)
 
-    tokens, cot, *video_pieces = whole_call(
+    tokens, *video_pieces = whole_call(
         arrange_tokens,
         "arrange_tokens",
-        [shape(ROWS, D), shape(ROWS, D)] + [shape(PIECE, D)] * 4,
+        [shape(ROWS, D)] + [shape(PIECE, D)] * 4,
         where,
         after(video, g1a),
-        cotangent,
         scalars=1,
     )
     video_pieces = shift(video_pieces)
@@ -1364,6 +1365,7 @@
     to_x = rows(g1b, y1, plane[:HALF])
     r2y, r2x = swap(to_y, UP), swap(to_x, ACROSS)
     c1 = swap(rows(g1a, g1b, x1, y1, r2y[:112], r2x[:96]), CORE)
+    cot = whole_call(pad_frames, "arrange_cotangent", shape(ROWS, D), after(cotangent, r2y))
     to_y = after(rows(plane[:HALF], r2x[96:], contract), *video_pieces[1:])
     to_x = after(rows(plane[HALF:], r2y[112:], expand_weight), *video_pieces[1:])
     r3y, r3x = swap(to_y, UP), swap(to_x, ACROSS)
@@ -1441,7 +1443,7 @@
         ],
         compiler_params=limit(24),
         cost_estimate=NO_COST,
-    )(after(tokens, to_y, to_x), params, exit_full, *places, plane, r2y, r2x, r3y, r3x, c2)
+    )(after(tokens, to_y, to_x, cot), params, exit_full, *places, plane, r2y, r2x, r3y, r3x, c2)
 
     c3 = swap(after(rows(expand_weight, contract, r3x[96:], r3y[96:]), normed_three), CORE)
     c4, c5 = swap(r4y, CORE), swap(r4x, CORE)
@@ -1466,7 +1468,7 @@
             pltpu.VMEM((ROWS, D), BF),
             pltpu.VMEM((ROWS, D), F32),
             pltpu.VMEM((ROWS, D), F32),
-            pltpu.VMEM((D, D), F32),
+            pltpu.VMEM((D, D), BF),
             pltpu.SemaphoreType.DMA((40,)),
         ],
         compiler_params=limit(28),
@@ -1524,7 +1526,7 @@
                 grid=(first,),
                 in_specs=specs,
                 out_specs=[pl.BlockSpec((4, SHARD, D), lambda i, w: (0, 0, i))] * 2,
-                scratch_shapes=[pltpu.VMEM((D, D), F32)],
+                scratch_shapes=[pltpu.VMEM((D, D), BF)],
             ),
             compiler_params=limit(16),
             cost_estimate=NO_COST,
@@ -1547,7 +1549,8 @@
     )(*video_pieces, after(grad_pieces[0], output), *grad_pieces[1:], packed_place, small, entry_full)
 
     placed = forward_sum.plane_two(small)
-    space_sum = ReductionBoth(where, keep_space, after(send_space, *placed), after(small, *placed))
+    space_sum = ReductionBoth(where, [keep_space], [after(send_space, *placed)])
+    space_sum.join(after(small, *placed))
     normed_back = shift([after(v, *placed) for v in normed_back])
     keep_time, send_time = grads((after(normed_place, *placed), grad_place))
     placed = space_sum.plane_one(send_time)

time: 301 us -> 300 us (level)
    pallas_call x24 -> x25, Pallas kernels: 20.2 us -> 20.2 us  [whole_call(): pl.pallas_call(functools.partial(kernel, **options), name=name, out_shape...]
  transfers between devices with their start and end apart: 54 -> 54, of which waited for: 26 -> 26; matrix products, arithmetic and copies ran while one was open for 3% -> 2% of each run, Pallas kernels for 24% -> 24%
where the time goes in v4:
time: 300 us
  waiting for transfers between devices  127 us (42%)
  Pallas kernels  99 us (33%)
  starting transfers between devices  63.8 us (21%)
  local copies, waits for them, and re-layouts  7.64 us (3%)
    ppermute x42, waiting for transfers between devices, swap(): return lax.ppermute(value, axis, pairs)  114 us
    ppermute x42, starting transfers between devices, swap(): return lax.ppermute(value, axis, pairs)  41.3 us
    ppermute x12, starting transfers between devices, shift(): lax.ppermute(pieces[k], 'frame', [(i, i ^ k) for i in range(4)])  22.5 us
    pallas_call x1, Pallas kernels, body(): pl.pallas_call(feed_forward, name='feed_forward', out_shape=[shape(*video...  20.8 us
    pallas_call x25, Pallas kernels, whole_call(): pl.pallas_call(functools.partial(kernel, **options), name=name, out_shape...  20.2 us
    pallas_call x1, Pallas kernels, body(): pl.pallas_call(temporal_back, name='temporal_back', out_shape=[shape(SPOT...  13.6 us
    ppermute x12, waiting for transfers between devices, shift(): lax.ppermute(pieces[k], 'frame', [(i, i ^ k) for i in range(4)])  13 us
    pallas_call x1, Pallas kernels, body(): pl.pallas_call(spatial_forward, name='spatial_forward', out_shape=[shape(...  12.5 us
  transfers between devices with their start and end apart: 54, of which 26 were waited for; matrix products, arithmetic and copies ran while one was open for 2% of the time, Pallas kernels for 24%

profile of v4, /device:TPU:0, one launch (start us, length us, event | category | flops | bytes accessed | tf_op | source)
XLA Modules:
  0.0 299.7 jit_solution(6349127550617294219)
XLA Ops:
  3.4 3.0 %collective-permute-start = (bf16[56,3072]{1,0:T(8,128)(2,1)S(1)}, bf16[56,3072]{1,0:T(8,128)(2,1)S(1)}, u32[]{:S(2)}, u32[]{:S(2)}) collective-permute-start(bf16[56,3072]{1,0:T(8,128)(2,1)S(1)} %get-tuple-element.149.refs_4_), channel_id=1, source_target_pairs={{0,2},{1,3},{2,0},{3,1},{4,6},{5,7},{6,4},{7,5},{8,10},{9,11},{10,... | collective-permute-start | bytes 1032200 | tf_op jit(solution)/shard_map/ppermute | solution.py:1118
  11.9 2.6 collective-permute-start.4
  18.6 20.0 %collective-permute-done.2.refs_8_ = bf16[160,3072]{1,0:T(8,128)(2,1)S(1)} collective-permute-done((bf16[160,3072]{1,0:T(8,128)(2,1)S(1)}, bf16[160,3072]{1,0:T(8,128)(2,1)S(1)}, u32[]{:S(2)}, u32[]{:S(2)}) %collective-permute-start.2) | collective-permute-done | bytes 983072 | tf_op jit(solution)/shard_map/ppermute | solution.py:1118
  41.3 2.3 collective-permute-done.8.refs_10_
  43.6 10.2 %temporal_forward.1 = (bf16[104,768]{1,0:T(8,128)(2,1)S(1)}, bf16[104,768]{1,0:T(8,128)(2,1)S(1)}, bf16[104,768]{1,0:T(8,128)(2,1)S(1)}, bf16[104,768]{1,0:T(8,1...) custom-call(bf16[104,768]{1,0:T(8,128)(2,1)S(1)} %get-tuple-element., ...), custom_call_target="tpu_custom_call" | custom-call | flops 1000 | bytes 1000 | tf_op jit(solution)/shard_map/temporal_forward/pallas_call | solution.py:1373
  53.8 2.7 collective-permute-start.10
  58.1 9.4 %collective-permute-done.6.refs_11_.refs_2_ = bf16[192,3072]{1,0:T(8,128)(2,1)S(1)} collective-permute-done((bf16[192,3072]{1,0:T(8,128)(2,1)S(1)}, bf16[192,3072]{1,0:T(8,128)(2,1)S(1)}, u32[]{:S(2)}, u32[]{:S(2)}) %collective-permute-start.6) | collective-permute-done | bytes 1179680 | tf_op jit(solution)/shard_map/ppermute | solution.py:1118
  74.0 12.5 %spatial_forward.1 = (f32[416,768]{1,0:T(8,128)S(1)}, bf16[416,768]{1,0:T(8,128)(2,1)S(1)}, bf16[768,2304]{1,0:T(8,128)(2,1)}, bf16[768,768]{1,0:T(8,128)(2,1)},...) custom-call(bf16[416,768]{1,0:T(8,128)(2,1)S(1)} %get-tuple-element., ...), custom_call_target="tpu_custom_call" | custom-call | flops 1000 | bytes 1000 | tf_op jit(solution)/shard_map/spatial_forward/pallas_call | solution.py:1417
  86.7 11.4 %collective-permute-done.15.refs_5_ = bf16[192,3072]{1,0:T(8,128)(2,1)S(1)} collective-permute-done((bf16[192,3072]{1,0:T(8,128)(2,1)S(1)}, bf16[192,3072]{1,0:T(8,128)(2,1)S(1)}, u32[]{:S(2)}, u32[]{:S(2)}) %collective-permute-start.15) | collective-permute-done | bytes 1179680 | tf_op jit(solution)/shard_map/ppermute | solution.py:1118
  98.6 2.3 collective-permute-done.18.refs_8_
  102.6 20.8 %feed_forward.1 = (bf16[1,2,196,768]{3,2,1,0:T(8,128)(2,1)S(1)}, f32[416,768]{1,0:T(8,128)S(1)}, bf16[416,768]{1,0:T(8,128)(2,1)S(1)}, bf16[4,96,3072]{2,1,0:T(8...) custom-call(s32[2]{0:T(128)S(1)} %pad_add_fusion.where, ...), custom_call_target="tpu_custom_call" | custom-call | flops 1000 | bytes 1000 | tf_op jit(solution)/shard_map/feed_forward/pallas_call | solution.py:1450
  124.0 9.9 %spatial_back.1.refs_0_.refs_3_ = bf16[416,2304]{1,0:T(8,128)(2,1)S(1)} custom-call(bf16[416,768]{1,0:T(8,128)(2,1)S(1)} %get-tuple-element.180.branch.refs_1_.refs_5_, bf16[416,2304]{1,0:T(8,128)(2,1)S(1)} %copy-done.4, bf16[768,768]{1,0:T(8,128)(2,1)S(1)} %copy-done.7), custom_call_target="tpu_custom_call" | custom-call | flops 1000 | bytes 1000 | tf_op jit(solution)/shard_map/spatial_back/pallas_call | solution.py:1482
  137.3 4.5 %spatial_back_norm.1 = (f32[416,768]{1,0:T(8,128)S(1)}, bf16[416,768]{1,0:T(8,128)(2,1)S(1)}, f32[16,768]{1,0:T(8,128)S(1)}, bf16[104,768]{1,0:T(8,128)(2,1)S(1)...) custom-call(s32[2]{0:T(128)S(1)} %pad_add_fusion.where, ...), custom_call_target="tpu_custom_call" | custom-call | flops 1000 | bytes 1000 | tf_op jit(solution)/shard_map/spatial_back_norm/pallas_call | solution.py:1098
  141.8 3.2 %collective-permute-start.22 = (bf16[104,768]{1,0:T(8,128)(2,1)S(1)}, bf16[104,768]{1,0:T(8,128)(2,1)S(1)}, u32[]{:S(2)}, u32[]{:S(2)}) collective-permute-start(bf16[104,768]{1,0:T(8,128)(2,1)S(1)} %get-tuple-element.204), channel_id=1, source_target_pairs={{0,8},{8,0},{16,24},{24,16},{1,9},{9,1},{17,25},{25,17},{2,10},{10... | collective-permute-start | bytes 479240 | tf_op jit(solution)/shard_map/ppermute | solution.py:1122
  148.4 6.1 %weight_grads.2 = (bf16[4,96,3840]{2,1,0:T(8,128)(2,1)S(1)}, bf16[4,96,3840]{2,1,0:T(8,128)(2,1)S(1)}) custom-call(s32[2]{0:T(128)S(1)} %pad_add_fusion.where, bf16[416,768]{1,0:T(8,128)(2,1)S(1)} %copy-done.8, bf16[416,768]{1,0:T(8,128)(2,1)S(1)} %get-tuple-element.196.refs_1_, bf16[416,768]{1,0:T(8,128)(2,1)S(1)} %copy-done.9, ...), custom_call_target="tpu_custom_call" | custom-call | flops 1000 | bytes 1000 | tf_op jit(solution)/shard_map/weight_grads/pallas_call | solution.py:1520
  154.5 4.9 %collective-permute-done.23.refs_6_ = bf16[104,768]{1,0:T(8,128)(2,1)S(1)} collective-permute-done((bf16[104,768]{1,0:T(8,128)(2,1)S(1)}, bf16[104,768]{1,0:T(8,128)(2,1)S(1)}, u32[]{:S(2)}, u32[]{:S(2)}) %collective-permute-start.23) | collective-permute-done | bytes 159776 | tf_op jit(solution)/shard_map/ppermute | solution.py:1122
  159.5 13.6 %temporal_back.1 = (bf16[400,2304]{1,0:T(8,128)(2,1)S(1)}, f32[16,768]{1,0:T(8,128)S(1)}, bf16[104,768]{1,0:T(8,128)(2,1)S(1)}, bf16[104,768]{1,0:T(8,128)(2,1)S...) custom-call(bf16[104,768]{1,0:T(8,128)(2,1)S(1)} %get-tuple-element.163.refs_0_, ...), custom_call_target="tpu_custom_call" | custom-call | flops 1000 | bytes 1000 | tf_op jit(solution)/shard_map/temporal_back/pallas_call | solution.py:1540
  175.8 2.8 collective-permute-start.31
  179.2 4.4 %collective-permute-start.30 = (bf16[104,768]{1,0:T(8,128)(2,1)S(1)}, bf16[104,768]{1,0:T(8,128)(2,1)S(1)}, u32[]{:S(2)}, u32[]{:S(2)}) collective-permute-start(bf16[104,768]{1,0:T(8,128)(2,1)S(1)} %get-tuple-element.229), channel_id=1, source_target_pairs={{0,16},{8,24},{16,0},{24,8},{1,17},{9,25},{17,1},{25,9},{2,18},{10... | collective-permute-start | bytes 479240 | tf_op jit(solution)/shard_map/ppermute | solution.py:1122
  183.6 3.7 %weight_grads.3 = (bf16[4,96,2304]{2,1,0:T(8,128)(2,1)S(1)}, bf16[4,96,2304]{2,1,0:T(8,128)(2,1)S(1)}) custom-call(s32[2]{0:T(128)S(1)} %pad_add_fusion.where, bf16[400,768]{1,0:T(8,128)(2,1)S(1)} %copy-done.11, bf16[400,2304]{1,0:T(8,128)(2,1)S(1)} %get-tuple-element.220.refs_1_), custom_call_target="tpu_custom_call" | custom-call | flops 1000 | bytes 1000 | tf_op jit(solution)/shard_map/weight_grads/pallas_call | solution.py:1520
  188.1 6.3 %collective-permute-done.30.refs_2_ = bf16[104,768]{1,0:T(8,128)(2,1)S(1)} collective-permute-done((bf16[104,768]{1,0:T(8,128)(2,1)S(1)}, bf16[104,768]{1,0:T(8,128)(2,1)S(1)}, u32[]{:S(2)}, u32[]{:S(2)}) %collective-permute-start.30) | collective-permute-done | bytes 159776 | tf_op jit(solution)/shard_map/ppermute | solution.py:1122
  201.7 8.6 %collective-permute-done.35.two = bf16[1,96,3072]{2,1,0:T(8,128)(2,1)S(1)} collective-permute-done((bf16[1,96,3072]{2,1,0:T(8,128)(2,1)S(1)}, bf16[1,96,3072]{2,1,0:T(8,128)(2,1)S(1)}, u32[]{:S(2)}, u32[]{:S(2)}) %collective-permute-start.35) | collective-permute-done | bytes 589856 | tf_op jit(solution)/shard_map/ppermute | solution.py:1118
  211.2 4.9 %collective-permute-done.36.from_y = bf16[96,3840]{1,0:T(8,128)(2,1)S(1)} collective-permute-done((bf16[96,3840]{1,0:T(8,128)(2,1)S(1)}, bf16[96,3840]{1,0:T(8,128)(2,1)S(1)}, u32[]{:S(2)}, u32[]{:S(2)}) %collective-permute-start.36) | collective-permute-done | bytes 737312 | tf_op jit(solution)/shard_map/ppermute | solution.py:1118
  219.1 3.4 %collective-permute-done.39.two = bf16[1,96,3072]{2,1,0:T(8,128)(2,1)S(1)} collective-permute-done((bf16[1,96,3072]{2,1,0:T(8,128)(2,1)S(1)}, bf16[1,96,3072]{2,1,0:T(8,128)(2,1)S(1)}, u32[]{:S(2)}, u32[]{:S(2)}) %collective-permute-start.39) | collective-permute-done | bytes 589856 | tf_op jit(solution)/shard_map/ppermute | solution.py:1118
  224.9 3.3 %collective-permute-done.40.got_x = bf16[48,3840]{1,0:T(8,128)(2,1)S(1)} collective-permute-done((bf16[48,3840]{1,0:T(8,128)(2,1)S(1)}, bf16[48,3840]{1,0:T(8,128)(2,1)S(1)}, u32[]{:S(2)}, u32[]{:S(2)}) %collective-permute-start.40) | collective-permute-done | bytes 368672 | tf_op jit(solution)/shard_map/ppermute | solution.py:1118
  231.6 2.6 collective-permute-start.46
  234.5 10.6 %collective-permute-done.43.refs_1_ = bf16[1,96,3072]{2,1,0:T(8,128)(2,1)S(1)} collective-permute-done((bf16[1,96,3072]{2,1,0:T(8,128)(2,1)S(1)}, bf16[1,96,3072]{2,1,0:T(8,128)(2,1)S(1)}, u32[]{:S(2)}, u32[]{:S(2)}) %collective-permute-start.43) | collective-permute-done | bytes 589856 | tf_op jit(solution)/shard_map/ppermute | solution.py:1118
  250.4 3.9 %collective-permute-done.46.near = bf16[56,3840]{1,0:T(8,128)(2,1)S(1)} collective-permute-done((bf16[56,3840]{1,0:T(8,128)(2,1)S(1)}, bf16[56,3840]{1,0:T(8,128)(2,1)S(1)}, u32[]{:S(2)}, u32[]{:S(2)}) %collective-permute-start.46) | collective-permute-done | bytes 430112 | tf_op jit(solution)/shard_map/ppermute | solution.py:1118
  255.9 2.6 collective-permute-start.48
  258.5 20.5 %collective-permute-done.48.two = bf16[1,48,2304]{2,1,0:T(8,128)(2,1)S(1)} collective-permute-done((bf16[1,48,2304]{2,1,0:T(8,128)(2,1)S(1)}, bf16[1,48,2304]{2,1,0:T(8,128)(2,1)S(1)}, u32[]{:S(2)}, u32[]{:S(2)}) %collective-permute-start.48) | collective-permute-done | bytes 221216 | tf_op jit(solution)/shard_map/ppermute | solution.py:1118
  279.8 2.5 collective-permute-start.53
  284.1 5.7 %collective-permute-done.49.two = bf16[1,48,2304]{2,1,0:T(8,128)(2,1)S(1)} collective-permute-done((bf16[1,48,2304]{2,1,0:T(8,128)(2,1)S(1)}, bf16[1,48,2304]{2,1,0:T(8,128)(2,1)S(1)}, u32[]{:S(2)}, u32[]{:S(2)}) %collective-permute-start.49) | collective-permute-done | bytes 221216 | tf_op jit(solution)/shard_map/ppermute | solution.py:1118
  (172 shorter events, 73.1 us)
Async XLA Ops:
  10.2 28.8 %collective-permute-start.3 = (bf16[104,768]{1,0:T(8,128)(2,1)S(1)}, bf16[104,768]{1,0:T(8,128)(2,1)S(1)}, u32[]{:S(2)}, u32[]{:S(2)}) collective-permute-start(bf16[104,768]{1,0:T(8,128)(2,1)S(1)} %get-tuple-element.155), channel_id=1, source_target_pairs={{0,8},{8,0},{16,24},{24,16},{1,9},{9,1},{17,25},{25,17},{2,10},{10... | collective-permute-start | bytes 479240 | tf_op jit(solution)/shard_map/ppermute | solution.py:1122
  11.9 27.1 %collective-permute-start.4 = (bf16[104,768]{1,0:T(8,128)(2,1)S(1)}, bf16[104,768]{1,0:T(8,128)(2,1)S(1)}, u32[]{:S(2)}, u32[]{:S(2)}) collective-permute-start(bf16[104,768]{1,0:T(8,128)(2,1)S(1)} %get-tuple-element.156), channel_id=1, source_target_pairs={{0,16},{8,24},{16,0},{24,8},{1,17},{9,25},{17,1},{25,9},{2,18},{10... | collective-permute-start | bytes 479240 | tf_op jit(solution)/shard_map/ppermute | solution.py:1122
  14.4 24.6 %collective-permute-start.5 = (bf16[104,768]{1,0:T(8,128)(2,1)S(1)}, bf16[104,768]{1,0:T(8,128)(2,1)S(1)}, u32[]{:S(2)}, u32[]{:S(2)}) collective-permute-start(bf16[104,768]{1,0:T(8,128)(2,1)S(1)} %get-tuple-element.157), channel_id=1, source_target_pairs={{0,24},{8,16},{16,8},{24,0},{1,25},{9,17},{17,9},{25,1},{2,26},{10... | collective-permute-start | bytes 479240 | tf_op jit(solution)/shard_map/ppermute | solution.py:1122
  16.2 22.4 %collective-permute-start.2 = (bf16[160,3072]{1,0:T(8,128)(2,1)S(1)}, bf16[160,3072]{1,0:T(8,128)(2,1)S(1)}, u32[]{:S(2)}, u32[]{:S(2)}) collective-permute-start(bf16[160,3072]{1,0:T(8,128)(2,1)S(1)} %pad_maximum_fusion.5), channel_id=1, source_target_pairs={{0,4},{1,5},{2,6},{3,7},{4,0},{5,1},{6,2},{7,3},{8,12},{9,13},{10,... | collective-permute-start | bytes 2949128 | tf_op jit(solution)/shard_map/ppermute | solution.py:1118
  17.9 20.8 %collective-permute-start.7 = (bf16[144,3072]{1,0:T(8,128)(2,1)S(1)}, bf16[144,3072]{1,0:T(8,128)(2,1)S(1)}, u32[]{:S(2)}, u32[]{:S(2)}) collective-permute-start(bf16[144,3072]{1,0:T(8,128)(2,1)S(1)} %pad_maximum_fusion.6), channel_id=1, source_target_pairs={{0,2},{1,3},{2,0},{3,1},{4,6},{5,7},{6,4},{7,5},{8,10},{9,11},{10,... | collective-permute-start | bytes 2654216 | tf_op jit(solution)/shard_map/ppermute | solution.py:1118
  39.0 28.4 %collective-permute-start.6 = (bf16[192,3072]{1,0:T(8,128)(2,1)S(1)}, bf16[192,3072]{1,0:T(8,128)(2,1)S(1)}, u32[]{:S(2)}, u32[]{:S(2)}) collective-permute-start(bf16[192,3072]{1,0:T(8,128)(2,1)S(1)} %pad_maximum_fusion.1), channel_id=1, source_target_pairs={{0,2},{1,3},{2,0},{3,1},{4,6},{5,7},{6,4},{7,5},{8,10},{9,11},{10,... | collective-permute-start | bytes 3538952 | tf_op jit(solution)/shard_map/ppermute | solution.py:1118
  39.8 29.4 %collective-permute-start.12 = (bf16[192,3072]{1,0:T(8,128)(2,1)S(1)}, bf16[192,3072]{1,0:T(8,128)(2,1)S(1)}, u32[]{:S(2)}, u32[]{:S(2)}) collective-permute-start(bf16[192,3072]{1,0:T(8,128)(2,1)S(1)} %pad_maximum_fusion.2), channel_id=1, source_target_pairs={{0,4},{1,5},{2,6},{3,7},{4,0},{5,1},{6,2},{7,3},{8,12},{9,13},{10,... | collective-permute-start | bytes 3538952 | tf_op jit(solution)/shard_map/ppermute | solution.py:1118
  53.8 14.8 %collective-permute-start.10 = (bf16[104,768]{1,0:T(8,128)(2,1)S(1)}, bf16[104,768]{1,0:T(8,128)(2,1)S(1)}, u32[]{:S(2)}, u32[]{:S(2)}) collective-permute-start(bf16[104,768]{1,0:T(8,128)(2,1)S(1)} %get-tuple-element.165), channel_id=1, source_target_pairs={{0,16},{8,24},{16,0},{24,8},{1,17},{9,25},{17,1},{25,9},{2,18},{10... | collective-permute-start | bytes 479240 | tf_op jit(solution)/shard_map/ppermute | solution.py:1122
  70.5 27.6 %collective-permute-start.15 = (bf16[192,3072]{1,0:T(8,128)(2,1)S(1)}, bf16[192,3072]{1,0:T(8,128)(2,1)S(1)}, u32[]{:S(2)}, u32[]{:S(2)}) collective-permute-start(bf16[192,3072]{1,0:T(8,128)(2,1)S(1)} %pad_maximum_fusion.4), channel_id=1, source_target_pairs={{0,2},{1,3},{2,0},{3,1},{4,6},{5,7},{6,4},{7,5},{8,10},{9,11},{10,... | collective-permute-start | bytes 3538952 | tf_op jit(solution)/shard_map/ppermute | solution.py:1118
  71.2 27.3 %collective-permute-start.14 = (bf16[192,3072]{1,0:T(8,128)(2,1)S(1)}, bf16[192,3072]{1,0:T(8,128)(2,1)S(1)}, u32[]{:S(2)}, u32[]{:S(2)}) collective-permute-start(bf16[192,3072]{1,0:T(8,128)(2,1)S(1)} %pad_maximum_fusion.3), channel_id=1, source_target_pairs={{0,4},{1,5},{2,6},{3,7},{4,0},{5,1},{6,2},{7,3},{8,12},{9,13},{10,... | collective-permute-start | bytes 3538952 | tf_op jit(solution)/shard_map/ppermute | solution.py:1118
  86.5 16.1 %collective-permute-start.16 = (bf16[384,3072]{1,0:T(8,128)(2,1)S(1)}, bf16[384,3072]{1,0:T(8,128)(2,1)S(1)}, u32[]{:S(2)}, u32[]{:S(2)}) collective-permute-start(bf16[384,3072]{1,0:T(8,128)(2,1)S(1)} %pad_maximum_fusion), channel_id=1, source_target_pairs={{0,1},{1,0},{2,3},{3,2},{4,5},{5,4},{6,7},{7,6},{8,9},{9,8},{10,11... | collective-permute-start | bytes 7077896 | tf_op jit(solution)/shard_map/ppermute | solution.py:1118
  135.2 37.9 %collective-permute-start.25 = (bf16[4,48,3072]{2,1,0:T(8,128)(2,1)S(1)}, bf16[4,48,3072]{2,1,0:T(8,128)(2,1)S(1)}, u32[]{:S(2)}, u32[]{:S(2)}) collective-permute-start(bf16[4,48,3072]{2,1,0:T(8,128)(2,1)S(1)} %get-tuple-element.193), channel_id=1, source_target_pairs={{0,4},{1,5},{2,6},{3,7},{4,0},{5,1},{6,2},{7,3},{8,12},{9,13},{10,... | collective-permute-start | bytes 3538952 | tf_op jit(solution)/shard_map/ppermute | solution.py:1118
  136.7 36.3 %collective-permute-start.21 = (bf16[4,48,3072]{2,1,0:T(8,128)(2,1)S(1)}, bf16[4,48,3072]{2,1,0:T(8,128)(2,1)S(1)}, u32[]{:S(2)}, u32[]{:S(2)}) collective-permute-start(bf16[4,48,3072]{2,1,0:T(8,128)(2,1)S(1)} %get-tuple-element.192), channel_id=1, source_target_pairs={{0,2},{1,3},{2,0},{3,1},{4,6},{5,7},{6,4},{7,5},{8,10},{9,11},{10,... | collective-permute-start | bytes 3538952 | tf_op jit(solution)/shard_map/ppermute | solution.py:1118
  141.8 12.7 %collective-permute-start.22 = (bf16[104,768]{1,0:T(8,128)(2,1)S(1)}, bf16[104,768]{1,0:T(8,128)(2,1)S(1)}, u32[]{:S(2)}, u32[]{:S(2)}) collective-permute-start(bf16[104,768]{1,0:T(8,128)(2,1)S(1)} %get-tuple-element.204), channel_id=1, source_target_pairs={{0,8},{8,0},{16,24},{24,16},{1,9},{9,1},{17,25},{25,17},{2,10},{10... | collective-permute-start | bytes 479240 | tf_op jit(solution)/shard_map/ppermute | solution.py:1122
  145.0 14.5 %collective-permute-start.23 = (bf16[104,768]{1,0:T(8,128)(2,1)S(1)}, bf16[104,768]{1,0:T(8,128)(2,1)S(1)}, u32[]{:S(2)}, u32[]{:S(2)}) collective-permute-start(bf16[104,768]{1,0:T(8,128)(2,1)S(1)} %get-tuple-element.205), channel_id=1, source_target_pairs={{0,16},{8,24},{16,0},{24,8},{1,17},{9,25},{17,1},{25,9},{2,18},{10... | collective-permute-start | bytes 479240 | tf_op jit(solution)/shard_map/ppermute | solution.py:1122
  173.7 20.6 %collective-permute-start.32 = (bf16[2,48,3072]{2,1,0:T(8,128)(2,1)S(1)}, bf16[2,48,3072]{2,1,0:T(8,128)(2,1)S(1)}, u32[]{:S(2)}, u32[]{:S(2)}) collective-permute-start(bf16[2,48,3072]{2,1,0:T(8,128)(2,1)S(1)} %get-tuple-element.216), channel_id=1, source_target_pairs={{0,2},{1,3},{2,0},{3,1},{4,6},{5,7},{6,4},{7,5},{8,10},{9,11},{10,... | collective-permute-start | bytes 1769480 | tf_op jit(solution)/shard_map/ppermute | solution.py:1118
  175.3 19.1 %collective-permute-start.26 = (bf16[2,48,3072]{2,1,0:T(8,128)(2,1)S(1)}, bf16[2,48,3072]{2,1,0:T(8,128)(2,1)S(1)}, u32[]{:S(2)}, u32[]{:S(2)}) collective-permute-start(bf16[2,48,3072]{2,1,0:T(8,128)(2,1)S(1)} %get-tuple-element.214), channel_id=1, source_target_pairs={{0,4},{1,5},{2,6},{3,7},{4,0},{5,1},{6,2},{7,3},{8,12},{9,13},{10,... | collective-permute-start | bytes 1769480 | tf_op jit(solution)/shard_map/ppermute | solution.py:1118
  179.2 15.2 %collective-permute-start.30 = (bf16[104,768]{1,0:T(8,128)(2,1)S(1)}, bf16[104,768]{1,0:T(8,128)(2,1)S(1)}, u32[]{:S(2)}, u32[]{:S(2)}) collective-permute-start(bf16[104,768]{1,0:T(8,128)(2,1)S(1)} %get-tuple-element.229), channel_id=1, source_target_pairs={{0,16},{8,24},{16,0},{24,8},{1,17},{9,25},{17,1},{25,9},{2,18},{10... | collective-permute-start | bytes 479240 | tf_op jit(solution)/shard_map/ppermute | solution.py:1122
  194.6 34.4 %collective-permute-start.33 = (bf16[4,96,2304]{2,1,0:T(8,128)(2,1)S(1)}, bf16[4,96,2304]{2,1,0:T(8,128)(2,1)S(1)}, u32[]{:S(2)}, u32[]{:S(2)}) collective-permute-start(bf16[4,96,2304]{2,1,0:T(8,128)(2,1)S(1)} %get-tuple-element.241), channel_id=1, source_target_pairs={{0,1},{1,0},{2,3},{3,2},{4,5},{5,4},{6,7},{7,6},{8,9},{9,8},{10,11... | collective-permute-start | bytes 5308424 | tf_op jit(solution)/shard_map/ppermute | solution.py:1118
  194.8 15.5 %collective-permute-start.35 = (bf16[1,96,3072]{2,1,0:T(8,128)(2,1)S(1)}, bf16[1,96,3072]{2,1,0:T(8,128)(2,1)S(1)}, u32[]{:S(2)}, u32[]{:S(2)}) collective-permute-start(bf16[1,96,3072]{2,1,0:T(8,128)(2,1)S(1)} %get-tuple-element.234.one), channel_id=1, source_target_pairs={{0,8},{24,16},{1,9},{25,17},{2,10},{26,18},{3,11},{27,19},{4,12},{... | collective-permute-start | bytes 1769480 | tf_op jit(solution)/shard_map/ppermute | solution.py:1118
  196.7 20.0 %collective-permute-start.34 = (bf16[104,3840]{1,0:T(8,128)(2,1)S(1)}, bf16[104,3840]{1,0:T(8,128)(2,1)S(1)}, u32[]{:S(2)}, u32[]{:S(2)}) collective-permute-start(bf16[104,3840]{1,0:T(8,128)(2,1)S(1)} %get-tuple-element.224), channel_id=1, source_target_pairs={{0,2},{1,3},{2,0},{3,1},{4,6},{5,7},{6,4},{7,5},{8,10},{9,11},{10,... | collective-permute-start | bytes 2396168 | tf_op jit(solution)/shard_map/ppermute | solution.py:1118
  197.8 18.3 %collective-permute-start.36 = (bf16[96,3840]{1,0:T(8,128)(2,1)S(1)}, bf16[96,3840]{1,0:T(8,128)(2,1)S(1)}, u32[]{:S(2)}, u32[]{:S(2)}) collective-permute-start(bf16[96,3840]{1,0:T(8,128)(2,1)S(1)} %get-tuple-element.225), channel_id=1, source_target_pairs={{0,4},{1,5},{2,6},{3,7},{4,0},{5,1},{6,2},{7,3},{8,12},{9,13},{10,... | collective-permute-start | bytes 2211848 | tf_op jit(solution)/shard_map/ppermute | solution.py:1118
  198.8 23.7 %collective-permute-start.39 = (bf16[1,96,3072]{2,1,0:T(8,128)(2,1)S(1)}, bf16[1,96,3072]{2,1,0:T(8,128)(2,1)S(1)}, u32[]{:S(2)}, u32[]{:S(2)}) collective-permute-start(bf16[1,96,3072]{2,1,0:T(8,128)(2,1)S(1)} %get-tuple-element.235.one), channel_id=1, source_target_pairs={{0,8},{24,16},{1,9},{25,17},{2,10},{26,18},{3,11},{27,19},{4,12},{... | collective-permute-start | bytes 1769480 | tf_op jit(solution)/shard_map/ppermute | solution.py:1118
  210.5 12.9 %collective-permute-start.38 = (bf16[1,96,3072]{2,1,0:T(8,128)(2,1)S(1)}, bf16[1,96,3072]{2,1,0:T(8,128)(2,1)S(1)}, u32[]{:S(2)}, u32[]{:S(2)}) collective-permute-start(bf16[1,96,3072]{2,1,0:T(8,128)(2,1)S(1)} %chain_two.2.one), channel_id=1, source_target_pairs={{8,16},{16,8},{9,17},{17,9},{10,18},{18,10},{11,19},{19,11},{12,20... | collective-permute-start | bytes 1769480 | tf_op jit(solution)/shard_map/ppermute | solution.py:1118
  223.6 21.5 %collective-permute-start.43 = (bf16[1,96,3072]{2,1,0:T(8,128)(2,1)S(1)}, bf16[1,96,3072]{2,1,0:T(8,128)(2,1)S(1)}, u32[]{:S(2)}, u32[]{:S(2)}) collective-permute-start(bf16[1,96,3072]{2,1,0:T(8,128)(2,1)S(1)} %chain_three.2.refs_0_), channel_id=1, source_target_pairs={{8,0},{16,24},{9,1},{17,25},{10,2},{18,26},{11,3},{19,27},{12,4},{... | collective-permute-start | bytes 1769480 | tf_op jit(solution)/shard_map/ppermute | solution.py:1118
  229.5 17.2 %collective-permute-start.44 = (bf16[2,48,2304]{2,1,0:T(8,128)(2,1)S(1)}, bf16[2,48,2304]{2,1,0:T(8,128)(2,1)S(1)}, u32[]{:S(2)}, u32[]{:S(2)}) collective-permute-start(bf16[2,48,2304]{2,1,0:T(8,128)(2,1)S(1)} %get-tuple-element.259), channel_id=1, source_target_pairs={{0,4},{1,5},{2,6},{3,7},{4,0},{5,1},{6,2},{7,3},{8,12},{9,13},{10,... | collective-permute-start | bytes 1327112 | tf_op jit(solution)/shard_map/ppermute | solution.py:1118
  231.1 15.6 %collective-permute-start.41 = (bf16[2,48,2304]{2,1,0:T(8,128)(2,1)S(1)}, bf16[2,48,2304]{2,1,0:T(8,128)(2,1)S(1)}, u32[]{:S(2)}, u32[]{:S(2)}) collective-permute-start(bf16[2,48,2304]{2,1,0:T(8,128)(2,1)S(1)} %get-tuple-element.258), channel_id=1, source_target_pairs={{0,2},{1,3},{2,0},{3,1},{4,6},{5,7},{6,4},{7,5},{8,10},{9,11},{10,... | collective-permute-start | bytes 1327112 | tf_op jit(solution)/shard_map/ppermute | solution.py:1118
  231.6 22.6 %collective-permute-start.46 = (bf16[56,3840]{1,0:T(8,128)(2,1)S(1)}, bf16[56,3840]{1,0:T(8,128)(2,1)S(1)}, u32[]{:S(2)}, u32[]{:S(2)}) collective-permute-start(bf16[56,3840]{1,0:T(8,128)(2,1)S(1)} %get-tuple-element.255), channel_id=1, source_target_pairs={{0,8},{8,0},{16,24},{24,16},{1,9},{9,1},{17,25},{25,17},{2,10},{10... | collective-permute-start | bytes 1290248 | tf_op jit(solution)/shard_map/ppermute | solution.py:1118
  249.1 33.3 %collective-permute-start.51 = (bf16[1,96,3072]{2,1,0:T(8,128)(2,1)S(1)}, bf16[1,96,3072]{2,1,0:T(8,128)(2,1)S(1)}, u32[]{:S(2)}, u32[]{:S(2)}) collective-permute-start(bf16[1,96,3072]{2,1,0:T(8,128)(2,1)S(1)} %chain_three.3.refs_0_), channel_id=1, source_target_pairs={{8,0},{16,24},{9,1},{17,25},{10,2},{18,26},{11,3},{19,27},{12,4},{... | collective-permute-start | bytes 1769480 | tf_op jit(solution)/shard_map/ppermute | solution.py:1118
  254.4 25.3 %collective-permute-start.50 = (bf16[56,3840]{1,0:T(8,128)(2,1)S(1)}, bf16[56,3840]{1,0:T(8,128)(2,1)S(1)}, u32[]{:S(2)}, u32[]{:S(2)}) collective-permute-start(bf16[56,3840]{1,0:T(8,128)(2,1)S(1)} %get-tuple-element.270.pair), channel_id=1, source_target_pairs={{0,16},{8,24},{16,0},{24,8},{1,17},{9,25},{17,1},{25,9},{2,18},{10... | collective-permute-start | bytes 1290248 | tf_op jit(solution)/shard_map/ppermute | solution.py:1118
  255.9 23.1 %collective-permute-start.48 = (bf16[1,48,2304]{2,1,0:T(8,128)(2,1)S(1)}, bf16[1,48,2304]{2,1,0:T(8,128)(2,1)S(1)}, u32[]{:S(2)}, u32[]{:S(2)}) collective-permute-start(bf16[1,48,2304]{2,1,0:T(8,128)(2,1)S(1)} %get-tuple-element.274), channel_id=1, source_target_pairs={{0,8},{8,0},{16,24},{24,16},{1,9},{9,1},{17,25},{25,17},{2,10},{10... | collective-permute-start | bytes 663560 | tf_op jit(solution)/shard_map/ppermute | solution.py:1118
  279.8 15.1 %collective-permute-start.53 = (bf16[1,48,3840]{2,1,0:T(8,128)(2,1)S(1)}, bf16[1,48,3840]{2,1,0:T(8,128)(2,1)S(1)}, u32[]{:S(2)}, u32[]{:S(2)}) collective-permute-start(bf16[1,48,3840]{2,1,0:T(8,128)(2,1)S(1)} %get-tuple-element.278.full), channel_id=1, source_target_pairs={{0,8},{8,0},{16,24},{24,16},{1,9},{9,1},{17,25},{25,17},{2,10},{10... | collective-permute-start | bytes 1105928 | tf_op jit(solution)/shard_map/ppermute | solution.py:1118
  (38 other events, 390.2 us)

commit v5 on v4

--- a/solution.py
+++ b/solution.py
@@ -553,24 +553,24 @@
     return copies
 
 
-def arrange_parameters(where, bias, *refs):
-    sources, (first, second), held, sems = refs[:5], refs[5:7], refs[7:12], refs[12]
+def arrange_parameters(where, *refs):
+    sources, (first, second), held, sems = refs[:6], refs[6:8], refs[8:14], refs[14]
     copies = [
         pltpu.make_async_copy(source, target, sems.at[i])
         for i, (source, target) in enumerate(zip(sources, held, strict=True))
     ]
     for c in copies:
         c.start()
-    entry, leave, gains, shifts, biases = held
+    entry, leave, gains, shifts, biases, bias = held
     own = where[0]
     lane = lax.broadcasted_iota(jnp.int32, (SHARD, D), 1)
     spread = jnp.where(lane == own * SHARD + row_index(SHARD), 1.0, 0.0).astype(BF)
     lane = lax.broadcasted_iota(jnp.int32, (384, D), 1)
     wide = jnp.where(lane == (own & 1) * 384 + row_index(384), 1.0, 0.0).astype(BF)
     four = lax.broadcasted_iota(jnp.int32, (4, D), 0)
-    bias_rows = jnp.where(four == own // 2, nn(bias[...], wide), 0.0)
     for c in copies:
         c.wait()
+    bias_rows = jnp.where(four == own // 2, nn(bias[...].reshape(1, 384), wide), 0.0)
     rows = jnp.concatenate(
         [nn(gains[...], spread), nn(shifts[...], spread), nn(biases[...], spread), bias_rows], axis=0
     )
@@ -1331,19 +1331,18 @@
     where = jnp.stack([own, lax.axis_index("frame")]).astype(jnp.int32)
     rows = lambda *parts: jnp.concatenate(parts, axis=0)
 
-    sources = (temporal_entry, temporal_exit, layer_gains, layer_shifts, branch_biases)
+    sources = (temporal_entry, temporal_exit, layer_gains, layer_shifts, branch_biases, expand_bias)
     g1a, g1b = pl.pallas_call(
         arrange_parameters,
         name="arrange_parameters",
         out_shape=[shape(HALF + 8, WIDE), shape(HALF, WIDE)],
-        in_specs=[pl.BlockSpec(memory_space=pltpu.SMEM), VMEM] + [HBM] * 5,
+        in_specs=[pl.BlockSpec(memory_space=pltpu.SMEM)] + [HBM] * 6,
         out_specs=[VMEM] * 2,
-        scratch_shapes=[pltpu.VMEM(v.shape, BF) for v in sources] + [pltpu.SemaphoreType.DMA((5,))],
+        scratch_shapes=[pltpu.VMEM(v.shape, BF) for v in sources] + [pltpu.SemaphoreType.DMA((6,))],
         compiler_params=limit(8),
         cost_estimate=NO_COST,
     )(
         where,
-        expand_bias.reshape(1, 384),
         *(pltpu.with_memory_space_constraint(v, pltpu.HBM) for v in sources),
     )
     x1, y1 = swap(g1a, ACROSS), swap(g1b, UP)

time: 300 us -> 299 us (level)
  no operation moved by 1% of the time
where the time goes in v5:
time: 299 us
  waiting for transfers between devices  127 us (42%)
  Pallas kernels  99 us (33%)
  starting transfers between devices  63.8 us (21%)
  local copies, waits for them, and re-layouts  6.87 us (2%)
    ppermute x42, waiting for transfers between devices, swap(): return lax.ppermute(value, axis, pairs)  114 us
    ppermute x42, starting transfers between devices, swap(): return lax.ppermute(value, axis, pairs)  41.3 us
    ppermute x12, starting transfers between devices, shift(): lax.ppermute(pieces[k], 'frame', [(i, i ^ k) for i in range(4)])  22.4 us
    pallas_call x1, Pallas kernels, body(): pl.pallas_call(feed_forward, name='feed_forward', out_shape=[shape(*video...  20.8 us
    pallas_call x25, Pallas kernels, whole_call(): pl.pallas_call(functools.partial(kernel, **options), name=name, out_shape...  20.2 us
    pallas_call x1, Pallas kernels, body(): pl.pallas_call(temporal_back, name='temporal_back', out_shape=[shape(SPOT...  13.6 us
    ppermute x12, waiting for transfers between devices, shift(): lax.ppermute(pieces[k], 'frame', [(i, i ^ k) for i in range(4)])  13 us
    pallas_call x1, Pallas kernels, body(): pl.pallas_call(spatial_forward, name='spatial_forward', out_shape=[shape(...  12.5 us
  transfers between devices with their start and end apart: 54, of which 26 were waited for; matrix products, arithmetic and copies ran while one was open for 2% of the time, Pallas kernels for 24%

profile of v5, /device:TPU:0, one launch (start us, length us, event | category | flops | bytes accessed | tf_op | source)
XLA Modules:
  0.0 298.9 jit_solution(13437338949511928753)
XLA Ops:
  2.7 3.0 %collective-permute-start = (bf16[56,3072]{1,0:T(8,128)(2,1)S(1)}, bf16[56,3072]{1,0:T(8,128)(2,1)S(1)}, u32[]{:S(2)}, u32[]{:S(2)}) collective-permute-start(bf16[56,3072]{1,0:T(8,128)(2,1)S(1)} %get-tuple-element.149.refs_4_), channel_id=1, source_target_pairs={{0,2},{1,3},{2,0},{3,1},{4,6},{5,7},{6,4},{7,5},{8,10},{9,11},{10,... | collective-permute-start | bytes 1032200 | tf_op jit(solution)/shard_map/ppermute | solution.py:1118
  11.1 2.6 collective-permute-start.4
  17.9 20.0 %collective-permute-done.2.refs_8_ = bf16[160,3072]{1,0:T(8,128)(2,1)S(1)} collective-permute-done((bf16[160,3072]{1,0:T(8,128)(2,1)S(1)}, bf16[160,3072]{1,0:T(8,128)(2,1)S(1)}, u32[]{:S(2)}, u32[]{:S(2)}) %collective-permute-start.2) | collective-permute-done | bytes 983072 | tf_op jit(solution)/shard_map/ppermute | solution.py:1118
  40.5 2.3 collective-permute-done.8.refs_10_
  42.9 10.2 %temporal_forward.1 = (bf16[104,768]{1,0:T(8,128)(2,1)S(1)}, bf16[104,768]{1,0:T(8,128)(2,1)S(1)}, bf16[104,768]{1,0:T(8,128)(2,1)S(1)}, bf16[104,768]{1,0:T(8,1...) custom-call(bf16[104,768]{1,0:T(8,128)(2,1)S(1)} %get-tuple-element., ...), custom_call_target="tpu_custom_call" | custom-call | flops 1000 | bytes 1000 | tf_op jit(solution)/shard_map/temporal_forward/pallas_call | solution.py:1372
  53.1 2.7 collective-permute-start.10
  57.3 9.4 %collective-permute-done.6.refs_11_.refs_2_ = bf16[192,3072]{1,0:T(8,128)(2,1)S(1)} collective-permute-done((bf16[192,3072]{1,0:T(8,128)(2,1)S(1)}, bf16[192,3072]{1,0:T(8,128)(2,1)S(1)}, u32[]{:S(2)}, u32[]{:S(2)}) %collective-permute-start.6) | collective-permute-done | bytes 1179680 | tf_op jit(solution)/shard_map/ppermute | solution.py:1118
  73.2 12.5 %spatial_forward.1 = (f32[416,768]{1,0:T(8,128)S(1)}, bf16[416,768]{1,0:T(8,128)(2,1)S(1)}, bf16[768,2304]{1,0:T(8,128)(2,1)}, bf16[768,768]{1,0:T(8,128)(2,1)},...) custom-call(bf16[416,768]{1,0:T(8,128)(2,1)S(1)} %get-tuple-element., ...), custom_call_target="tpu_custom_call" | custom-call | flops 1000 | bytes 1000 | tf_op jit(solution)/shard_map/spatial_forward/pallas_call | solution.py:1416
  85.9 11.4 %collective-permute-done.15.refs_5_ = bf16[192,3072]{1,0:T(8,128)(2,1)S(1)} collective-permute-done((bf16[192,3072]{1,0:T(8,128)(2,1)S(1)}, bf16[192,3072]{1,0:T(8,128)(2,1)S(1)}, u32[]{:S(2)}, u32[]{:S(2)}) %collective-permute-start.15) | collective-permute-done | bytes 1179680 | tf_op jit(solution)/shard_map/ppermute | solution.py:1118
  97.9 2.3 collective-permute-done.18.refs_8_
  101.9 20.8 %feed_forward.1 = (bf16[1,2,196,768]{3,2,1,0:T(8,128)(2,1)S(1)}, f32[416,768]{1,0:T(8,128)S(1)}, bf16[416,768]{1,0:T(8,128)(2,1)S(1)}, bf16[4,96,3072]{2,1,0:T(8...) custom-call(s32[2]{0:T(128)S(1)} %pad_add_fusion.where, ...), custom_call_target="tpu_custom_call" | custom-call | flops 1000 | bytes 1000 | tf_op jit(solution)/shard_map/feed_forward/pallas_call | solution.py:1449
  123.2 9.9 %spatial_back.1.refs_0_.refs_3_ = bf16[416,2304]{1,0:T(8,128)(2,1)S(1)} custom-call(bf16[416,768]{1,0:T(8,128)(2,1)S(1)} %get-tuple-element.180.branch.refs_1_.refs_5_, bf16[416,2304]{1,0:T(8,128)(2,1)S(1)} %copy-done.4, bf16[768,768]{1,0:T(8,128)(2,1)S(1)} %copy-done.7), custom_call_target="tpu_custom_call" | custom-call | flops 1000 | bytes 1000 | tf_op jit(solution)/shard_map/spatial_back/pallas_call | solution.py:1481
  136.6 4.5 %spatial_back_norm.1 = (f32[416,768]{1,0:T(8,128)S(1)}, bf16[416,768]{1,0:T(8,128)(2,1)S(1)}, f32[16,768]{1,0:T(8,128)S(1)}, bf16[104,768]{1,0:T(8,128)(2,1)S(1)...) custom-call(s32[2]{0:T(128)S(1)} %pad_add_fusion.where, ...), custom_call_target="tpu_custom_call" | custom-call | flops 1000 | bytes 1000 | tf_op jit(solution)/shard_map/spatial_back_norm/pallas_call | solution.py:1098
  141.1 3.2 %collective-permute-start.22 = (bf16[104,768]{1,0:T(8,128)(2,1)S(1)}, bf16[104,768]{1,0:T(8,128)(2,1)S(1)}, u32[]{:S(2)}, u32[]{:S(2)}) collective-permute-start(bf16[104,768]{1,0:T(8,128)(2,1)S(1)} %get-tuple-element.204), channel_id=1, source_target_pairs={{0,8},{8,0},{16,24},{24,16},{1,9},{9,1},{17,25},{25,17},{2,10},{10... | collective-permute-start | bytes 479240 | tf_op jit(solution)/shard_map/ppermute | solution.py:1122
  147.6 6.1 %weight_grads.2 = (bf16[4,96,3840]{2,1,0:T(8,128)(2,1)S(1)}, bf16[4,96,3840]{2,1,0:T(8,128)(2,1)S(1)}) custom-call(s32[2]{0:T(128)S(1)} %pad_add_fusion.where, bf16[416,768]{1,0:T(8,128)(2,1)S(1)} %copy-done.8, bf16[416,768]{1,0:T(8,128)(2,1)S(1)} %get-tuple-element.196.refs_1_, bf16[416,768]{1,0:T(8,128)(2,1)S(1)} %copy-done.9, ...), custom_call_target="tpu_custom_call" | custom-call | flops 1000 | bytes 1000 | tf_op jit(solution)/shard_map/weight_grads/pallas_call | solution.py:1519
  153.8 4.9 %collective-permute-done.23.refs_6_ = bf16[104,768]{1,0:T(8,128)(2,1)S(1)} collective-permute-done((bf16[104,768]{1,0:T(8,128)(2,1)S(1)}, bf16[104,768]{1,0:T(8,128)(2,1)S(1)}, u32[]{:S(2)}, u32[]{:S(2)}) %collective-permute-start.23) | collective-permute-done | bytes 159776 | tf_op jit(solution)/shard_map/ppermute | solution.py:1122
  158.7 13.6 %temporal_back.1 = (bf16[400,2304]{1,0:T(8,128)(2,1)S(1)}, f32[16,768]{1,0:T(8,128)S(1)}, bf16[104,768]{1,0:T(8,128)(2,1)S(1)}, bf16[104,768]{1,0:T(8,128)(2,1)S...) custom-call(bf16[104,768]{1,0:T(8,128)(2,1)S(1)} %get-tuple-element.163.refs_0_, ...), custom_call_target="tpu_custom_call" | custom-call | flops 1000 | bytes 1000 | tf_op jit(solution)/shard_map/temporal_back/pallas_call | solution.py:1539
  175.0 2.8 collective-permute-start.31
  178.4 4.4 %collective-permute-start.30 = (bf16[104,768]{1,0:T(8,128)(2,1)S(1)}, bf16[104,768]{1,0:T(8,128)(2,1)S(1)}, u32[]{:S(2)}, u32[]{:S(2)}) collective-permute-start(bf16[104,768]{1,0:T(8,128)(2,1)S(1)} %get-tuple-element.229), channel_id=1, source_target_pairs={{0,16},{8,24},{16,0},{24,8},{1,17},{9,25},{17,1},{25,9},{2,18},{10... | collective-permute-start | bytes 479240 | tf_op jit(solution)/shard_map/ppermute | solution.py:1122
  182.8 3.7 %weight_grads.3 = (bf16[4,96,2304]{2,1,0:T(8,128)(2,1)S(1)}, bf16[4,96,2304]{2,1,0:T(8,128)(2,1)S(1)}) custom-call(s32[2]{0:T(128)S(1)} %pad_add_fusion.where, bf16[400,768]{1,0:T(8,128)(2,1)S(1)} %copy-done.11, bf16[400,2304]{1,0:T(8,128)(2,1)S(1)} %get-tuple-element.220.refs_1_), custom_call_target="tpu_custom_call" | custom-call | flops 1000 | bytes 1000 | tf_op jit(solution)/shard_map/weight_grads/pallas_call | solution.py:1519
  187.3 6.3 %collective-permute-done.30.refs_2_ = bf16[104,768]{1,0:T(8,128)(2,1)S(1)} collective-permute-done((bf16[104,768]{1,0:T(8,128)(2,1)S(1)}, bf16[104,768]{1,0:T(8,128)(2,1)S(1)}, u32[]{:S(2)}, u32[]{:S(2)}) %collective-permute-start.30) | collective-permute-done | bytes 159776 | tf_op jit(solution)/shard_map/ppermute | solution.py:1122
  201.0 8.6 %collective-permute-done.35.two = bf16[1,96,3072]{2,1,0:T(8,128)(2,1)S(1)} collective-permute-done((bf16[1,96,3072]{2,1,0:T(8,128)(2,1)S(1)}, bf16[1,96,3072]{2,1,0:T(8,128)(2,1)S(1)}, u32[]{:S(2)}, u32[]{:S(2)}) %collective-permute-start.35) | collective-permute-done | bytes 589856 | tf_op jit(solution)/shard_map/ppermute | solution.py:1118
  210.5 4.9 %collective-permute-done.36.from_y = bf16[96,3840]{1,0:T(8,128)(2,1)S(1)} collective-permute-done((bf16[96,3840]{1,0:T(8,128)(2,1)S(1)}, bf16[96,3840]{1,0:T(8,128)(2,1)S(1)}, u32[]{:S(2)}, u32[]{:S(2)}) %collective-permute-start.36) | collective-permute-done | bytes 737312 | tf_op jit(solution)/shard_map/ppermute | solution.py:1118
  218.4 3.4 %collective-permute-done.39.two = bf16[1,96,3072]{2,1,0:T(8,128)(2,1)S(1)} collective-permute-done((bf16[1,96,3072]{2,1,0:T(8,128)(2,1)S(1)}, bf16[1,96,3072]{2,1,0:T(8,128)(2,1)S(1)}, u32[]{:S(2)}, u32[]{:S(2)}) %collective-permute-start.39) | collective-permute-done | bytes 589856 | tf_op jit(solution)/shard_map/ppermute | solution.py:1118
  224.2 3.3 %collective-permute-done.40.got_x = bf16[48,3840]{1,0:T(8,128)(2,1)S(1)} collective-permute-done((bf16[48,3840]{1,0:T(8,128)(2,1)S(1)}, bf16[48,3840]{1,0:T(8,128)(2,1)S(1)}, u32[]{:S(2)}, u32[]{:S(2)}) %collective-permute-start.40) | collective-permute-done | bytes 368672 | tf_op jit(solution)/shard_map/ppermute | solution.py:1118
  230.9 2.6 collective-permute-start.46
  233.7 10.6 %collective-permute-done.43.refs_1_ = bf16[1,96,3072]{2,1,0:T(8,128)(2,1)S(1)} collective-permute-done((bf16[1,96,3072]{2,1,0:T(8,128)(2,1)S(1)}, bf16[1,96,3072]{2,1,0:T(8,128)(2,1)S(1)}, u32[]{:S(2)}, u32[]{:S(2)}) %collective-permute-start.43) | collective-permute-done | bytes 589856 | tf_op jit(solution)/shard_map/ppermute | solution.py:1118
  249.6 3.9 %collective-permute-done.46.near = bf16[56,3840]{1,0:T(8,128)(2,1)S(1)} collective-permute-done((bf16[56,3840]{1,0:T(8,128)(2,1)S(1)}, bf16[56,3840]{1,0:T(8,128)(2,1)S(1)}, u32[]{:S(2)}, u32[]{:S(2)}) %collective-permute-start.46) | collective-permute-done | bytes 430112 | tf_op jit(solution)/shard_map/ppermute | solution.py:1118
  255.2 2.6 collective-permute-start.48
  257.7 20.5 %collective-permute-done.48.two = bf16[1,48,2304]{2,1,0:T(8,128)(2,1)S(1)} collective-permute-done((bf16[1,48,2304]{2,1,0:T(8,128)(2,1)S(1)}, bf16[1,48,2304]{2,1,0:T(8,128)(2,1)S(1)}, u32[]{:S(2)}, u32[]{:S(2)}) %collective-permute-start.48) | collective-permute-done | bytes 221216 | tf_op jit(solution)/shard_map/ppermute | solution.py:1118
  279.1 2.5 collective-permute-start.53
  283.3 5.7 %collective-permute-done.49.two = bf16[1,48,2304]{2,1,0:T(8,128)(2,1)S(1)} collective-permute-done((bf16[1,48,2304]{2,1,0:T(8,128)(2,1)S(1)}, bf16[1,48,2304]{2,1,0:T(8,128)(2,1)S(1)}, u32[]{:S(2)}, u32[]{:S(2)}) %collective-permute-start.49) | collective-permute-done | bytes 221216 | tf_op jit(solution)/shard_map/ppermute | solution.py:1118
  (171 shorter events, 72.3 us)
Async XLA Ops:
  9.5 28.8 %collective-permute-start.3 = (bf16[104,768]{1,0:T(8,128)(2,1)S(1)}, bf16[104,768]{1,0:T(8,128)(2,1)S(1)}, u32[]{:S(2)}, u32[]{:S(2)}) collective-permute-start(bf16[104,768]{1,0:T(8,128)(2,1)S(1)} %get-tuple-element.155), channel_id=1, source_target_pairs={{0,8},{8,0},{16,24},{24,16},{1,9},{9,1},{17,25},{25,17},{2,10},{10... | collective-permute-start | bytes 479240 | tf_op jit(solution)/shard_map/ppermute | solution.py:1122
  11.1 27.1 %collective-permute-start.4 = (bf16[104,768]{1,0:T(8,128)(2,1)S(1)}, bf16[104,768]{1,0:T(8,128)(2,1)S(1)}, u32[]{:S(2)}, u32[]{:S(2)}) collective-permute-start(bf16[104,768]{1,0:T(8,128)(2,1)S(1)} %get-tuple-element.156), channel_id=1, source_target_pairs={{0,16},{8,24},{16,0},{24,8},{1,17},{9,25},{17,1},{25,9},{2,18},{10... | collective-permute-start | bytes 479240 | tf_op jit(solution)/shard_map/ppermute | solution.py:1122
  13.7 24.6 %collective-permute-start.5 = (bf16[104,768]{1,0:T(8,128)(2,1)S(1)}, bf16[104,768]{1,0:T(8,128)(2,1)S(1)}, u32[]{:S(2)}, u32[]{:S(2)}) collective-permute-start(bf16[104,768]{1,0:T(8,128)(2,1)S(1)} %get-tuple-element.157), channel_id=1, source_target_pairs={{0,24},{8,16},{16,8},{24,0},{1,25},{9,17},{17,9},{25,1},{2,26},{10... | collective-permute-start | bytes 479240 | tf_op jit(solution)/shard_map/ppermute | solution.py:1122
  15.5 22.4 %collective-permute-start.2 = (bf16[160,3072]{1,0:T(8,128)(2,1)S(1)}, bf16[160,3072]{1,0:T(8,128)(2,1)S(1)}, u32[]{:S(2)}, u32[]{:S(2)}) collective-permute-start(bf16[160,3072]{1,0:T(8,128)(2,1)S(1)} %pad_maximum_fusion.5), channel_id=1, source_target_pairs={{0,4},{1,5},{2,6},{3,7},{4,0},{5,1},{6,2},{7,3},{8,12},{9,13},{10,... | collective-permute-start | bytes 2949128 | tf_op jit(solution)/shard_map/ppermute | solution.py:1118
  17.1 20.8 %collective-permute-start.7 = (bf16[144,3072]{1,0:T(8,128)(2,1)S(1)}, bf16[144,3072]{1,0:T(8,128)(2,1)S(1)}, u32[]{:S(2)}, u32[]{:S(2)}) collective-permute-start(bf16[144,3072]{1,0:T(8,128)(2,1)S(1)} %pad_maximum_fusion.6), channel_id=1, source_target_pairs={{0,2},{1,3},{2,0},{3,1},{4,6},{5,7},{6,4},{7,5},{8,10},{9,11},{10,... | collective-permute-start | bytes 2654216 | tf_op jit(solution)/shard_map/ppermute | solution.py:1118
  38.3 28.4 %collective-permute-start.6 = (bf16[192,3072]{1,0:T(8,128)(2,1)S(1)}, bf16[192,3072]{1,0:T(8,128)(2,1)S(1)}, u32[]{:S(2)}, u32[]{:S(2)}) collective-permute-start(bf16[192,3072]{1,0:T(8,128)(2,1)S(1)} %pad_maximum_fusion.1), channel_id=1, source_target_pairs={{0,2},{1,3},{2,0},{3,1},{4,6},{5,7},{6,4},{7,5},{8,10},{9,11},{10,... | collective-permute-start | bytes 3538952 | tf_op jit(solution)/shard_map/ppermute | solution.py:1118
  39.1 29.4 %collective-permute-start.12 = (bf16[192,3072]{1,0:T(8,128)(2,1)S(1)}, bf16[192,3072]{1,0:T(8,128)(2,1)S(1)}, u32[]{:S(2)}, u32[]{:S(2)}) collective-permute-start(bf16[192,3072]{1,0:T(8,128)(2,1)S(1)} %pad_maximum_fusion.2), channel_id=1, source_target_pairs={{0,4},{1,5},{2,6},{3,7},{4,0},{5,1},{6,2},{7,3},{8,12},{9,13},{10,... | collective-permute-start | bytes 3538952 | tf_op jit(solution)/shard_map/ppermute | solution.py:1118
  53.1 14.8 %collective-permute-start.10 = (bf16[104,768]{1,0:T(8,128)(2,1)S(1)}, bf16[104,768]{1,0:T(8,128)(2,1)S(1)}, u32[]{:S(2)}, u32[]{:S(2)}) collective-permute-start(bf16[104,768]{1,0:T(8,128)(2,1)S(1)} %get-tuple-element.165), channel_id=1, source_target_pairs={{0,16},{8,24},{16,0},{24,8},{1,17},{9,25},{17,1},{25,9},{2,18},{10... | collective-permute-start | bytes 479240 | tf_op jit(solution)/shard_map/ppermute | solution.py:1122
  69.7 27.6 %collective-permute-start.15 = (bf16[192,3072]{1,0:T(8,128)(2,1)S(1)}, bf16[192,3072]{1,0:T(8,128)(2,1)S(1)}, u32[]{:S(2)}, u32[]{:S(2)}) collective-permute-start(bf16[192,3072]{1,0:T(8,128)(2,1)S(1)} %pad_maximum_fusion.4), channel_id=1, source_target_pairs={{0,2},{1,3},{2,0},{3,1},{4,6},{5,7},{6,4},{7,5},{8,10},{9,11},{10,... | collective-permute-start | bytes 3538952 | tf_op jit(solution)/shard_map/ppermute | solution.py:1118
  70.5 27.3 %collective-permute-start.14 = (bf16[192,3072]{1,0:T(8,128)(2,1)S(1)}, bf16[192,3072]{1,0:T(8,128)(2,1)S(1)}, u32[]{:S(2)}, u32[]{:S(2)}) collective-permute-start(bf16[192,3072]{1,0:T(8,128)(2,1)S(1)} %pad_maximum_fusion.3), channel_id=1, source_target_pairs={{0,4},{1,5},{2,6},{3,7},{4,0},{5,1},{6,2},{7,3},{8,12},{9,13},{10,... | collective-permute-start | bytes 3538952 | tf_op jit(solution)/shard_map/ppermute | solution.py:1118
  85.8 16.1 %collective-permute-start.16 = (bf16[384,3072]{1,0:T(8,128)(2,1)S(1)}, bf16[384,3072]{1,0:T(8,128)(2,1)S(1)}, u32[]{:S(2)}, u32[]{:S(2)}) collective-permute-start(bf16[384,3072]{1,0:T(8,128)(2,1)S(1)} %pad_maximum_fusion), channel_id=1, source_target_pairs={{0,1},{1,0},{2,3},{3,2},{4,5},{5,4},{6,7},{7,6},{8,9},{9,8},{10,11... | collective-permute-start | bytes 7077896 | tf_op jit(solution)/shard_map/ppermute | solution.py:1118
  134.4 37.9 %collective-permute-start.25 = (bf16[4,48,3072]{2,1,0:T(8,128)(2,1)S(1)}, bf16[4,48,3072]{2,1,0:T(8,128)(2,1)S(1)}, u32[]{:S(2)}, u32[]{:S(2)}) collective-permute-start(bf16[4,48,3072]{2,1,0:T(8,128)(2,1)S(1)} %get-tuple-element.193), channel_id=1, source_target_pairs={{0,4},{1,5},{2,6},{3,7},{4,0},{5,1},{6,2},{7,3},{8,12},{9,13},{10,... | collective-permute-start | bytes 3538952 | tf_op jit(solution)/shard_map/ppermute | solution.py:1118
  136.0 36.3 %collective-permute-start.21 = (bf16[4,48,3072]{2,1,0:T(8,128)(2,1)S(1)}, bf16[4,48,3072]{2,1,0:T(8,128)(2,1)S(1)}, u32[]{:S(2)}, u32[]{:S(2)}) collective-permute-start(bf16[4,48,3072]{2,1,0:T(8,128)(2,1)S(1)} %get-tuple-element.192), channel_id=1, source_target_pairs={{0,2},{1,3},{2,0},{3,1},{4,6},{5,7},{6,4},{7,5},{8,10},{9,11},{10,... | collective-permute-start | bytes 3538952 | tf_op jit(solution)/shard_map/ppermute | solution.py:1118
  141.1 12.7 %collective-permute-start.22 = (bf16[104,768]{1,0:T(8,128)(2,1)S(1)}, bf16[104,768]{1,0:T(8,128)(2,1)S(1)}, u32[]{:S(2)}, u32[]{:S(2)}) collective-permute-start(bf16[104,768]{1,0:T(8,128)(2,1)S(1)} %get-tuple-element.204), channel_id=1, source_target_pairs={{0,8},{8,0},{16,24},{24,16},{1,9},{9,1},{17,25},{25,17},{2,10},{10... | collective-permute-start | bytes 479240 | tf_op jit(solution)/shard_map/ppermute | solution.py:1122
  144.2 14.5 %collective-permute-start.23 = (bf16[104,768]{1,0:T(8,128)(2,1)S(1)}, bf16[104,768]{1,0:T(8,128)(2,1)S(1)}, u32[]{:S(2)}, u32[]{:S(2)}) collective-permute-start(bf16[104,768]{1,0:T(8,128)(2,1)S(1)} %get-tuple-element.205), channel_id=1, source_target_pairs={{0,16},{8,24},{16,0},{24,8},{1,17},{9,25},{17,1},{25,9},{2,18},{10... | collective-permute-start | bytes 479240 | tf_op jit(solution)/shard_map/ppermute | solution.py:1122
  173.0 20.7 %collective-permute-start.32 = (bf16[2,48,3072]{2,1,0:T(8,128)(2,1)S(1)}, bf16[2,48,3072]{2,1,0:T(8,128)(2,1)S(1)}, u32[]{:S(2)}, u32[]{:S(2)}) collective-permute-start(bf16[2,48,3072]{2,1,0:T(8,128)(2,1)S(1)} %get-tuple-element.216), channel_id=1, source_target_pairs={{0,2},{1,3},{2,0},{3,1},{4,6},{5,7},{6,4},{7,5},{8,10},{9,11},{10,... | collective-permute-start | bytes 1769480 | tf_op jit(solution)/shard_map/ppermute | solution.py:1118
  174.5 19.1 %collective-permute-start.26 = (bf16[2,48,3072]{2,1,0:T(8,128)(2,1)S(1)}, bf16[2,48,3072]{2,1,0:T(8,128)(2,1)S(1)}, u32[]{:S(2)}, u32[]{:S(2)}) collective-permute-start(bf16[2,48,3072]{2,1,0:T(8,128)(2,1)S(1)} %get-tuple-element.214), channel_id=1, source_target_pairs={{0,4},{1,5},{2,6},{3,7},{4,0},{5,1},{6,2},{7,3},{8,12},{9,13},{10,... | collective-permute-start | bytes 1769480 | tf_op jit(solution)/shard_map/ppermute | solution.py:1118
  178.4 15.2 %collective-permute-start.30 = (bf16[104,768]{1,0:T(8,128)(2,1)S(1)}, bf16[104,768]{1,0:T(8,128)(2,1)S(1)}, u32[]{:S(2)}, u32[]{:S(2)}) collective-permute-start(bf16[104,768]{1,0:T(8,128)(2,1)S(1)} %get-tuple-element.229), channel_id=1, source_target_pairs={{0,16},{8,24},{16,0},{24,8},{1,17},{9,25},{17,1},{25,9},{2,18},{10... | collective-permute-start | bytes 479240 | tf_op jit(solution)/shard_map/ppermute | solution.py:1122
  193.9 34.4 %collective-permute-start.33 = (bf16[4,96,2304]{2,1,0:T(8,128)(2,1)S(1)}, bf16[4,96,2304]{2,1,0:T(8,128)(2,1)S(1)}, u32[]{:S(2)}, u32[]{:S(2)}) collective-permute-start(bf16[4,96,2304]{2,1,0:T(8,128)(2,1)S(1)} %get-tuple-element.241), channel_id=1, source_target_pairs={{0,1},{1,0},{2,3},{3,2},{4,5},{5,4},{6,7},{7,6},{8,9},{9,8},{10,11... | collective-permute-start | bytes 5308424 | tf_op jit(solution)/shard_map/ppermute | solution.py:1118
  194.1 15.5 %collective-permute-start.35 = (bf16[1,96,3072]{2,1,0:T(8,128)(2,1)S(1)}, bf16[1,96,3072]{2,1,0:T(8,128)(2,1)S(1)}, u32[]{:S(2)}, u32[]{:S(2)}) collective-permute-start(bf16[1,96,3072]{2,1,0:T(8,128)(2,1)S(1)} %get-tuple-element.234.one), channel_id=1, source_target_pairs={{0,8},{24,16},{1,9},{25,17},{2,10},{26,18},{3,11},{27,19},{4,12},{... | collective-permute-start | bytes 1769480 | tf_op jit(solution)/shard_map/ppermute | solution.py:1118
  196.0 20.0 %collective-permute-start.34 = (bf16[104,3840]{1,0:T(8,128)(2,1)S(1)}, bf16[104,3840]{1,0:T(8,128)(2,1)S(1)}, u32[]{:S(2)}, u32[]{:S(2)}) collective-permute-start(bf16[104,3840]{1,0:T(8,128)(2,1)S(1)} %get-tuple-element.224), channel_id=1, source_target_pairs={{0,2},{1,3},{2,0},{3,1},{4,6},{5,7},{6,4},{7,5},{8,10},{9,11},{10,... | collective-permute-start | bytes 2396168 | tf_op jit(solution)/shard_map/ppermute | solution.py:1118
  197.1 18.3 %collective-permute-start.36 = (bf16[96,3840]{1,0:T(8,128)(2,1)S(1)}, bf16[96,3840]{1,0:T(8,128)(2,1)S(1)}, u32[]{:S(2)}, u32[]{:S(2)}) collective-permute-start(bf16[96,3840]{1,0:T(8,128)(2,1)S(1)} %get-tuple-element.225), channel_id=1, source_target_pairs={{0,4},{1,5},{2,6},{3,7},{4,0},{5,1},{6,2},{7,3},{8,12},{9,13},{10,... | collective-permute-start | bytes 2211848 | tf_op jit(solution)/shard_map/ppermute | solution.py:1118
  198.1 23.7 %collective-permute-start.39 = (bf16[1,96,3072]{2,1,0:T(8,128)(2,1)S(1)}, bf16[1,96,3072]{2,1,0:T(8,128)(2,1)S(1)}, u32[]{:S(2)}, u32[]{:S(2)}) collective-permute-start(bf16[1,96,3072]{2,1,0:T(8,128)(2,1)S(1)} %get-tuple-element.235.one), channel_id=1, source_target_pairs={{0,8},{24,16},{1,9},{25,17},{2,10},{26,18},{3,11},{27,19},{4,12},{... | collective-permute-start | bytes 1769480 | tf_op jit(solution)/shard_map/ppermute | solution.py:1118
  209.7 12.9 %collective-permute-start.38 = (bf16[1,96,3072]{2,1,0:T(8,128)(2,1)S(1)}, bf16[1,96,3072]{2,1,0:T(8,128)(2,1)S(1)}, u32[]{:S(2)}, u32[]{:S(2)}) collective-permute-start(bf16[1,96,3072]{2,1,0:T(8,128)(2,1)S(1)} %chain_two.2.one), channel_id=1, source_target_pairs={{8,16},{16,8},{9,17},{17,9},{10,18},{18,10},{11,19},{19,11},{12,20... | collective-permute-start | bytes 1769480 | tf_op jit(solution)/shard_map/ppermute | solution.py:1118
  222.9 21.5 %collective-permute-start.43 = (bf16[1,96,3072]{2,1,0:T(8,128)(2,1)S(1)}, bf16[1,96,3072]{2,1,0:T(8,128)(2,1)S(1)}, u32[]{:S(2)}, u32[]{:S(2)}) collective-permute-start(bf16[1,96,3072]{2,1,0:T(8,128)(2,1)S(1)} %chain_three.2.refs_0_), channel_id=1, source_target_pairs={{8,0},{16,24},{9,1},{17,25},{10,2},{18,26},{11,3},{19,27},{12,4},{... | collective-permute-start | bytes 1769480 | tf_op jit(solution)/shard_map/ppermute | solution.py:1118
  228.8 17.2 %collective-permute-start.44 = (bf16[2,48,2304]{2,1,0:T(8,128)(2,1)S(1)}, bf16[2,48,2304]{2,1,0:T(8,128)(2,1)S(1)}, u32[]{:S(2)}, u32[]{:S(2)}) collective-permute-start(bf16[2,48,2304]{2,1,0:T(8,128)(2,1)S(1)} %get-tuple-element.259), channel_id=1, source_target_pairs={{0,4},{1,5},{2,6},{3,7},{4,0},{5,1},{6,2},{7,3},{8,12},{9,13},{10,... | collective-permute-start | bytes 1327112 | tf_op jit(solution)/shard_map/ppermute | solution.py:1118
  230.4 15.6 %collective-permute-start.41 = (bf16[2,48,2304]{2,1,0:T(8,128)(2,1)S(1)}, bf16[2,48,2304]{2,1,0:T(8,128)(2,1)S(1)}, u32[]{:S(2)}, u32[]{:S(2)}) collective-permute-start(bf16[2,48,2304]{2,1,0:T(8,128)(2,1)S(1)} %get-tuple-element.258), channel_id=1, source_target_pairs={{0,2},{1,3},{2,0},{3,1},{4,6},{5,7},{6,4},{7,5},{8,10},{9,11},{10,... | collective-permute-start | bytes 1327112 | tf_op jit(solution)/shard_map/ppermute | solution.py:1118
  230.9 22.6 %collective-permute-start.46 = (bf16[56,3840]{1,0:T(8,128)(2,1)S(1)}, bf16[56,3840]{1,0:T(8,128)(2,1)S(1)}, u32[]{:S(2)}, u32[]{:S(2)}) collective-permute-start(bf16[56,3840]{1,0:T(8,128)(2,1)S(1)} %get-tuple-element.255), channel_id=1, source_target_pairs={{0,8},{8,0},{16,24},{24,16},{1,9},{9,1},{17,25},{25,17},{2,10},{10... | collective-permute-start | bytes 1290248 | tf_op jit(solution)/shard_map/ppermute | solution.py:1118
  248.3 33.3 %collective-permute-start.51 = (bf16[1,96,3072]{2,1,0:T(8,128)(2,1)S(1)}, bf16[1,96,3072]{2,1,0:T(8,128)(2,1)S(1)}, u32[]{:S(2)}, u32[]{:S(2)}) collective-permute-start(bf16[1,96,3072]{2,1,0:T(8,128)(2,1)S(1)} %chain_three.3.refs_0_), channel_id=1, source_target_pairs={{8,0},{16,24},{9,1},{17,25},{10,2},{18,26},{11,3},{19,27},{12,4},{... | collective-permute-start | bytes 1769480 | tf_op jit(solution)/shard_map/ppermute | solution.py:1118
  253.7 25.3 %collective-permute-start.50 = (bf16[56,3840]{1,0:T(8,128)(2,1)S(1)}, bf16[56,3840]{1,0:T(8,128)(2,1)S(1)}, u32[]{:S(2)}, u32[]{:S(2)}) collective-permute-start(bf16[56,3840]{1,0:T(8,128)(2,1)S(1)} %get-tuple-element.270.pair), channel_id=1, source_target_pairs={{0,16},{8,24},{16,0},{24,8},{1,17},{9,25},{17,1},{25,9},{2,18},{10... | collective-permute-start | bytes 1290248 | tf_op jit(solution)/shard_map/ppermute | solution.py:1118
  255.2 23.1 %collective-permute-start.48 = (bf16[1,48,2304]{2,1,0:T(8,128)(2,1)S(1)}, bf16[1,48,2304]{2,1,0:T(8,128)(2,1)S(1)}, u32[]{:S(2)}, u32[]{:S(2)}) collective-permute-start(bf16[1,48,2304]{2,1,0:T(8,128)(2,1)S(1)} %get-tuple-element.274), channel_id=1, source_target_pairs={{0,8},{8,0},{16,24},{24,16},{1,9},{9,1},{17,25},{25,17},{2,10},{10... | collective-permute-start | bytes 663560 | tf_op jit(solution)/shard_map/ppermute | solution.py:1118
  279.1 15.1 %collective-permute-start.53 = (bf16[1,48,3840]{2,1,0:T(8,128)(2,1)S(1)}, bf16[1,48,3840]{2,1,0:T(8,128)(2,1)S(1)}, u32[]{:S(2)}, u32[]{:S(2)}) collective-permute-start(bf16[1,48,3840]{2,1,0:T(8,128)(2,1)S(1)} %get-tuple-element.278.full), channel_id=1, source_target_pairs={{0,8},{8,0},{16,24},{24,16},{1,9},{9,1},{17,25},{25,17},{2,10},{10... | collective-permute-start | bytes 1105928 | tf_op jit(solution)/shard_map/ppermute | solution.py:1118
  (38 other events, 387.9 us)
